TPU v7x, 32 devices: a whole 2x2x4 slice. The times are simulated.
32 devices in a mesh: fsdp: 8 (over z, x), seq: 2 (over core), replica: 2 (over y).
Axes of the slice: x: 2, y: 2, z: 4, core: 2. Of those that a mesh axis runs over, the one named last changes fastest.
Arguments:
- clips_in: bfloat16 [16, 448, 1024], P(('fsdp', 'replica'), 'seq'), may hold values from -6 to 6
- cotangent: bfloat16 [16, 448, 1024], P(('fsdp', 'replica'), 'seq'), may hold values from -6 to 6
- clip_mask: int32 [16], P(('fsdp', 'replica')), may hold values 0 or 1
- norm1_gain: bfloat16 [2, 1024], P(None, ('fsdp', 'seq')), may hold values from 0.25 to 1.75
- norm1_bias: bfloat16 [2, 1024], P(None, ('fsdp', 'seq')), may hold values from -1.5 to 1.5
- qkv_weight: bfloat16 [2, 1024, 3072], P(None, ('fsdp', 'seq')), may hold values from -0.1875 to 0.1875
- query_bias: bfloat16 [2, 1024], P(None, ('fsdp', 'seq')), may hold values from -1.5 to 1.5
- value_bias: bfloat16 [2, 1024], P(None, ('fsdp', 'seq')), may hold values from -0.25 to 0.25
- proj_weight: bfloat16 [2, 1024, 1024], P(None, ('fsdp', 'seq')), may hold values from -2 to 2
- proj_bias: bfloat16 [2, 1024], P(None, ('fsdp', 'seq')), may hold values from -1.5 to 1.5
- norm2_gain: bfloat16 [2, 1024], P(None, ('fsdp', 'seq')), may hold values from 0.25 to 1.75
- norm2_bias: bfloat16 [2, 1024], P(None, ('fsdp', 'seq')), may hold values from -1.5 to 1.5
- up_weight: bfloat16 [2, 1024, 4096], P(None, ('fsdp', 'seq')), may hold values from -0.1875 to 0.1875
- up_bias: bfloat16 [2, 4096], P(None, ('fsdp', 'seq')), may hold values from -1.5 to 1.5
- down_weight: bfloat16 [2, 4096, 1024], P(None, ('fsdp', 'seq')), may hold values from -0.09375 to 0.09375
- down_bias: bfloat16 [2, 1024], P(None, ('fsdp', 'seq')), may hold values from -1.5 to 1.5
Outputs:
- clips_out: bfloat16 [16, 448, 1024], P(('fsdp', 'replica'), 'seq')
- input_grad: float32 [16, 448, 1024], P(('fsdp', 'replica'), 'seq')
- grad_norm1_gain: float32 [2, 1024], P(None, ('fsdp', 'seq'))
- grad_norm1_bias: float32 [2, 1024], P(None, ('fsdp', 'seq'))
- grad_qkv_weight: float32 [2, 1024, 3072], P(None, ('fsdp', 'seq'))
- grad_query_bias: float32 [2, 1024], P(None, ('fsdp', 'seq'))
- grad_value_bias: float32 [2, 1024], P(None, ('fsdp', 'seq'))
- grad_proj_weight: float32 [2, 1024, 1024], P(None, ('fsdp', 'seq'))
- grad_proj_bias: float32 [2, 1024], P(None, ('fsdp', 'seq'))
- grad_norm2_gain: float32 [2, 1024], P(None, ('fsdp', 'seq'))
- grad_norm2_bias: float32 [2, 1024], P(None, ('fsdp', 'seq'))
- grad_up_weight: float32 [2, 1024, 4096], P(None, ('fsdp', 'seq'))
- grad_up_bias: float32 [2, 4096], P(None, ('fsdp', 'seq'))
- grad_down_weight: float32 [2, 4096, 1024], P(None, ('fsdp', 'seq'))
- grad_down_bias: float32 [2, 1024], P(None, ('fsdp', 'seq'))
All inputs are finite; a program needn't handle non-finite values. No bound on the sum of `clip_mask` on one device may be relied on, other than what follows from the above.
Results may differ from a plain program's by a relative error of at most 0.013.
Values may be sent and summed in bfloat16 or wider, within the bound.
No kernel may reach another device: no remote copies, remote signals or barrier semaphores. Data moves between devices by JAX's collectives and lax.ppermute only.
A program may use at most 256 MiB of HBM per device.

v0:
```python
import jax
import jax.numpy as jnp
from jax import lax
from jax.sharding import PartitionSpec as P

HEADS = 16
LAYERS = 2


norm_eps = 1e-06


def layer_norm(inputs, gain, shift):
    center = inputs - jnp.mean(inputs, axis=-1, keepdims=True)
    spread = jnp.mean(center * center, axis=-1, keepdims=True)
    return center * lax.rsqrt(spread + norm_eps) * gain + shift


def exact_gelu(inputs):
    return jax.nn.gelu(inputs, approximate=False)


def widen(array):
    return array.astype(jnp.float32)


def fetch_layer(params, layer_at):
    parts = [weight[layer_at] for weight in params]
    return (
        lax.all_gather(parts[0], ("fsdp", "seq"), axis=0, tiled=True),
        lax.all_gather(parts[1], ("fsdp", "seq"), axis=0, tiled=True),
        lax.all_gather(parts[2], ("fsdp", "seq"), axis=0, tiled=True),
        lax.all_gather(parts[3], ("fsdp", "seq"), axis=0, tiled=True),
        lax.all_gather(parts[4], ("fsdp", "seq"), axis=0, tiled=True),
        lax.all_gather(parts[5], ("fsdp", "seq"), axis=0, tiled=True),
        lax.all_gather(parts[6], ("fsdp", "seq"), axis=0, tiled=True),
        lax.all_gather(parts[7], ("fsdp", "seq"), axis=0, tiled=True),
        lax.all_gather(parts[8], ("fsdp", "seq"), axis=0, tiled=True),
        lax.all_gather(parts[9], ("fsdp", "seq"), axis=0, tiled=True),
        lax.all_gather(parts[10], ("fsdp", "seq"), axis=0, tiled=True),
        lax.all_gather(parts[11], ("fsdp", "seq"), axis=0, tiled=True),
        lax.all_gather(parts[12], ("fsdp", "seq"), axis=0, tiled=True),
    )


def fetch_again(params, layer_at):
    parts = [weight[layer_at] for weight in params]
    return (
        lax.all_gather(parts[0], ("fsdp", "seq"), axis=0, tiled=True),
        lax.all_gather(parts[1], ("fsdp", "seq"), axis=0, tiled=True),
        lax.all_gather(parts[2], ("fsdp", "seq"), axis=0, tiled=True),
        lax.all_gather(parts[3], ("fsdp", "seq"), axis=0, tiled=True),
        lax.all_gather(parts[4], ("fsdp", "seq"), axis=0, tiled=True),
        lax.all_gather(parts[5], ("fsdp", "seq"), axis=0, tiled=True),
        lax.all_gather(parts[6], ("fsdp", "seq"), axis=0, tiled=True),
        lax.all_gather(parts[7], ("fsdp", "seq"), axis=0, tiled=True),
        lax.all_gather(parts[8], ("fsdp", "seq"), axis=0, tiled=True),
        lax.all_gather(parts[9], ("fsdp", "seq"), axis=0, tiled=True),
        lax.all_gather(parts[10], ("fsdp", "seq"), axis=0, tiled=True),
        lax.all_gather(parts[11], ("fsdp", "seq"), axis=0, tiled=True),
        lax.all_gather(parts[12], ("fsdp", "seq"), axis=0, tiled=True),
    )


def reduce_grads(grads):
    shares = (
        lax.psum_scatter(grads[0], ("fsdp", "seq"), scatter_dimension=0, tiled=True),
        lax.psum_scatter(grads[1], ("fsdp", "seq"), scatter_dimension=0, tiled=True),
        lax.psum_scatter(grads[2], ("fsdp", "seq"), scatter_dimension=0, tiled=True),
        lax.psum_scatter(grads[3], ("fsdp", "seq"), scatter_dimension=0, tiled=True),
        lax.psum_scatter(grads[4], ("fsdp", "seq"), scatter_dimension=0, tiled=True),
        lax.psum_scatter(grads[5], ("fsdp", "seq"), scatter_dimension=0, tiled=True),
        lax.psum_scatter(grads[6], ("fsdp", "seq"), scatter_dimension=0, tiled=True),
        lax.psum_scatter(grads[7], ("fsdp", "seq"), scatter_dimension=0, tiled=True),
        lax.psum_scatter(grads[8], ("fsdp", "seq"), scatter_dimension=0, tiled=True),
        lax.psum_scatter(grads[9], ("fsdp", "seq"), scatter_dimension=0, tiled=True),
        lax.psum_scatter(grads[10], ("fsdp", "seq"), scatter_dimension=0, tiled=True),
        lax.psum_scatter(grads[11], ("fsdp", "seq"), scatter_dimension=0, tiled=True),
        lax.psum_scatter(grads[12], ("fsdp", "seq"), scatter_dimension=0, tiled=True),
    )
    return (
        lax.psum(shares[0].astype(jnp.bfloat16), "replica").astype(jnp.float32),
        lax.psum(shares[1].astype(jnp.bfloat16), "replica").astype(jnp.float32),
        lax.psum(shares[2].astype(jnp.bfloat16), "replica").astype(jnp.float32),
        lax.psum(shares[3].astype(jnp.bfloat16), "replica").astype(jnp.float32),
        lax.psum(shares[4].astype(jnp.bfloat16), "replica").astype(jnp.float32),
        lax.psum(shares[5].astype(jnp.bfloat16), "replica").astype(jnp.float32),
        lax.psum(shares[6].astype(jnp.bfloat16), "replica").astype(jnp.float32),
        lax.psum(shares[7].astype(jnp.bfloat16), "replica").astype(jnp.float32),
        lax.psum(shares[8].astype(jnp.bfloat16), "replica").astype(jnp.float32),
        lax.psum(shares[9].astype(jnp.bfloat16), "replica").astype(jnp.float32),
        lax.psum(shares[10].astype(jnp.bfloat16), "replica").astype(jnp.float32),
        lax.psum(shares[11].astype(jnp.bfloat16), "replica").astype(jnp.float32),
        lax.psum(shares[12].astype(jnp.bfloat16), "replica").astype(jnp.float32),
    )


def forward_layer(resid, weights):
    (
        gain_one,
        shift_one,
        qkv_weight,
        query_bias,
        value_bias,
        proj_weight,
        proj_bias,
        gain_two,
        shift_two,
        up_weight,
        up_bias,
        down_weight,
        down_bias,
    ) = weights
    clip_count, tok_count, width = resid.shape
    head_size = width // HEADS
    normed = layer_norm(resid, widen(gain_one), widen(shift_one)).astype(jnp.bfloat16)
    joined = jnp.einsum("ctd,de->cte", normed, qkv_weight, preferred_element_type=jnp.float32)
    queries = ((joined[..., :width] + widen(query_bias)) * 0.125).astype(jnp.bfloat16)
    keys_local = joined[..., width : 2 * width].astype(jnp.bfloat16)
    values_local = (joined[..., 2 * width :] + widen(value_bias)).astype(jnp.bfloat16)
    keys_all, values_all = (
        lax.all_gather(keys_local, "seq", axis=1, tiled=True),
        lax.all_gather(values_local, "seq", axis=1, tiled=True),
    )
    key_count = keys_all.shape[1]
    query_heads = queries.reshape(clip_count, tok_count, HEADS, head_size)
    key_heads = keys_all.reshape(clip_count, key_count, HEADS, head_size)
    value_heads = values_all.reshape(clip_count, key_count, HEADS, head_size)
    scores = jnp.einsum(
        "cqhd,ckhd->chqk", query_heads, key_heads, preferred_element_type=jnp.float32
    )
    peak = jnp.max(scores, axis=-1, keepdims=True)
    expd = jnp.exp(scores - peak)
    total = jnp.sum(expd, axis=-1, keepdims=True)
    probs = (expd / total).astype(jnp.bfloat16)
    log_total = peak + jnp.log(total)
    attended = jnp.einsum("chqk,ckhd->cqhd", probs, value_heads, preferred_element_type=jnp.float32)
    attended = attended.reshape(clip_count, tok_count, width).astype(jnp.bfloat16)
    branch = jnp.einsum(
        "ctd,de->cte", attended, proj_weight, preferred_element_type=jnp.float32
    ) + widen(proj_bias)
    mid = resid + branch
    normed_two = layer_norm(mid, widen(gain_two), widen(shift_two)).astype(jnp.bfloat16)
    pre = jnp.einsum(
        "ctd,df->ctf", normed_two, up_weight, preferred_element_type=jnp.float32
    ) + widen(up_bias)
    active = exact_gelu(pre).astype(jnp.bfloat16)
    mlp_out = jnp.einsum(
        "ctf,fd->ctd", active, down_weight, preferred_element_type=jnp.float32
    ) + widen(down_bias)
    kept = (
        resid,
        normed,
        query_heads,
        key_heads,
        value_heads,
        log_total,
        attended,
        mid,
        normed_two,
        pre,
        active,
    )
    return (mid + mlp_out, kept)


def backward_layer(grad, weights, kept):
    (
        gain_one,
        shift_one,
        qkv_weight,
        query_bias,
        value_bias,
        proj_weight,
        proj_bias,
        gain_two,
        shift_two,
        up_weight,
        up_bias,
        down_weight,
        down_bias,
    ) = weights
    (
        resid,
        normed,
        query_heads,
        key_heads,
        value_heads,
        log_total,
        attended,
        mid,
        normed_two,
        pre,
        active,
    ) = kept
    clip_count, tok_count, width = resid.shape
    head_size = width // HEADS
    key_count = key_heads.shape[1]
    d_mlp = grad.astype(jnp.bfloat16)
    down_weight_grad = jnp.einsum("ctf,cte->fe", active, d_mlp, preferred_element_type=jnp.float32)
    down_bias_grad = jnp.sum(widen(d_mlp), axis=(0, 1))
    d_active = jnp.einsum("cte,fe->ctf", d_mlp, down_weight, preferred_element_type=jnp.float32)
    gelu_back = jax.vjp(exact_gelu, pre)[1]
    d_pre = gelu_back(d_active)[0].astype(jnp.bfloat16)
    up_weight_grad = jnp.einsum(
        "ctd,ctf->df", normed_two, d_pre, preferred_element_type=jnp.float32
    )
    up_bias_grad = jnp.sum(widen(d_pre), axis=(0, 1))
    d_normed_two = jnp.einsum("ctf,df->ctd", d_pre, up_weight, preferred_element_type=jnp.float32)
    norm_back_two = jax.vjp(layer_norm, mid, widen(gain_two), widen(shift_two))[1]
    d_mid_norm, gain_two_grad, shift_two_grad = norm_back_two(d_normed_two)
    d_mid = grad + d_mid_norm
    d_branch = d_mid.astype(jnp.bfloat16)
    proj_weight_grad = jnp.einsum(
        "ctd,cte->de", attended, d_branch, preferred_element_type=jnp.float32
    )
    proj_bias_grad = jnp.sum(widen(d_branch), axis=(0, 1))
    d_attended = jnp.einsum(
        "cte,de->ctd", d_branch, proj_weight, preferred_element_type=jnp.float32
    )
    d_attended = d_attended.astype(jnp.bfloat16).reshape(clip_count, tok_count, HEADS, head_size)
    scores = jnp.einsum(
        "cqhd,ckhd->chqk", query_heads, key_heads, preferred_element_type=jnp.float32
    )
    probs_full = jnp.exp(scores - log_total)
    probs = probs_full.astype(jnp.bfloat16)
    d_probs = jnp.einsum(
        "cqhd,ckhd->chqk", d_attended, value_heads, preferred_element_type=jnp.float32
    )
    d_values_all = jnp.einsum(
        "chqk,cqhd->ckhd", probs, d_attended, preferred_element_type=jnp.float32
    )
    d_scores = probs_full * (d_probs - jnp.sum(probs_full * d_probs, axis=-1, keepdims=True))
    d_scores = d_scores.astype(jnp.bfloat16)
    d_queries = jnp.einsum(
        "chqk,ckhd->cqhd", d_scores, key_heads, preferred_element_type=jnp.float32
    )
    d_keys_all = jnp.einsum(
        "chqk,cqhd->ckhd", d_scores, query_heads, preferred_element_type=jnp.float32
    )
    d_keys, d_values = (
        lax.psum_scatter(
            d_keys_all.reshape(clip_count, key_count, width).astype(jnp.bfloat16),
            "seq",
            scatter_dimension=1,
            tiled=True,
        ).astype(jnp.float32),
        lax.psum_scatter(
            d_values_all.reshape(clip_count, key_count, width).astype(jnp.bfloat16),
            "seq",
            scatter_dimension=1,
            tiled=True,
        ).astype(jnp.float32),
    )
    d_query_scaled = d_queries.astype(jnp.bfloat16).reshape(clip_count, tok_count, width) * 0.125
    d_keys_low = d_keys.astype(jnp.bfloat16)
    d_values_low = d_values.astype(jnp.bfloat16)
    d_joined = jnp.concatenate([d_query_scaled, d_keys_low, d_values_low], axis=-1)
    qkv_weight_grad = jnp.einsum(
        "ctd,cte->de", normed, d_joined, preferred_element_type=jnp.float32
    )
    query_bias_grad = jnp.sum(widen(d_query_scaled), axis=(0, 1))
    value_bias_grad = jnp.sum(widen(d_values_low), axis=(0, 1))
    d_normed = jnp.einsum("cte,de->ctd", d_joined, qkv_weight, preferred_element_type=jnp.float32)
    norm_back_one = jax.vjp(layer_norm, resid, widen(gain_one), widen(shift_one))[1]
    d_resid_norm, gain_one_grad, shift_one_grad = norm_back_one(d_normed)
    grads = (
        gain_one_grad,
        shift_one_grad,
        qkv_weight_grad,
        query_bias_grad,
        value_bias_grad,
        proj_weight_grad,
        proj_bias_grad,
        gain_two_grad,
        shift_two_grad,
        up_weight_grad,
        up_bias_grad,
        down_weight_grad,
        down_bias_grad,
    )
    return (d_mid + d_resid_norm, grads)


def on_device(
    clips_in,
    cotangent,
    clip_mask,
    norm1_gain,
    norm1_bias,
    qkv_weight,
    query_bias,
    value_bias,
    proj_weight,
    proj_bias,
    norm2_gain,
    norm2_bias,
    up_weight,
    up_bias,
    down_weight,
    down_bias,
):
    params = (
        norm1_gain,
        norm1_bias,
        qkv_weight,
        query_bias,
        value_bias,
        proj_weight,
        proj_bias,
        norm2_gain,
        norm2_bias,
        up_weight,
        up_bias,
        down_weight,
        down_bias,
    )
    resid = widen(clips_in)
    stash = []
    first_weights = []
    for layer_at in range(LAYERS):
        weights = fetch_layer(params, layer_at)
        resid, kept = forward_layer(resid, weights)
        stash.append(kept)
        first_weights.append(weights)
    clips_out = resid.astype(jnp.bfloat16)
    grad = widen(cotangent) * widen(clip_mask)[:, None, None]
    layer_grads = [None] * LAYERS
    for layer_at in reversed(range(LAYERS)):
        weights = fetch_again(params, layer_at)
        grad, grads = backward_layer(grad, weights, stash[layer_at])
        layer_grads[layer_at] = reduce_grads(grads)
    stacked = [
        jnp.stack([layer_grads[layer_at][which] for layer_at in range(LAYERS)], axis=0)
        for which in range(13)
    ]
    return (
        clips_out,
        grad,
        stacked[0],
        stacked[1],
        stacked[2],
        stacked[3],
        stacked[4],
        stacked[5],
        stacked[6],
        stacked[7],
        stacked[8],
        stacked[9],
        stacked[10],
        stacked[11],
        stacked[12],
    )


def solution(mesh):
    return jax.shard_map(
        on_device,
        mesh=mesh,
        in_specs=(
            P(("fsdp", "replica"), "seq", None),
            P(("fsdp", "replica"), "seq", None),
            P(("fsdp", "replica")),
            P(None, ("fsdp", "seq")),
            P(None, ("fsdp", "seq")),
            P(None, ("fsdp", "seq"), None),
            P(None, ("fsdp", "seq")),
            P(None, ("fsdp", "seq")),
            P(None, ("fsdp", "seq"), None),
            P(None, ("fsdp", "seq")),
            P(None, ("fsdp", "seq")),
            P(None, ("fsdp", "seq")),
            P(None, ("fsdp", "seq"), None),
            P(None, ("fsdp", "seq")),
            P(None, ("fsdp", "seq"), None),
            P(None, ("fsdp", "seq")),
        ),
        out_specs=(
            P(("fsdp", "replica"), "seq", None),
            P(("fsdp", "replica"), "seq", None),
            P(None, ("fsdp", "seq")),
            P(None, ("fsdp", "seq")),
            P(None, ("fsdp", "seq"), None),
            P(None, ("fsdp", "seq")),
            P(None, ("fsdp", "seq")),
            P(None, ("fsdp", "seq"), None),
            P(None, ("fsdp", "seq")),
            P(None, ("fsdp", "seq")),
            P(None, ("fsdp", "seq")),
            P(None, ("fsdp", "seq"), None),
            P(None, ("fsdp", "seq")),
            P(None, ("fsdp", "seq"), None),
            P(None, ("fsdp", "seq")),
        ),
        check_vma=False,
    )
```

profile of v0, /device:TPU:0, one launch (start us, length us, event | category | flops | bytes accessed | tf_op | source)
XLA Modules:
  0.0 1922.8 jit_solution(17729268449949438481)
XLA Ops:
  23.1 65.8 %all-reduce.35 = (bf16[1024]{0:T(1024)(128)(2,1)S(1)}, bf16[1024]{0:T(1024)(128)(2,1)S(1)}, bf16[1024]{0:T(1024)(128)(2,1)S(1)}, bf16[1024]{0:T(1024)(128)(2,1)S...) all-reduce(bf16[1024]{0:T(1024)(128)(2,1)S(1)} %dynamic-update-slic, ...), channel_id=3, replica_groups=mesh['fsdp'=8,'seq'=2,'replica'=2] {'fsdp','seq'}, use_global_device_ids=true, to_apply=%add.1 | all-reduce | flops 16384 | bytes 65536
  89.1 17.2 all-gather.23
  106.3 19.3 %all-gather.10 = bf16[1,4096]{1,0:T(2,128)(2,1)S(1)} all-gather(bf16[1,256]{1,0:T(2,128)(2,1)S(1)} %get-tuple-element.113), channel_id=12, replica_groups=mesh['fsdp'=8,'seq'=2,'replica'=2] {'fsdp','seq'}, dimensions={1}, use_global_device_ids=true | all-gather | bytes 8704 | tf_op jit(solution)/shard_map/all_gather | solution.py:40
  125.9 4.8 fusion.34
  134.3 3.1 all_gather.106
  143.1 3.3 fusion.95
  149.3 45.1 %all-gather.39.cloned.1.call-done = bf16[1,1024,4096]{2,1,0:T(8,128)(2,1)} async-done(((bf16[1,64,4096]{2,1,0:T(8,128)(2,1)}), bf16[1,1024,4096]{2,1,0:T(8,128)(2,1)}) %all-gather.39.cloned.1.call-update) | async-done | bytes 8388624 | tf_op jit(solution)/shard_map/all_gather | solution.py:39
  194.4 14.3 multiply_convert_fusion.3
  208.7 61.2 %all-gather.41.cloned.1.call-done = bf16[1,4096,1024]{2,1,0:T(8,128)(2,1)} async-done(((bf16[1,256,1024]{2,1,0:T(8,128)(2,1)}), bf16[1,4096,1024]{2,1,0:T(8,128)(2,1)}) %all-gather.41.cloned.1.call-update) | async-done | bytes 8388624 | tf_op jit(solution)/shard_map/all_gather | solution.py:41
  269.9 6.1 fusion.224
  276.3 56.3 %all-gather.43.cloned.1.call-done = bf16[1,1024,3072]{2,1,0:T(8,128)(2,1)} async-done(((bf16[1,64,3072]{2,1,0:T(8,128)(2,1)}), bf16[1,1024,3072]{2,1,0:T(8,128)(2,1)}) %all-gather.43.cloned.1.call-update) | async-done | bytes 6291472 | tf_op jit(solution)/shard_map/all_gather | solution.py:32
  332.6 4.5 fusion.37
  342.4 4.5 all_gather.121
  353.4 3.3 fusion.94
  356.7 18.2 all-gather.45.cloned.1.call-done
  377.8 73.0 %all-gather.47.cloned.1.call-done = bf16[1,1024,4096]{2,1,0:T(8,128)(2,1)} async-done(((bf16[1,64,4096]{2,1,0:T(8,128)(2,1)}), bf16[1,1024,4096]{2,1,0:T(8,128)(2,1)}) %all-gather.47.cloned.1.call-update) | async-done | bytes 8388624 | tf_op jit(solution)/shard_map/all_gather | solution.py:39
  450.7 14.5 multiply_convert_fusion.2
  465.2 60.6 %all-gather.49.cloned.1.call-done = bf16[1,4096,1024]{2,1,0:T(8,128)(2,1)} async-done(((bf16[1,256,1024]{2,1,0:T(8,128)(2,1)}), bf16[1,4096,1024]{2,1,0:T(8,128)(2,1)}) %all-gather.49.cloned.1.call-update) | async-done | bytes 8388624 | tf_op jit(solution)/shard_map/all_gather | solution.py:41
  525.8 9.6 convert_reduce_fusion
  535.4 2.8 fusion.143
  544.2 5.6 fusion.72
  549.8 6.0 copy.65
  555.9 2.7 copy.81
  558.7 6.0 multiply_reduce_fusion.1
  564.7 4.1 multiply_convert_fusion.1
  572.4 6.0 copy.63
  578.4 2.7 copy.82
  581.3 4.5 convert_reduce_fusion.5
  588.2 2.9 copy.66
  593.7 3.0 copy.64
  596.7 5.6 fusion.145
  603.2 12.0 convert_reduce_fusion.1
  615.3 2.8 fusion.144
  623.2 5.4 fusion.75
  628.6 6.0 copy.69
  634.6 2.7 copy.79
  637.4 5.7 multiply_reduce_fusion
  643.1 4.2 multiply_convert_fusion
  650.9 6.1 copy.67
  656.9 2.7 copy.80
  659.8 3.7 fusion.163
  663.6 4.0 fusion.157
  667.7 7.7 fusion.151
  675.5 4.6 convert_reduce_fusion.6
  682.6 3.1 copy.70
  688.2 3.0 copy.68
  691.2 8.0 fusion.150
  700.2 9.7 fusion.166
  710.0 9.8 fusion.201
  720.4 9.8 fusion.206
  731.4 9.6 fusion.160
  744.0 6.8 fusion.119
  755.3 65.2 %reduce-scatter.25.cloned.1.call-done = f32[64,1024]{1,0:T(8,128)} async-done(((f32[1024,1024]{1,0:T(8,128)}), f32[64,1024]{1,0:T(8,128)}) %reduce-scatter.25.cloned.1.call-update) | async-done | bytes 262160 | tf_op jit(solution)/shard_map/reduce_scatter | solution.py:72
  822.2 136.2 %reduce-scatter.23.cloned.1.call-done = f32[64,3072]{1,0:T(8,128)} async-done(((f32[1024,3072]{1,0:T(8,128)}), f32[64,3072]{1,0:T(8,128)}) %reduce-scatter.23.cloned.1.call-update) | async-done | bytes 786448 | tf_op jit(solution)/shard_map/reduce_scatter | solution.py:69
  960.4 136.2 %reduce-scatter.21.cloned.1.call-done = f32[64,3072]{1,0:T(8,128)} async-done(((f32[1024,3072]{1,0:T(8,128)}), f32[64,3072]{1,0:T(8,128)}) %reduce-scatter.21.cloned.1.call-update) | async-done | bytes 786448 | tf_op jit(solution)/shard_map/reduce_scatter | solution.py:69
  1098.5 178.6 %reduce-scatter.35.cloned.1.call-done = f32[256,1024]{1,0:T(8,128)} async-done(((f32[4096,1024]{1,0:T(8,128)}), f32[256,1024]{1,0:T(8,128)}) %reduce-scatter.35.cloned.1.call-update) | async-done | bytes 1048592 | tf_op jit(solution)/shard_map/reduce_scatter | solution.py:78
  1279.2 178.3 %reduce-scatter.31.cloned.1.call-done = f32[64,4096]{1,0:T(8,128)} async-done(((f32[1024,4096]{1,0:T(8,128)}), f32[64,4096]{1,0:T(8,128)}) %reduce-scatter.31.cloned.1.call-update) | async-done | bytes 1048592 | tf_op jit(solution)/shard_map/reduce_scatter | solution.py:76
  1459.6 178.5 %reduce-scatter.29.cloned.1.call-done = f32[64,4096]{1,0:T(8,128)} async-done(((f32[1024,4096]{1,0:T(8,128)}), f32[64,4096]{1,0:T(8,128)}) %reduce-scatter.29.cloned.1.call-update) | async-done | bytes 1048592 | tf_op jit(solution)/shard_map/reduce_scatter | solution.py:76
  1640.1 178.3 %reduce-scatter.33.cloned.1.call-done = f32[256,1024]{1,0:T(8,128)} async-done(((f32[4096,1024]{1,0:T(8,128)}), f32[256,1024]{1,0:T(8,128)}) %reduce-scatter.33.cloned.1.call-update) | async-done | bytes 1048592 | tf_op jit(solution)/shard_map/reduce_scatter | solution.py:78
  1820.6 5.2 fusion.136
  1828.1 60.4 %all-reduce.34 = (bf16[1024]{0:T(1024)(128)(2,1)S(1)}, bf16[1024]{0:T(1024)(128)(2,1)S(1)}, bf16[1024]{0:T(1024)(128)(2,1)S(1)}, bf16[1024]{0:T(1024)(128)(2,1)S...) all-reduce(f32[1024]{0:T(1024)S(1)} %get-tuple-element.19, ...), channel_id=33, replica_groups=mesh['fsdp'=8,'seq'=2,'replica'=2] {'fsdp','seq'}, use_global_device_ids=true, to_apply=%region_30.0.clone | all-reduce | flops 24576 | bytes 147456
  1889.2 8.7 all-reduce.36
  1904.4 2.7 all-reduce.40.cloned.1.call-done
  1911.4 2.7 maximum_convert_fusion
  (341 shorter events, 108.7 us)
Async XLA Ops:
  7.2 6.5 copy-start.35
  7.2 118.7 %all-gather.35.cloned.1.call-start = ((), (), s32[]{:S(2)}) async-start(), calls=%async_computation.20 | async-start | bytes 6684672 | tf_op jit(solution)/shard_map/all_gather | solution.py:32
  9.4 8.8 copy-start.4
  9.4 137.1 %all-gather.37.cloned.1.call-start = ((), (), s32[]{:S(2)}) async-start(), calls=%async_computation.21 | async-start | bytes 2228224 | tf_op jit(solution)/shard_map/all_gather | solution.py:35
  11.2 7.1 copy-start.53
  11.2 7.1 copy-start.54
  11.2 7.1 copy-start.55
  11.2 7.2 copy-start.56
  11.2 7.2 copy-start.57
  11.3 7.2 copy-start.58
  11.3 7.2 copy-start.59
  11.3 7.2 copy-start.60
  11.3 7.2 copy-start.52
  11.3 77.6 %copy-start.50 = (bf16[2,256]{1,0:T(2,128)(2,1)S(1)}, bf16[2,256]{1,0:T(2,128)(2,1)}, u32[]{:S(2)}) copy-start(bf16[2,256]{1,0:T(2,128)(2,1)} %param.29) | copy-start | bytes 3076
  11.3 183.1 %all-gather.39.cloned.1.call-start = ((), (), s32[]{:S(2)}) async-start(), calls=%async_computation.22 | async-start | bytes 8912896 | tf_op jit(solution)/shard_map/all_gather | solution.py:39
  13.7 256.3 %all-gather.41.cloned.1.call-start = ((), (), s32[]{:S(2)}) async-start(), calls=%async_computation.23 | async-start | bytes 8912896 | tf_op jit(solution)/shard_map/all_gather | solution.py:41
  14.8 317.9 %all-gather.43.cloned.1.call-start = ((), (), s32[]{:S(2)}) async-start(), calls=%async_computation.24 | async-start | bytes 6684672 | tf_op jit(solution)/shard_map/all_gather | solution.py:32
  15.4 359.6 %all-gather.45.cloned.1.call-start = ((), (), s32[]{:S(2)}) async-start(), calls=%async_computation.25 | async-start | bytes 2228224 | tf_op jit(solution)/shard_map/all_gather | solution.py:35
  15.9 434.8 %all-gather.47.cloned.1.call-start = ((), (), s32[]{:S(2)}) async-start(), calls=%async_computation.26 | async-start | bytes 8912896 | tf_op jit(solution)/shard_map/all_gather | solution.py:39
  16.7 509.1 %all-gather.49.cloned.1.call-start = ((), (), s32[]{:S(2)}) async-start(), calls=%async_computation.27 | async-start | bytes 8912896 | tf_op jit(solution)/shard_map/all_gather | solution.py:41
  17.4 568.3 %reduce-scatter.39.cloned.1.call-start = ((), (), s32[]{:S(2)}) async-start(), calls=%async_computation.29 | async-start | bytes 1376256
  18.3 112.4 %copy-start.44 = (f32[224]{0:T(256)}, f32[224]{0:T(256)S(1)}, u32[]{:S(2)}) copy-start(f32[224]{0:T(256)S(1)} %broadcast_multiply_fusion.3) | copy-start | bytes 2692
  88.9 41.9 %copy-start.42 = (f32[1024]{0:T(1024)}, f32[1024]{0:T(1024)S(1)}, u32[]{:S(2)}) copy-start(f32[1024]{0:T(1024)S(1)} %convert_element_type.565) | copy-start | bytes 12292
  88.9 37.0 %copy-start.40 = (f32[1024]{0:T(1024)}, f32[1024]{0:T(1024)S(1)}, u32[]{:S(2)}) copy-start(f32[1024]{0:T(1024)S(1)} %convert_element_type.564) | copy-start | bytes 12292
  89.0 105.4 %copy-start.38 = (f32[1024]{0:T(1024)}, f32[1024]{0:T(1024)S(1)}, u32[]{:S(2)}) copy-start(f32[1024]{0:T(1024)S(1)} %convert_element_type.570) | copy-start | bytes 12292
  125.8 4.9 copy-start.48
  125.8 4.9 copy-start.46
  131.3 8.8 copy-start.14
  134.3 5.8 copy-start.8
  342.4 8.0 copy-start.9
  525.8 9.6 copy-start.61
  535.4 4.2 copy-start.21
  558.6 32.4 %reduce-scatter.37.cloned.1.call-start = ((), (), s32[]{:S(2)}) async-start(), calls=%async_computation.28 | async-start | bytes 1376256
  581.2 99.0 %reduce-scatter.43.cloned.1.call-start = ((), (), s32[]{:S(2)}) async-start(), calls=%async_computation.31 | async-start | bytes 1376256
  591.0 11.2 copy-start.16
  596.7 6.0 copy-start.13
  596.7 6.0 copy-start.22
  602.3 13.0 slice-start
  603.2 15.3 copy-start.6
  603.2 12.1 slice-start.1
  637.4 48.4 %reduce-scatter.41.cloned.1.call-start = ((), (), s32[]{:S(2)}) async-start(), calls=%async_computation.30 | async-start | bytes 1376256
  643.1 6.0 copy-start.15
  650.9 8.9 copy-start.30
  659.7 94.0 %reduce-scatter.27.cloned.1.call-start = ((), (), s32[]{:S(2)}) async-start(), calls=%async_computation.15 | async-start | bytes 4456448 | tf_op jit(solution)/shard_map/reduce_scatter | solution.py:72
  663.5 4.2 copy-start.17
  663.5 157.0 %reduce-scatter.25.cloned.1.call-start = ((), (), s32[]{:S(2)}) async-start(), calls=%async_computation.14 | async-start | bytes 4456448 | tf_op jit(solution)/shard_map/reduce_scatter | solution.py:72
  667.6 290.8 %reduce-scatter.23.cloned.1.call-start = ((), (), s32[]{:S(2)}) async-start(), calls=%async_computation.13 | async-start | bytes 13369344 | tf_op jit(solution)/shard_map/reduce_scatter | solution.py:69
  675.5 421.1 %reduce-scatter.21.cloned.1.call-start = ((), (), s32[]{:S(2)}) async-start(), calls=%async_computation.12 | async-start | bytes 13369344 | tf_op jit(solution)/shard_map/reduce_scatter | solution.py:69
  680.1 11.1 copy-start.5
  680.1 11.1 copy-start.41
  680.1 11.1 copy-start.43
  680.1 11.1 copy-start.45
  680.1 11.1 copy-start.47
  699.2 577.9 %reduce-scatter.35.cloned.1.call-start = ((), (), s32[]{:S(2)}) async-start(), calls=%async_computation.19 | async-start | bytes 17825792 | tf_op jit(solution)/shard_map/reduce_scatter | solution.py:78
  709.9 747.6 %reduce-scatter.31.cloned.1.call-start = ((), (), s32[]{:S(2)}) async-start(), calls=%async_computation.17 | async-start | bytes 17825792 | tf_op jit(solution)/shard_map/reduce_scatter | solution.py:76
  719.8 918.3 %reduce-scatter.29.cloned.1.call-start = ((), (), s32[]{:S(2)}) async-start(), calls=%async_computation.16 | async-start | bytes 17825792 | tf_op jit(solution)/shard_map/reduce_scatter | solution.py:76
  730.3 1088.2 %reduce-scatter.33.cloned.1.call-start = ((), (), s32[]{:S(2)}) async-start(), calls=%async_computation.18 | async-start | bytes 17825792 | tf_op jit(solution)/shard_map/reduce_scatter | solution.py:78
  741.1 1166.1 %all-reduce.40.cloned.1.call-start = ((), (), s32[]{:S(2)}) async-start(), calls=%async_computation.32 | async-start | bytes 6291456 | tf_op jit(solution)/shard_map/psum | solution.py:84
  1279.2 541.4 %copy-start.18 = (bf16[1,224,1024]{1,2,0:T(8,128)(2,1)S(1)}, bf16[1,224,1024]{1,2,0:T(8,128)(2,1)}, u32[]{:S(2)}) copy-start(bf16[1,224,1024]{1,2,0:T(8,128)(2,1)} %copy.70) | copy-start | bytes 1376260
  1279.2 541.4 %copy-start.27 = (bf16[16,64,224]{2,1,0:T(8,128)(2,1)S(1)}, bf16[16,64,224]{2,1,0:T(8,128)(2,1)}, u32[]{:S(2)}) copy-start(bf16[16,64,224]{2,1,0:T(8,128)(2,1)} %get-tuple-element.156) | copy-start | bytes 1376260
  1820.6 6.9 copy-start.49
  1825.9 77.2 %copy-start.11 = (f32[1,224,1024]{2,1,0:T(8,128)S(1)}, f32[1,224,1024]{2,1,0:T(8,128)}, u32[]{:S(2)}) copy-start(f32[1,224,1024]{2,1,0:T(8,128)} %copy-done.10) | copy-start | bytes 2752516
  1907.1 6.9 copy-start.36
  1907.1 6.9 copy-start.37
  (21 other events, 37.9 us)
Sparse Core Ops, SparseCore 0:
  10.9 64.8 all-gather.34
  78.4 40.1 all-gather.36
  121.3 72.9 all-gather.38
  197.0 72.9 all-gather.40
  272.6 59.9 all-gather.42
  334.7 40.2 all-gather.44
  377.7 73.0 all-gather.46
  452.9 72.8 all-gather.48
  558.7 6.8 reduce-scatter.38
  581.3 7.1 reduce-scatter.36
  637.5 7.1 reduce-scatter.42
  659.8 7.3 reduce-scatter.40
  671.1 73.9 reduce-scatter.26
  748.8 71.7 reduce-scatter.24
  824.5 133.9 reduce-scatter.22
  962.3 134.1 reduce-scatter.20
  1100.5 176.5 reduce-scatter.34
  1281.1 176.4 reduce-scatter.30
  1461.6 176.4 reduce-scatter.28
  1642.0 176.4 reduce-scatter.32
  1821.8 85.3 all-reduce.39
where the time goes:
time: 1930 us; the launch traced here: 1920 us
  waiting for transfers between devices  1370 us (71%)
  matrix products  204 us (11%)
  blocking collectives  184 us (10%)
  local copies, waits for them, and re-layouts  90.5 us (5%)
  other arithmetic  52.9 us (3%)
    reduce_scatter x2, waiting for transfers between devices, reduce_grads(): lax.psum_scatter(grads[11], ('fsdp', 'seq'), scatter_dimension=0, tiled=T...  357 us
    reduce_scatter x2, waiting for transfers between devices, reduce_grads(): lax.psum_scatter(grads[9], ('fsdp', 'seq'), scatter_dimension=0, tiled=True)  357 us
    reduce_scatter x2, waiting for transfers between devices, reduce_grads(): lax.psum_scatter(grads[2], ('fsdp', 'seq'), scatter_dimension=0, tiled=True)  272 us
    unnamed x2, blocking collectives  126 us
    all_gather x2, waiting for transfers between devices, fetch_layer(): lax.all_gather(parts[11], ('fsdp', 'seq'), axis=0, tiled=True)  122 us
    all_gather x2, waiting for transfers between devices, fetch_layer(): lax.all_gather(parts[9], ('fsdp', 'seq'), axis=0, tiled=True)  118 us
    unnamed x187, local copies, waits for them, and re-layouts  73.2 us
    reduce_scatter x2, waiting for transfers between devices, reduce_grads(): lax.psum_scatter(grads[5], ('fsdp', 'seq'), scatter_dimension=0, tiled=True)  65.3 us
  transfers between devices with their start and end apart: 21, of which 14 were waited for; matrix products, arithmetic and copies ran while one was open for 13% of the time, Pallas kernels for 0%

commit v1 on v0

v1 whole, which is shorter than its diff:
```python
import functools

import jax
import jax.numpy as jnp
from jax import lax
from jax.experimental import pallas as pl
from jax.experimental.pallas import tpu as pltpu
from jax.sharding import PartitionSpec as P


HEADS = 16
LAYERS = 2
norm_eps = 1e-06
bf16 = jnp.bfloat16
f32 = jnp.float32


def widen(array):
    return array.astype(f32)


def dot(a, b, dims):
    return lax.dot_general(a, b, (dims, ((), ())), preferred_element_type=f32)


def mm(a, b):
    return dot(a, b, ((1,), (0,)))


def mm_t(a, b):
    return dot(a, b, ((1,), (1,)))


def t_mm(a, b):
    return dot(a, b, ((0,), (0,)))


PAIR = [(0, 1), (1, 0)]


def core_swap(v):
    return lax.ppermute(v, "seq", PAIR)


def y_swap(v):
    return lax.ppermute(v, "replica", PAIR)


def x_swap(v, n):
    return lax.ppermute(v, "fsdp", [(f, f ^ 1) for f in range(n)])


def z_from(v, k, n):
    nz = n // 2
    return lax.ppermute(
        v, "fsdp", [(((z + k) % nz) * 2 + x, z * 2 + x) for z in range(nz) for x in range(2)]
    )


def pick(array, axis, at):
    return lax.dynamic_index_in_dim(array, at, axis, keepdims=False)


TILE = 32
COLS = 256
VMEM_LIMIT = 14 * 1024 * 1024


def call(body, outs, args, flops, transcendentals=0, scratch=()):
    touched = sum(a.size * a.dtype.itemsize for a in args)
    outs = tuple(jax.ShapeDtypeStruct(shape, dtype) for shape, dtype in outs)
    touched = touched + sum(o.size * o.dtype.itemsize for o in outs)
    return pl.pallas_call(
        body,
        out_shape=outs,
        scratch_shapes=list(scratch),
        compiler_params=pltpu.CompilerParams(vmem_limit_bytes=VMEM_LIMIT),
        cost_estimate=pl.CostEstimate(
            flops=flops, bytes_accessed=touched, transcendentals=transcendentals
        ),
    )(*args)


def norm_parts(inputs):
    center = inputs - jnp.mean(inputs, axis=-1, keepdims=True)
    spread = jnp.mean(center * center, axis=-1, keepdims=True)
    scale = lax.rsqrt(spread + norm_eps)
    return center * scale, scale


def norm_grad(e, inputs, gain):
    unit, scale = norm_parts(inputs)
    eg = e * gain
    d = scale * (
        eg
        - jnp.mean(eg, axis=-1, keepdims=True)
        - unit * jnp.mean(eg * unit, axis=-1, keepdims=True)
    )
    return d, e * unit


def eight(v):
    return jnp.sum(v.reshape(v.shape[0] // 8, 8, v.shape[1]), axis=0)


def by_rows(half_rows, step):
    for half in range(2):

        @pl.loop(0, half_rows // TILE)
        def _(i):
            start = pl.multiple_of(i * TILE, TILE)
            step(pl.ds(half * half_rows + start, TILE), half, pl.ds(start, TILE))


def by_cols(width, step):
    @pl.loop(0, width // COLS)
    def _(i):
        step(pl.ds(pl.multiple_of(i * COLS, COLS), COLS))


def summed(sent, whole, half, part):
    rows = sent[1].shape[0] // 2
    side = pl.ds((1 - half) * rows + part.start, TILE)
    total = sent[0][whole, :] + widen(sent[1][side, :])
    return total + widen(sent[2 + half][part, :])


def put_part(part_ref, low_ref, cols, value):
    part_ref[:, cols] = value
    low_ref[:, cols] = value.astype(bf16)


def heads_of(ref, width, size, h):
    return [ref[:, i * width + h * size : i * width + (h + 1) * size] for i in range(3)]


def attend_body(first, heads, size, *refs):
    if first:
        base, vec, w_qkv, fix, w_proj, normed, qkv, attended, part, low = refs
        sent = None
    else:
        base, s0, s1, s2, s3, vec, w_qkv, fix, w_proj = refs[:9]
        resid, normed, qkv, attended, part, low = refs[9:]
        sent = (s0, s1, s2, s3)
    width = heads * size

    def norm(whole, half, part_rows):
        value = widen(base[whole, :])
        if sent is not None:
            value = value + (summed(sent, whole, half, part_rows) + vec[2:3, :])
            resid[whole, :] = value
        unit, _ = norm_parts(value)
        normed[whole, :] = (unit * vec[0:1, :] + vec[1:2, :]).astype(bf16)

    by_rows(base.shape[0] // 2, norm)

    def project(cols):
        value = (mm(normed[...], w_qkv[:, cols]) + fix[0:1, cols]) * fix[1:2, cols]
        qkv[:, cols] = value.astype(bf16)

    by_cols(3 * width, project)
    for h in range(heads):
        q, k, v = heads_of(qkv, width, size, h)
        s = mm_t(q, k)
        e = jnp.exp(s - jnp.max(s, axis=-1, keepdims=True))
        p = (e / jnp.sum(e, axis=-1, keepdims=True)).astype(bf16)
        attended[:, h * size : (h + 1) * size] = mm(p, v).astype(bf16)
    by_cols(part.shape[1], lambda cols: put_part(part, low, cols, mm(attended[...], w_proj[:, cols])))


def attend(base, sent, vec, w_qkv, fix, w_proj, heads, size):
    toks, width = base.shape
    first = sent is None
    outs = [((toks, width), bf16), ((toks, 3 * heads * size), bf16)]
    outs = outs + [((toks, heads * size), bf16), ((toks, width), f32), ((toks, width), bf16)]
    if not first:
        outs = [((toks, width), f32)] + outs
    args = [base, *(sent or ()), vec, w_qkv, fix, w_proj]
    flops = 8 * toks * width * heads * size + 4 * heads * toks * toks * size
    got = call(
        functools.partial(attend_body, first, heads, size), outs, args, flops, heads * toks * toks
    )
    return got if not first else (base, *got)


ROOT_HALF = 0.7071067811865476
ROOT_TWO_PI_INV = 0.3989422804014327


def widen_body(base, s0, s1, s2, s3, vec, w_up, up_b, mid, normed, active, slope):
    sent = (s0, s1, s2, s3)

    def norm(whole, half, part_rows):
        value = widen(base[whole, :])
        value = value + (summed(sent, whole, half, part_rows) + vec[2:3, :])
        mid[whole, :] = value
        unit, _ = norm_parts(value)
        normed[whole, :] = (unit * vec[0:1, :] + vec[1:2, :]).astype(bf16)

    by_rows(base.shape[0] // 2, norm)

    def up(cols):
        pre = mm(normed[...], w_up[:, cols]) + up_b[:, cols]
        half = 0.5 * (1.0 + lax.erf(pre * ROOT_HALF))
        active[:, cols] = (pre * half).astype(bf16)
        slope[:, cols] = half + pre * (ROOT_TWO_PI_INV * jnp.exp(-0.5 * pre * pre))

    by_cols(w_up.shape[1], up)


def go_up(base, sent, vec, w_up, up_b):
    toks, width = base.shape
    hid = w_up.shape[1]
    outs = [((toks, width), f32), ((toks, width), bf16)]
    outs = outs + [((toks, hid), bf16), ((toks, hid), f32)]
    args = [base, *sent, vec, w_up, up_b]
    return call(widen_body, outs, args, 2 * toks * width * hid, toks * hid)


def down_body(active, w_down, part, low):
    by_cols(part.shape[1], lambda cols: put_part(part, low, cols, mm(active[...], w_down[:, cols])))


def go_down(active, w_down):
    shape = (active.shape[0], w_down.shape[1])
    flops = 2 * active.size * w_down.shape[1]
    return call(down_body, [(shape, f32), (shape, bf16)], [active, w_down], flops)


def mlp_back_tail(d_mlp, slope, w_down, w_up, d_pre, part, low, up_sum):
    def back(cols):
        value = (mm_t(d_mlp[...], w_down[cols, :]) * slope[:, cols]).astype(bf16)
        d_pre[:, cols] = value
        up_sum[:, cols] = eight(widen(value))

    by_cols(w_down.shape[0], back)
    by_cols(part.shape[1], lambda cols: put_part(part, low, cols, mm_t(d_pre[...], w_up[cols, :])))


def mlp_back_first(d_mlp, slope, w_down, w_up, d_pre, part, low, up_sum):
    mlp_back_tail(d_mlp, slope, w_down, w_up, d_pre, part, low, up_sum)


def mlp_back_body(base, d_mid, s0, s1, s2, s3, vec, slope, w_down, w_up, *outs):
    grad, d_mlp, d_pre, part, low, up_sum, sums = outs
    sums[...] = jnp.zeros_like(sums)

    def norm(whole, half, part_rows):
        e = summed((s0, s1, s2, s3), whole, half, part_rows)
        d, by_gain = norm_grad(e, widen(base[whole, :]), vec[0:1, :])
        value = d_mid[whole, :] + d
        grad[whole, :] = value
        low_value = value.astype(bf16)
        d_mlp[whole, :] = low_value
        sums[0:8, :] += eight(by_gain)
        sums[8:16, :] += eight(e)
        sums[16:24, :] += eight(widen(low_value))

    by_rows(base.shape[0] // 2, norm)
    mlp_back_tail(d_mlp, slope, w_down, w_up, d_pre, part, low, up_sum)


def mlp_back(first, base, d_mid, sent, vec, slope, w_down, w_up):
    toks, hid = slope.shape
    width = w_up.shape[0]
    outs = [((toks, hid), bf16), ((toks, width), f32), ((toks, width), bf16), ((8, hid), f32)]
    flops = 4 * toks * hid * width
    if first is not None:
        args = [first, slope, w_down, w_up]
        return call(mlp_back_first, outs, args, flops)
    outs = [((toks, width), f32), ((toks, width), bf16), *outs, ((24, width), f32)]
    args = [base, d_mid, *sent, vec, slope, w_down, w_up]
    return call(mlp_back_body, outs, args, flops)


def attend_back_body(heads, size, grad, mid, s0, s1, s2, s3, vec, qkv, w_proj, w_qkv, *refs):
    d_mid, d_branch, d_joined, part, low, sums, joined_sum, d_att = refs
    width = heads * size
    sums[...] = jnp.zeros_like(sums)

    def norm(whole, half, part_rows):
        e = summed((s0, s1, s2, s3), whole, half, part_rows)
        d, by_gain = norm_grad(e, mid[whole, :], vec[0:1, :])
        value = widen(grad[whole, :]) + d
        d_mid[whole, :] = value
        low_value = value.astype(bf16)
        d_branch[whole, :] = low_value
        sums[0:8, :] += eight(by_gain)
        sums[8:16, :] += eight(e)
        sums[16:24, :] += eight(widen(low_value))

    by_rows(mid.shape[0] // 2, norm)
    d_att[...] = mm_t(d_branch[...], w_proj[...]).astype(bf16)
    for h in range(heads):
        q, k, v = heads_of(qkv, width, size, h)
        d = d_att[:, h * size : (h + 1) * size]
        s = mm_t(q, k)
        e = jnp.exp(s - jnp.max(s, axis=-1, keepdims=True))
        p = e / jnp.sum(e, axis=-1, keepdims=True)
        dp = mm_t(d, v)
        ds = (p * (dp - jnp.sum(p * dp, axis=-1, keepdims=True))).astype(bf16)
        dq = (widen(mm(ds, k).astype(bf16)) * 0.125).astype(bf16)
        dk = t_mm(ds, q).astype(bf16)
        dv = t_mm(p.astype(bf16), d).astype(bf16)
        for i, value in enumerate((dq, dk, dv)):
            d_joined[:, i * width + h * size : i * width + (h + 1) * size] = value
    joined_sum[...] = eight(widen(d_joined[...]))
    by_cols(
        part.shape[1], lambda cols: put_part(part, low, cols, mm_t(d_joined[...], w_qkv[cols, :]))
    )


def attend_back(grad, mid, sent, vec, qkv, w_proj, w_qkv, heads, size):
    toks, width = mid.shape
    wide = 3 * heads * size
    outs = [((toks, width), f32), ((toks, width), bf16), ((toks, wide), bf16)]
    outs = outs + [((toks, width), f32), ((toks, width), bf16)]
    outs = outs + [((24, width), f32), ((8, wide), f32)]
    args = [grad, mid, *sent, vec, qkv, w_proj, w_qkv]
    flops = 8 * toks * width * heads * size + 10 * heads * toks * toks * size
    return call(
        functools.partial(attend_back_body, heads, size),
        outs,
        args,
        flops,
        heads * toks * toks,
        [pltpu.VMEM((toks, heads * size), bf16)],
    )


def last_body(base, d_mid, s0, s1, s2, s3, vec, grad, sums):
    sums[...] = jnp.zeros_like(sums)

    def norm(whole, half, part_rows):
        e = summed((s0, s1, s2, s3), whole, half, part_rows)
        d, by_gain = norm_grad(e, widen(base[whole, :]), vec[0:1, :])
        grad[whole, :] = d_mid[whole, :] + d
        sums[0:8, :] += eight(by_gain)
        sums[8:16, :] += eight(e)

    by_rows(base.shape[0] // 2, norm)


def last_back(base, d_mid, sent, vec):
    outs = [(base.shape, f32), ((16, base.shape[1]), f32)]
    return call(last_body, outs, [base, d_mid, *sent, vec], 20 * base.size)


def place_body(count, rows, extra, at_ref, *refs):
    blocks, outs, sems = refs[:count], refs[count:-1], refs[-1]
    copies = []
    for i in range(count):
        start = pl.multiple_of(at_ref[i] * rows, rows)
        source = blocks[i].at[pl.ds(0, rows)] if extra else blocks[i]
        copies.append(
            pltpu.make_async_copy(source, outs[0].at[pl.ds(start, rows)], sems.at[0, i])
        )
        if extra:
            start = pl.multiple_of(at_ref[i] * extra, extra)
            copies.append(
                pltpu.make_async_copy(
                    blocks[i].at[pl.ds(rows, extra)],
                    outs[1].at[pl.ds(start, extra)],
                    sems.at[1, i],
                )
            )
    for copy in copies:
        copy.start()
    for copy in copies:
        copy.wait()


def place(blocks, at, extra):
    count, (rows, cols) = len(blocks), blocks[0].shape
    outs = [jax.ShapeDtypeStruct((count * (rows - extra), cols), bf16)]
    if extra:
        outs.append(jax.ShapeDtypeStruct((count * extra, cols), bf16))
    return pl.pallas_call(
        functools.partial(place_body, count, rows - extra, extra),
        grid_spec=pltpu.PrefetchScalarGridSpec(
            num_scalar_prefetch=1,
            grid=(),
            in_specs=[pl.BlockSpec(memory_space=pltpu.VMEM)] * count,
            out_specs=[pl.BlockSpec(memory_space=pl.ANY)] * len(outs),
            scratch_shapes=[pltpu.SemaphoreType.DMA((2, count))],
        ),
        out_shape=tuple(outs),
        compiler_params=pltpu.CompilerParams(vmem_limit_bytes=VMEM_LIMIT),
        cost_estimate=pl.CostEstimate(
            flops=0, bytes_accessed=4 * count * rows * cols, transcendentals=0
        ),
        name="place",
    )(at, *blocks)


def gather_rows(unit, me, n, extra=0):
    nz = n // 2
    blocks = [unit] + [z_from(unit, k, n) for k in range(1, nz)]
    blocks = blocks + [x_swap(block, n) for block in blocks]
    z, x = me // 2, me % 2
    at = [((z + k) % nz) * 2 + x for k in range(nz)]
    at = at + [((z + k) % nz) * 2 + 1 - x for k in range(nz)]
    return place(blocks, jnp.stack(at).astype(jnp.int32), extra)


def gather_line(unit, me, n):
    nz = n // 2
    blocks = [unit] + [z_from(unit, k, n) for k in range(1, nz)]
    z = me // 2
    at = jnp.stack([(z + k) % nz for k in range(nz)]).astype(jnp.int32)
    return place(blocks, at, 0)[0]


def scatter_line(grad, me, n):
    nz = n // 2
    z = me // 2
    total = widen(pick(grad, 0, z))
    for k in range(1, nz):
        sent = pick(grad, 0, (z - k) % nz)
        came = z_from(sent, k, n)
        total = total + widen(came)
    return total


def scatter_rows(grad, me, n):
    nz = n // 2
    rows = grad.shape[0] // n
    blocks = grad.reshape(nz, 2, rows, grad.shape[1])
    x = me % 2
    sent = pick(blocks, 1, 1 - x)
    other = x_swap(sent, n)
    summed_low = (widen(pick(blocks, 1, x)) + widen(other)).astype(grad.dtype)
    return scatter_line(summed_low, me, n)


def send_part(part, low):
    side = core_swap(low)
    half = part.shape[0] // 2
    mine = (part[:half] + widen(side[half:])).astype(bf16)
    across = y_swap(mine)
    beside = core_swap(across)
    return part, side, across, beside


def on_device(
    clips_in,
    cotangent,
    clip_mask,
    norm1_gain,
    norm1_bias,
    qkv_weight,
    query_bias,
    value_bias,
    proj_weight,
    proj_bias,
    norm2_gain,
    norm2_bias,
    up_weight,
    up_bias,
    down_weight,
    down_bias,
    *,
    n,
):
    c, y, f = lax.axis_index("seq"), lax.axis_index("replica"), lax.axis_index("fsdp")
    quarter = 2 * y + c
    toks, width = clips_in.shape[1], clips_in.shape[2]
    rows = qkv_weight.shape[1]
    hid_rows = down_weight.shape[1]
    hidden = up_weight.shape[2]
    size = width // HEADS
    heads = HEADS // 4
    fast = n == 8 and rows == size and hid_rows == 4 * rows

    def pair_tokens(own):
        side = core_swap(own)
        across = y_swap(own)
        beside = core_swap(across)
        mine = jnp.concatenate([own, side], axis=0)
        other = jnp.concatenate([across, beside], axis=0)
        return jnp.where(y == 0, mine, other), jnp.where(y == 0, other, mine)

    def qkv_cols(w, at):
        w = w.reshape(*w.shape[:-1], 3, heads, 4, size)
        return pick(w, w.ndim - 2, at).reshape(*w.shape[:-4], 3 * heads * size)

    def up_cols(w, at_c, at_y):
        w = w.reshape(*w.shape[:-1], n, 2, 2, hid_rows // 2)
        w = pick(w, w.ndim - 2, at_y)
        return pick(w, w.ndim - 2, at_c).reshape(*w.shape[:-3], hidden // 4)

    def both(mine, theirs, axis):
        return jnp.where(
            c == 0,
            jnp.concatenate([mine, theirs], axis=axis),
            jnp.concatenate([theirs, mine], axis=axis),
        )

    flat = [
        norm1_gain,
        norm1_bias,
        query_bias,
        value_bias,
        proj_bias,
        norm2_gain,
        norm2_bias,
        down_bias,
    ]
    packed = jnp.concatenate(flat + [up_bias], axis=1)
    weights = []
    if fast:
        theirs = qkv_cols(qkv_weight, 2 * y + 1 - c)
        small = jnp.concatenate([packed, jnp.zeros((6, packed.shape[1]), bf16)], axis=0)
        theirs = jnp.concatenate([theirs.reshape(2 * rows, -1), small], axis=0)
        theirs = core_swap(theirs)
        mine = qkv_cols(qkv_weight, quarter)
        qkv_units = [
            both(mine[layer], theirs[layer * rows : (layer + 1) * rows], 0)
            for layer in range(LAYERS)
        ]
        side = theirs[2 * rows : 2 * rows + LAYERS]
        spare = jnp.zeros((16 - 2 * LAYERS, packed.shape[1]), bf16)
        qkv_units[0] = jnp.concatenate([qkv_units[0], both(packed, side, 0), spare], axis=0)
        up_units = both(up_cols(up_weight, c, y), core_swap(up_cols(up_weight, 1 - c, y)), 1)
        down_units = lax.dynamic_slice_in_dim(
            down_weight, y * (hid_rows // 2), hid_rows // 2, axis=1
        )
        proj_units = jnp.where(f % 2 == y, proj_weight, x_swap(proj_weight, n))
        everything = None
        for layer in range(LAYERS):
            extra = 16 if layer == 0 else 0
            got = gather_rows(qkv_units[layer], f, n, extra)
            if extra:
                everything = got[1].reshape(n, 16, -1)[:, : 2 * LAYERS]
                everything = everything.reshape(n, 2, LAYERS, -1).reshape(2 * n, LAYERS, -1)
            weights.append(
                (
                    got[0],
                    gather_line(proj_units[layer], f, n),
                    gather_rows(up_units[layer], f, n)[0],
                    gather_rows(down_units[layer], f, n)[0],
                )
            )
    else:
        everything = lax.all_gather(packed, ("fsdp", "seq"), axis=0)
        for layer in range(LAYERS):
            full = [
                lax.all_gather(w[layer], ("fsdp", "seq"), axis=0, tiled=True)
                for w in (qkv_weight, proj_weight, up_weight, down_weight)
            ]
            by_head = full[1].reshape(heads, 4, size, width)
            by_hid = full[3].reshape(n, 2, 2, hid_rows // 2, width)
            weights.append(
                (
                    qkv_cols(full[0], quarter),
                    pick(by_head, 1, quarter).reshape(heads * size, width),
                    up_cols(full[2], c, y),
                    pick(pick(by_hid, 2, y), 1, c).reshape(hidden // 4, width),
                )
            )

    smalls = []
    for layer in range(LAYERS):
        here = everything[:, layer]
        vectors = here[:, : 8 * rows].reshape(2 * n, 8, rows).transpose(1, 0, 2)
        vectors = widen(vectors.reshape(8, width))
        up_b = here[:, 8 * rows :].reshape(n, 2, 2, hid_rows // 2)
        up_b = widen(pick(pick(up_b, 2, y), 1, c).reshape(1, hidden // 4))
        by_head = vectors.reshape(8, heads, 4, size)
        by_head = pick(by_head, 2, quarter).reshape(8, heads * size)
        zero = jnp.zeros_like(by_head[0])
        add = jnp.concatenate([by_head[2], zero, by_head[3]])
        times = jnp.concatenate([zero + 0.125, zero + 1.0, zero + 1.0])
        smalls.append((vectors, jnp.stack([add, times]), up_b))

    streams = range(2)
    resid = list(pair_tokens(clips_in[0]))
    sent = [None, None]
    stash = []
    for layer in range(LAYERS):
        vectors, fix, up_b = smalls[layer]
        w_qkv, w_proj, w_up, w_down = weights[layer]
        past = smalls[layer - 1][0][7] if layer else vectors[7]
        vec_one = jnp.stack([vectors[0], vectors[1], past])
        vec_two = jnp.stack([vectors[5], vectors[6], vectors[4]])
        kept = []
        for s in streams:
            before, normed, qkv, attended, part, low = attend(
                resid[s], sent[s], vec_one, w_qkv, fix, w_proj, heads, size
            )
            got = send_part(part, low)
            mid, normed_two, active, slope = go_up(before, got, vec_two, w_up, up_b)
            kept.append((before, normed, qkv, attended, mid, normed_two, active, slope))
            part, low = go_down(active, w_down)
            sent[s] = send_part(part, low)
            resid[s] = mid
        stash.append(kept)

    def own_rows(pair):
        return jnp.where(y == 0, pair[0][:toks], pair[1][:toks])

    whole = [
        resid[s][:toks]
        + (
            (sent[s][0][:toks] + widen(sent[s][1][toks:])) + widen(sent[s][2])
            + smalls[-1][0][7]
        )
        for s in streams
    ]
    clips_out = own_rows(whole).astype(bf16)[None]

    masked = (widen(cotangent[0]) * widen(clip_mask)[0]).astype(bf16)
    start = pair_tokens(masked)
    grads = [None] * LAYERS
    mlp_sums = [None] * LAYERS
    att_sums = [None] * LAYERS
    d_mid, sent = [None, None], [None, None]

    def both_t_mm(left, right):
        return t_mm(
            jnp.concatenate(left, axis=0), jnp.concatenate(right, axis=0)
        ).astype(bf16)

    norm_one_sums = [None] * LAYERS
    for layer in reversed(range(LAYERS)):
        vectors = smalls[layer][0]
        w_qkv, w_proj, w_up, w_down = weights[layer]
        kept = stash[layer]
        d_mlp, d_pre, d_branch, d_joined, grad = [], [], [], [], []
        ups, sums = [], []
        last = layer == LAYERS - 1
        for s in streams:
            slope = kept[s][7]
            if last:
                got = mlp_back(start[s], None, None, None, None, slope, w_down, w_up)
                grad.append(start[s])
                d_mlp.append(start[s])
            else:
                after = stash[layer + 1][s][0]
                vec = smalls[layer + 1][0][0:1]
                got = mlp_back(None, after, d_mid[s], sent[s], vec, slope, w_down, w_up)
                grad.append(got[0])
                d_mlp.append(got[1])
                sums.append(got[6])
                got = got[2:6]
            d_pre.append(got[0])
            ups.append(got[3])
            sent[s] = send_part(got[1], got[2])
        if last:
            down_sum = sum(jnp.sum(widen(d), axis=0) for d in d_mlp)
        else:
            total = jnp.sum((sums[0] + sums[1]).reshape(3, 8, width), axis=1)
            norm_one_sums[layer + 1] = total[:2]
            down_sum = total[2]
        g_down = both_t_mm([k[6] for k in kept], d_mlp)
        g_up = both_t_mm([k[5] for k in kept], d_pre)
        mlp_sums[layer] = (down_sum, jnp.sum(ups[0] + ups[1], axis=0))
        sums, joined = [], []
        for s in streams:
            _, _, qkv, _, mid = kept[s][:5]
            got = attend_back(grad[s], mid, sent[s], vectors[5:6], qkv, w_proj, w_qkv, heads, size)
            d_mid[s] = got[0]
            d_branch.append(got[1])
            d_joined.append(got[2])
            sums.append(got[5])
            joined.append(got[6])
            sent[s] = send_part(got[3], got[4])
        g_proj = both_t_mm([k[3] for k in kept], d_branch)
        g_qkv = both_t_mm([k[1] for k in kept], d_joined)
        total = jnp.sum((sums[0] + sums[1]).reshape(3, 8, width), axis=1)
        att_sums[layer] = (total, jnp.sum(joined[0] + joined[1], axis=0))
        grads[layer] = (g_qkv, g_proj, g_up, g_down)
    final = [last_back(stash[0][s][0], d_mid[s], sent[s], smalls[0][0][0:1]) for s in streams]
    total = jnp.sum((final[0][1] + final[1][1]).reshape(2, 8, width), axis=1)
    norm_one_sums[0] = total
    input_grad = own_rows([final[0][0], final[1][0]])[None]

    here = (jnp.arange(4) == quarter).reshape(1, 1, 4, 1)
    at_c = (jnp.arange(2) == c).reshape(1, 2, 1, 1)
    at_y = (jnp.arange(2) == y).reshape(1, 1, 2, 1)
    by_owner = []
    for layer in range(LAYERS):
        att, joined = att_sums[layer]
        down_sum, up_sum = mlp_sums[layer]
        joined = joined.reshape(3, heads, 1, size)[0::2]
        joined = jnp.where(here, joined, 0.0).reshape(2, width)
        alike = [norm_one_sums[layer], att, down_sum[None]]
        alike = 0.25 * jnp.concatenate(alike, axis=0)
        vecs = jnp.concatenate([alike, joined], axis=0)
        vecs = vecs.reshape(8, 2 * n, rows).transpose(1, 0, 2).reshape(n, 2, 8 * rows)
        up = jnp.where(at_c & at_y, up_sum.reshape(n, 1, 1, hid_rows // 2), 0.0)
        by_owner.append(jnp.concatenate([vecs, up.reshape(n, 2, hid_rows)], axis=2))
    by_owner = jnp.stack(by_owner, axis=2)
    if fast:
        tiny = by_owner.reshape(n * 2 * LAYERS, -1)
        tiny = scatter_rows(tiny, f, n).reshape(2, LAYERS, -1)
        tiny = pick(tiny, 0, c) + core_swap(pick(tiny, 0, 1 - c))
        tiny = tiny + y_swap(tiny)
    else:
        total = lax.psum(by_owner, ("fsdp", "seq", "replica"))
        tiny = pick(pick(total, 0, f), 0, c)
    vec = tiny[:, : 8 * rows].reshape(LAYERS, 8, rows)
    up_bias_grad = tiny[:, 8 * rows :]

    def in_order(mine, theirs, first):
        return jnp.where(first == 0, mine, theirs), jnp.where(first == 0, theirs, mine)

    def to_rows(grad):
        halves = grad.reshape(2, rows, grad.shape[1])
        theirs = core_swap(pick(halves, 0, 1 - c).astype(bf16))
        pair = jnp.stack(in_order(pick(halves, 0, c), widen(theirs), c), axis=1)
        across = widen(y_swap(pair.astype(bf16)))
        return jnp.concatenate(in_order(pair, across, y), axis=1)

    outs = []
    for layer in range(LAYERS):
        g_qkv, g_proj, g_up, g_down = grads[layer]
        if fast:
            g = to_rows(scatter_rows(g_qkv, f, n))
            g = g.reshape(rows, 4, 3, heads, size).transpose(0, 2, 3, 1, 4)
            qkv_out = g.reshape(rows, 3 * width)
            g = scatter_line(g_proj.reshape(n // 2, rows, width), f, n)
            g = g + widen(x_swap(g.astype(bf16), n))
            proj_out = jnp.where(f % 2 == y, g, widen(y_swap(g.astype(bf16))))
            g = to_rows(scatter_rows(g_up, f, n))
            g = g.reshape(rows, 2, 2, n, hid_rows // 2).transpose(0, 3, 2, 1, 4)
            up_out = g.reshape(rows, hidden)
            g = scatter_rows(g_down, f, n)
            across = widen(y_swap(g.astype(bf16)))
            down_out = jnp.concatenate(in_order(g, across, y), axis=0)
        else:
            axes = ("replica", "seq")

            def owned(full):
                block = lax.psum_scatter(full, "fsdp", scatter_dimension=0, tiled=True)
                half = block.shape[0] // 2
                return widen(lax.dynamic_slice_in_dim(block, c * half, half, axis=0))

            g = lax.all_gather(g_qkv, axes, axis=0).reshape(4, width, 3, heads, size)
            qkv_out = owned(g.transpose(1, 2, 3, 0, 4).reshape(width, 3 * width))
            g = lax.all_gather(g_proj, axes, axis=0).reshape(4, heads, size, width)
            proj_out = owned(g.transpose(1, 0, 2, 3).reshape(width, width))
            g = lax.all_gather(g_up, axes, axis=0)
            g = g.reshape(2, 2, width, n, hid_rows // 2)
            up_out = owned(g.transpose(2, 3, 1, 0, 4).reshape(width, hidden))
            g = lax.all_gather(g_down, axes, axis=0)
            g = g.reshape(2, 2, n, hid_rows // 2, width)
            down_out = owned(g.transpose(2, 1, 0, 3, 4).reshape(hidden, width))
        outs.append((qkv_out, proj_out, up_out, down_out))
    qkv_out, proj_out, up_out, down_out = [
        jnp.stack([outs[layer][i] for layer in range(LAYERS)]) for i in range(4)
    ]
    return (
        clips_out,
        input_grad,
        vec[:, 0],
        vec[:, 1],
        qkv_out,
        vec[:, 6],
        vec[:, 7],
        proj_out,
        vec[:, 4],
        vec[:, 2],
        vec[:, 3],
        up_out,
        up_bias_grad,
        down_out,
        vec[:, 5],
    )


def solution(mesh):
    tokens = P(("fsdp", "replica"), "seq", None)
    vector = P(None, ("fsdp", "seq"))
    matrix = P(None, ("fsdp", "seq"), None)
    kinds = [
        vector,
        vector,
        matrix,
        vector,
        vector,
        matrix,
        vector,
        vector,
        vector,
        matrix,
        vector,
        matrix,
        vector,
    ]
    return jax.shard_map(
        functools.partial(on_device, n=mesh.shape["fsdp"]),
        mesh=mesh,
        in_specs=(tokens, tokens, P(("fsdp", "replica")), *kinds),
        out_specs=(tokens, tokens, *kinds),
        check_vma=False,
    )
```

time: 1930 us -> 961 us (0.50)
  waiting for transfers between devices: 1370 us -> 355 us
  matrix products: 204 us -> 18.6 us
  blocking collectives: 184 us -> 0 us
  Pallas kernels: 0 us -> 176 us
  starting transfers between devices: 1.33 us -> 173 us
  local copies, waits for them, and re-layouts: 90.5 us -> 175 us
    reduce_scatter x8 -> x0, waiting for transfers between devices: 1050 us -> none  [the longest x2 357 us: reduce_grads(): lax.psum_scatter(grads[11], ('fsdp', 'seq'), scatter_dimension=0, tiled=T...]
    ppermute x0 -> x153, waiting for transfers between devices: none -> 355 us  [the longest x51 149 us: z_from(): lax.ppermute(v, 'fsdp', [((z + k) % nz * 2 + x, z * 2 + x) for z in range...]
    all_gather x8 -> x0, waiting for transfers between devices: 315 us -> none  [the longest x2 122 us: fetch_layer(): lax.all_gather(parts[11], ('fsdp', 'seq'), axis=0, tiled=True)]
    dot_general x36 -> x8, matrix products: 204 us -> 18.6 us  [dot(): return lax.dot_general(a, b, (dims, ((), ())), preferred_element_type=f32)]
    pallas_call x0 -> x30, Pallas kernels: none -> 176 us  [the longest x22 160 us: call(): pl.pallas_call(body, out_shape=outs, scratch_shapes=list(scratch), compil...]
    ppermute x0 -> x153, starting transfers between devices: none -> 173 us  [the longest x51 98.4 us: z_from(): lax.ppermute(v, 'fsdp', [((z + k) % nz * 2 + x, z * 2 + x) for z in range...]
    unnamed x2 -> x0, blocking collectives: 126 us -> none
    all_gather x6 -> x0, blocking collectives: 49 us -> none  [the longest x2 36.4 us: fetch_layer(): lax.all_gather(parts[10], ('fsdp', 'seq'), axis=0, tiled=True)]
  transfers between devices with their start and end apart: 21 -> 153, of which waited for: 14 -> 61; matrix products, arithmetic and copies ran while one was open for 13% -> 15% of each run, Pallas kernels for 0% -> 17%
where the time goes in v1:
time: 961 us; the launch traced here: 952 us
  waiting for transfers between devices  355 us (37%)
  Pallas kernels  176 us (18%)
  local copies, waits for them, and re-layouts  175 us (18%)
  starting transfers between devices  173 us (18%)
  other arithmetic  50 us (5%)
  matrix products  18.6 us (2%)
    pallas_call x22, Pallas kernels, call(): pl.pallas_call(body, out_shape=outs, scratch_shapes=list(scratch), compil...  160 us
    ppermute x51, waiting for transfers between devices, z_from(): lax.ppermute(v, 'fsdp', [((z + k) % nz * 2 + x, z * 2 + x) for z in range...  149 us
    ppermute x34, waiting for transfers between devices, x_swap(): return lax.ppermute(v, 'fsdp', [(f, f ^ 1) for f in range(n)])  147 us
    unnamed x490, local copies, waits for them, and re-layouts  99.7 us
    ppermute x51, starting transfers between devices, z_from(): lax.ppermute(v, 'fsdp', [((z + k) % nz * 2 + x, z * 2 + x) for z in range...  98.4 us
    ppermute x27, waiting for transfers between devices, y_swap(): return lax.ppermute(v, 'replica', PAIR)  57.7 us
    ppermute x34, starting transfers between devices, x_swap(): return lax.ppermute(v, 'fsdp', [(f, f ^ 1) for f in range(n)])  39.3 us
    ppermute x27, starting transfers between devices, y_swap(): return lax.ppermute(v, 'replica', PAIR)  29.6 us
  transfers between devices with their start and end apart: 153, of which 61 were waited for; matrix products, arithmetic and copies ran while one was open for 15% of the time, Pallas kernels for 17%

profile of v1, /device:TPU:0, one launch (start us, length us, event | category | flops | bytes accessed | tf_op | source)
XLA Modules:
  0.0 952.2 jit_solution(2506256192793169924)
XLA Ops:
  27.4 11.5 %collective-permute-done.13.refs_2_ = bf16[64,1024]{1,0:T(8,128)(2,1)S(1)} collective-permute-done((bf16[64,1024]{1,0:T(8,128)(2,1)S(1)}, bf16[64,1024]{1,0:T(8,128)(2,1)S(1)}, u32[]{:S(2)}, u32[]{:S(2)}) %collective-permute-start.13) | collective-permute-done | bytes 131104 | tf_op jit(solution)/shard_map/ppermute | solution.py:55
  39.5 6.8 collective-permute-done.12.refs_1_
  54.6 4.7 collective-permute-done.10.refs_7_
  59.4 4.7 collective-permute-done.9.refs_6_
  64.1 3.8 collective-permute-done.8.refs_5_
  82.3 8.6 shard_map.277
  96.6 5.1 dynamic-slice_reduce_fusion.2
  103.9 8.6 shard_map.271
  117.7 5.3 collective-permute-start.28
  131.2 8.4 collective-permute-done.27.refs_2_
  150.5 4.1 collective-permute-done.31.refs_6_
  154.6 6.7 collective-permute-start.21
  161.4 3.5 collective-permute-start.20
  164.8 5.1 collective-permute-start.19
  175.6 4.6 collective-permute-done.20.refs_2_
  190.1 3.9 collective-permute-done.23.refs_5_
  202.3 6.8 shard_map.278
  213.0 7.1 shard_map.272
  242.5 4.2 collective-permute-done.44.refs_2_
  252.4 4.0 collective-permute-done.38.refs_3_
  256.9 6.9 collective-permute-done.37.refs_2_
  279.4 10.3 %shard_map.280 = (f32[448,1024]{1,0:T(8,128)S(1)}, bf16[448,1024]{1,0:T(8,128)(2,1)S(1)}, bf16[448,768]{1,0:T(8,128)(2,1)S(1)}, bf16[448,256]{1,0:T(8,128)(2,1)S...) custom-call(f32[448,1024]{1,0:T(8,128)S(1)} %copy-done.21, f32[448,1024]{1,0:T(8,128)S(1)} %copy-done.59, ...), custom_call_target="tpu_custom_call" | custom-call | flops 1145044992 | bytes 14043136 | tf_op jit(solution)/shard_map/pallas_call | solution.py:73
  296.3 10.0 %shard_map.274 = (f32[448,1024]{1,0:T(8,128)S(1)}, bf16[448,1024]{1,0:T(8,128)(2,1)S(1)}, bf16[448,768]{1,0:T(8,128)(2,1)S(1)}, bf16[448,256]{1,0:T(8,128)(2,1)S...) custom-call(f32[448,1024]{1,0:T(8,128)S(1)} %copy-done.18, f32[448,1024]{1,0:T(8,128)S(1)} %copy-done.57, ...), custom_call_target="tpu_custom_call" | custom-call | flops 1145044992 | bytes 14043136 | tf_op jit(solution)/shard_map/pallas_call | solution.py:73
  316.8 8.6 collective-permute-done.77
  331.9 7.2 collective-permute-done.60.refs_5_
  341.8 5.1 collective-permute-done.50.refs_2_
  396.3 6.7 shard_map.281
  403.1 3.6 shard_map.288
  409.1 6.6 shard_map.275
  419.9 3.6 shard_map.283
  429.8 23.0 %collective-permute-done.137 = bf16[4,128,1024]{2,1,0:T(8,128)(2,1)S(1)} collective-permute-done((bf16[4,128,1024]{2,1,0:T(8,128)(2,1)S(1)}, bf16[4,128,1024]{2,1,0:T(8,128)(2,1)S(1)}, u32[]{:S(2)}, u32[]{:S(2)}) %collective-permute-start.137) | collective-permute-done | bytes 1048608 | tf_op jit(solution)/shard_map/ppermute | solution.py:50
  453.3 4.7 collective-permute-start.138
  458.6 15.8 %collective-permute-done.148 = bf16[4,128,1024]{2,1,0:T(8,128)(2,1)S(1)} collective-permute-done((bf16[4,128,1024]{2,1,0:T(8,128)(2,1)S(1)}, bf16[4,128,1024]{2,1,0:T(8,128)(2,1)S(1)}, u32[]{:S(2)}, u32[]{:S(2)}) %collective-permute-start.148) | collective-permute-done | bytes 1048608 | tf_op jit(solution)/shard_map/ppermute | solution.py:50
  474.9 4.8 collective-permute-start.149
  491.4 12.9 %collective-permute-done.150 = bf16[128,1024]{1,0:T(8,128)(2,1)S(1)} collective-permute-done((bf16[128,1024]{1,0:T(8,128)(2,1)S(1)}, bf16[128,1024]{1,0:T(8,128)(2,1)S(1)}, u32[]{:S(2)}, u32[]{:S(2)}) %collective-permute-start.150) | collective-permute-done | bytes 262176 | tf_op jit(solution)/shard_map/ppermute | solution.py:55
  506.4 16.5 %collective-permute-done.80.s2 = bf16[224,1024]{1,0:T(8,128)(2,1)} collective-permute-done((bf16[224,1024]{1,0:T(8,128)(2,1)S(1)}, bf16[224,1024]{1,0:T(8,128)(2,1)}, u32[]{:S(2)}, u32[]{:S(2)}) %collective-permute-start.80) | collective-permute-done | bytes 458784 | tf_op jit(solution)/shard_map/ppermute | solution.py:46
  527.5 5.6 collective-permute-done.142
  546.4 13.0 %shard_map.289 = (f32[448,1024]{1,0:T(8,128)S(1)}, bf16[448,1024]{1,0:T(8,128)(2,1)S(1)}, bf16[448,768]{1,0:T(8,128)(2,1)S(1)}, f32[448,1024]{1,0:T(8,128)S(1)},...) custom-call(bf16[448,1024]{1,0:T(8,128)(2,1)S(1)} %copy-done.67, ...), custom_call_target="tpu_custom_call" | custom-call | flops 1453326336 | bytes 15527936 | tf_op jit(solution)/shard_map/pallas_call | solution.py:73
  560.6 12.5 %shard_map.284 = (f32[448,1024]{1,0:T(8,128)S(1)}, bf16[448,1024]{1,0:T(8,128)(2,1)S(1)}, bf16[448,768]{1,0:T(8,128)(2,1)S(1)}, f32[448,1024]{1,0:T(8,128)S(1)},...) custom-call(bf16[448,1024]{1,0:T(8,128)(2,1)S(1)} %copy-done.65, ...), custom_call_target="tpu_custom_call" | custom-call | flops 1453326336 | bytes 15527936 | tf_op jit(solution)/shard_map/pallas_call | solution.py:73
  576.2 3.8 collective-permute-start.126
  595.0 11.4 %collective-permute-done.129 = bf16[64,1024]{1,0:T(8,128)(2,1)S(1)} collective-permute-done((bf16[64,1024]{1,0:T(8,128)(2,1)S(1)}, bf16[64,1024]{1,0:T(8,128)(2,1)S(1)}, u32[]{:S(2)}, u32[]{:S(2)}) %collective-permute-start.129) | collective-permute-done | bytes 131104 | tf_op jit(solution)/shard_map/ppermute | solution.py:50
  616.4 5.4 collective-permute-done.116
  623.0 7.2 collective-permute-done.117
  633.6 10.6 %collective-permute-done.83.s2 = bf16[224,1024]{1,0:T(8,128)(2,1)} collective-permute-done((bf16[224,1024]{1,0:T(8,128)(2,1)S(1)}, bf16[224,1024]{1,0:T(8,128)(2,1)}, u32[]{:S(2)}, u32[]{:S(2)}) %collective-permute-start.83) | collective-permute-done | bytes 458784 | tf_op jit(solution)/shard_map/ppermute | solution.py:46
  644.1 3.6 collective-permute-done.120
  651.7 3.6 copy.78
  655.3 3.4 stack_reshape.13
  666.3 10.2 %shard_map.290 = (f32[448,1024]{1,0:T(8,128)S(1)}, bf16[448,1024]{1,0:T(8,128)(2,1)S(1)}, bf16[448,1024]{1,0:T(8,128)(2,1)S(1)}, f32[448,1024]{1,0:T(8,128)S(1)}...) custom-call(f32[448,1024]{1,0:T(8,128)S(1)} %copy-done.13, f32[448,1024]{1,0:T(8,128)S(1)} %copy-done.87, ...), custom_call_target="tpu_custom_call" | custom-call | flops 1879048192 | bytes 19927040 | tf_op jit(solution)/shard_map/pallas_call | solution.py:73
  677.8 9.6 %shard_map.285 = (f32[448,1024]{1,0:T(8,128)S(1)}, bf16[448,1024]{1,0:T(8,128)(2,1)S(1)}, bf16[448,1024]{1,0:T(8,128)(2,1)S(1)}, f32[448,1024]{1,0:T(8,128)S(1)}...) custom-call(f32[448,1024]{1,0:T(8,128)S(1)} %copy-done.16, ...), custom_call_target="tpu_custom_call" | custom-call | flops 1879048192 | bytes 19927040 | tf_op jit(solution)/shard_map/pallas_call | solution.py:73
  694.2 4.5 convolution_convert_fusion.1
  708.0 38.4 %collective-permute-done.131 = bf16[4,128,1024]{2,1,0:T(8,128)(2,1)S(1)} collective-permute-done((bf16[4,128,1024]{2,1,0:T(8,128)(2,1)S(1)}, bf16[4,128,1024]{2,1,0:T(8,128)(2,1)S(1)}, u32[]{:S(2)}, u32[]{:S(2)}) %collective-permute-start.131) | collective-permute-done | bytes 1048608 | tf_op jit(solution)/shard_map/ppermute | solution.py:50
  752.6 8.3 collective-permute-done.132
  763.7 7.1 collective-permute-start.146
  770.8 10.7 %collective-permute-done.133 = bf16[128,1024]{1,0:T(8,128)(2,1)S(1)} collective-permute-done((bf16[128,1024]{1,0:T(8,128)(2,1)S(1)}, bf16[128,1024]{1,0:T(8,128)(2,1)S(1)}, u32[]{:S(2)}, u32[]{:S(2)}) %collective-permute-start.133) | collective-permute-done | bytes 262176 | tf_op jit(solution)/shard_map/ppermute | solution.py:55
  782.5 14.1 %collective-permute-done.145 = bf16[128,1024]{1,0:T(8,128)(2,1)S(1)} collective-permute-done((bf16[128,1024]{1,0:T(8,128)(2,1)S(1)}, bf16[128,1024]{1,0:T(8,128)(2,1)S(1)}, u32[]{:S(2)}, u32[]{:S(2)}) %collective-permute-start.145) | collective-permute-done | bytes 262176 | tf_op jit(solution)/shard_map/ppermute | solution.py:55
  799.6 6.3 collective-permute-done.147
  824.6 11.6 %shard_map.291 = (f32[448,1024]{1,0:T(8,128)S(1)}, bf16[448,1024]{1,0:T(8,128)(2,1)S(1)}, bf16[448,768]{1,0:T(8,128)(2,1)S(1)}, f32[448,1024]{1,0:T(8,128)S(1)},...) custom-call(f32[448,1024]{1,0:T(8,128)S(1)} %copy-done.97, f32[448,1024]{1,0:T(8,128)S(1)} %copy-done.22, ...), custom_call_target="tpu_custom_call" | custom-call | flops 1453326336 | bytes 16445440 | tf_op jit(solution)/shard_map/pallas_call | solution.py:73
  837.5 13.3 %shard_map.286 = (f32[448,1024]{1,0:T(8,128)S(1)}, bf16[448,1024]{1,0:T(8,128)(2,1)S(1)}, bf16[448,768]{1,0:T(8,128)(2,1)S(1)}, f32[448,1024]{1,0:T(8,128)S(1)},...) custom-call(f32[448,1024]{1,0:T(8,128)S(1)} %copy-done.95, f32[448,1024]{1,0:T(8,128)S(1)} %copy-done.19, ...), custom_call_target="tpu_custom_call" | custom-call | flops 1453326336 | bytes 16445440 | tf_op jit(solution)/shard_map/pallas_call | solution.py:73
  869.2 3.5 collective-permute-done.122
  874.6 11.9 %collective-permute-done.124 = bf16[64,1024]{1,0:T(8,128)(2,1)S(1)} collective-permute-done((bf16[64,1024]{1,0:T(8,128)(2,1)S(1)}, bf16[64,1024]{1,0:T(8,128)(2,1)S(1)}, u32[]{:S(2)}, u32[]{:S(2)}) %collective-permute-start.124) | collective-permute-done | bytes 131104 | tf_op jit(solution)/shard_map/ppermute | solution.py:50
  902.4 6.9 collective-permute-done.111
  910.0 4.8 collective-permute-done.89.s2
  917.8 5.4 shard_map.292
  924.5 5.3 shard_map.287
  (995 shorter events, 431.6 us)
Async XLA Ops:
  9.4 42.4 %collective-permute-start.1 = (bf16[224,1024]{1,0:T(8,128)(2,1)}, bf16[224,1024]{1,0:T(8,128)(2,1)}, u32[]{:S(2)}, u32[]{:S(2)}) collective-permute-start(bf16[224,1024]{1,0:T(8,128)(2,1)} %bitcast), channel_id=1, source_target_pairs={{0,1},{1,0},{2,3},{3,2},{4,5},{5,4},{6,7},{7,6},{8,9},{9,8},{10,11... | collective-permute-start | bytes 1376264 | tf_op jit(solution)/shard_map/ppermute | solution.py:46
  18.3 20.6 %collective-permute-start.13 = (bf16[64,1024]{1,0:T(8,128)(2,1)S(1)}, bf16[64,1024]{1,0:T(8,128)(2,1)S(1)}, u32[]{:S(2)}, u32[]{:S(2)}) collective-permute-start(bf16[64,1024]{1,0:T(8,128)(2,1)S(1)} %get-tuple-element.300.refs_0_), channel_id=1, source_target_pairs={{16,0},{20,4},{24,8},{28,12},{0,16},{4,20},{8,24},{12,28},{17,1},{... | collective-permute-start | bytes 393224 | tf_op jit(solution)/shard_map/ppermute | solution.py:55
  21.0 26.9 %collective-permute-start.6 = (bf16[144,768]{1,0:T(8,128)(2,1)S(1)}, bf16[144,768]{1,0:T(8,128)(2,1)S(1)}, u32[]{:S(2)}, u32[]{:S(2)}) collective-permute-start(bf16[144,768]{1,0:T(8,128)(2,1)S(1)} %maximum_maximum_fusion.refs_0_), channel_id=1, source_target_pairs={{24,0},{28,4},{0,8},{4,12},{8,16},{12,20},{16,24},{20,28},{25,1},{... | collective-permute-start | bytes 663560 | tf_op jit(solution)/shard_map/ppermute | solution.py:55
  21.1 27.3 %collective-permute-start.5 = (bf16[144,768]{1,0:T(8,128)(2,1)S(1)}, bf16[144,768]{1,0:T(8,128)(2,1)S(1)}, u32[]{:S(2)}, u32[]{:S(2)}) collective-permute-start(bf16[144,768]{1,0:T(8,128)(2,1)S(1)} %maximum_maximum_fusion.refs_0_), channel_id=1, source_target_pairs={{16,0},{20,4},{24,8},{28,12},{0,16},{4,20},{8,24},{12,28},{17,1},{... | collective-permute-start | bytes 663560 | tf_op jit(solution)/shard_map/ppermute | solution.py:55
  24.7 25.1 %collective-permute-start.4 = (bf16[144,768]{1,0:T(8,128)(2,1)S(1)}, bf16[144,768]{1,0:T(8,128)(2,1)S(1)}, u32[]{:S(2)}, u32[]{:S(2)}) collective-permute-start(bf16[144,768]{1,0:T(8,128)(2,1)S(1)} %maximum_maximum_fusion.refs_0_), channel_id=1, source_target_pairs={{8,0},{12,4},{16,8},{20,12},{24,16},{28,20},{0,24},{4,28},{9,1},{1... | collective-permute-start | bytes 663560 | tf_op jit(solution)/shard_map/ppermute | solution.py:55
  51.8 28.7 %collective-permute-start = (bf16[224,1024]{1,0:T(8,128)(2,1)}, bf16[224,1024]{1,0:T(8,128)(2,1)}, u32[]{:S(2)}, u32[]{:S(2)}) collective-permute-start(bf16[224,1024]{1,0:T(8,128)(2,1)} %bitcast), channel_id=1, source_target_pairs={{0,2},{2,0},{1,3},{3,1},{4,6},{6,4},{5,7},{7,5},{8,10},{10,8},{9,1... | collective-permute-start | bytes 1376264 | tf_op jit(solution)/shard_map/ppermute | solution.py:42
  54.6 24.0 %collective-permute-start.2 = (bf16[224,1024]{1,0:T(8,128)(2,1)}, bf16[224,1024]{1,0:T(8,128)(2,1)}, u32[]{:S(2)}, u32[]{:S(2)}) collective-permute-start(bf16[224,1024]{1,0:T(8,128)(2,1)} %collective-permute-done.1), channel_id=1, source_target_pairs={{0,2},{2,0},{1,3},{3,1},{4,6},{6,4},{5,7},{7,5},{8,10},{10,8},{9,1... | collective-permute-start | bytes 1376264 | tf_op jit(solution)/shard_map/ppermute | solution.py:42
  93.9 48.1 %collective-permute-start.65 = (bf16[448,1024]{1,0:T(8,128)(2,1)}, bf16[448,1024]{1,0:T(8,128)(2,1)}, u32[]{:S(2)}, u32[]{:S(2)}) collective-permute-start(bf16[448,1024]{1,0:T(8,128)(2,1)} %get-tuple-element.133), channel_id=1, source_target_pairs={{0,2},{2,0},{1,3},{3,1},{4,6},{6,4},{5,7},{7,5},{8,10},{10,8},{9,1... | collective-permute-start | bytes 2752520 | tf_op jit(solution)/shard_map/ppermute | solution.py:42
  103.4 19.6 %collective-permute-start.18 = (bf16[2,64,1024]{2,1,0:T(8,128)(2,1)}, bf16[2,64,1024]{2,1,0:T(8,128)(2,1)}, u32[]{:S(2)}, u32[]{:S(2)}) collective-permute-start(bf16[2,64,1024]{2,1,0:T(8,128)(2,1)} %reshape.377), channel_id=1, source_target_pairs={{0,2},{2,0},{1,3},{3,1},{4,6},{6,4},{5,7},{7,5},{8,10},{10,8},{9,1... | collective-permute-start | bytes 786440 | tf_op jit(solution)/shard_map/ppermute | solution.py:42
  115.7 49.2 %collective-permute-start.15 = (bf16[448,1024]{1,0:T(8,128)(2,1)}, bf16[448,1024]{1,0:T(8,128)(2,1)}, u32[]{:S(2)}, u32[]{:S(2)}) collective-permute-start(bf16[448,1024]{1,0:T(8,128)(2,1)} %get-tuple-element.120), channel_id=1, source_target_pairs={{0,2},{2,0},{1,3},{3,1},{4,6},{6,4},{5,7},{7,5},{8,10},{10,8},{9,1... | collective-permute-start | bytes 2752520 | tf_op jit(solution)/shard_map/ppermute | solution.py:42
  144.3 29.7 %collective-permute-start.66 = (bf16[224,1024]{1,0:T(8,128)(2,1)S(1)}, bf16[224,1024]{1,0:T(8,128)(2,1)}, u32[]{:S(2)}, u32[]{:S(2)}) collective-permute-start(bf16[224,1024]{1,0:T(8,128)(2,1)S(1)} %add_convert_fusion.10), channel_id=1, source_target_pairs={{0,1},{1,0},{2,3},{3,2},{4,5},{5,4},{6,7},{7,6},{8,9},{9,8},{10,11... | collective-permute-start | bytes 1376264 | tf_op jit(solution)/shard_map/ppermute | solution.py:46
  149.0 22.8 %collective-permute-start.22 = (bf16[128,1024]{1,0:T(8,128)(2,1)S(1)}, bf16[128,1024]{1,0:T(8,128)(2,1)S(1)}, u32[]{:S(2)}, u32[]{:S(2)}) collective-permute-start(bf16[128,1024]{1,0:T(8,128)(2,1)S(1)} %get-tuple-element.294.refs_0_), channel_id=1, source_target_pairs={{0,4},{4,0},{8,12},{12,8},{16,20},{20,16},{24,28},{28,24},{1,5},{5... | collective-permute-start | bytes 786440 | tf_op jit(solution)/shard_map/ppermute | solution.py:50
  154.6 19.4 %collective-permute-start.21 = (bf16[128,1024]{1,0:T(8,128)(2,1)S(1)}, bf16[128,1024]{1,0:T(8,128)(2,1)S(1)}, u32[]{:S(2)}, u32[]{:S(2)}) collective-permute-start(bf16[128,1024]{1,0:T(8,128)(2,1)S(1)} %get-tuple-element.294.refs_0_), channel_id=1, source_target_pairs={{24,0},{28,4},{0,8},{4,12},{8,16},{12,20},{16,24},{20,28},{25,1},{... | collective-permute-start | bytes 786440 | tf_op jit(solution)/shard_map/ppermute | solution.py:55
  174.1 28.2 %collective-permute-start.67 = (bf16[224,1024]{1,0:T(8,128)(2,1)}, bf16[224,1024]{1,0:T(8,128)(2,1)}, u32[]{:S(2)}, u32[]{:S(2)}) collective-permute-start(bf16[224,1024]{1,0:T(8,128)(2,1)} %collective-permute-done.66.s2), channel_id=1, source_target_pairs={{0,2},{2,0},{1,3},{3,1},{4,6},{6,4},{5,7},{7,5},{8,10},{10,8},{9,1... | collective-permute-start | bytes 1376264 | tf_op jit(solution)/shard_map/ppermute | solution.py:42
  186.5 26.4 %collective-permute-start.17 = (bf16[224,1024]{1,0:T(8,128)(2,1)}, bf16[224,1024]{1,0:T(8,128)(2,1)S(1)}, u32[]{:S(2)}, u32[]{:S(2)}) collective-permute-start(bf16[224,1024]{1,0:T(8,128)(2,1)} %collective-permute-done.16.s2), channel_id=1, source_target_pairs={{0,2},{2,0},{1,3},{3,1},{4,6},{6,4},{5,7},{7,5},{8,10},{10,8},{9,1... | collective-permute-start | bytes 1376264 | tf_op jit(solution)/shard_map/ppermute | solution.py:42
  230.4 19.5 %collective-permute-start.39 = (bf16[128,768]{1,0:T(8,128)(2,1)S(1)}, bf16[128,768]{1,0:T(8,128)(2,1)S(1)}, u32[]{:S(2)}, u32[]{:S(2)}) collective-permute-start(bf16[128,768]{1,0:T(8,128)(2,1)S(1)} %maximum_select_fusion.2.refs_0_), channel_id=1, source_target_pairs={{0,4},{4,0},{8,12},{12,8},{16,20},{20,16},{24,28},{28,24},{1,5},{5... | collective-permute-start | bytes 589832 | tf_op jit(solution)/shard_map/ppermute | solution.py:50
  242.0 37.3 %collective-permute-start.34 = (bf16[224,1024]{1,0:T(8,128)(2,1)S(1)}, bf16[224,1024]{1,0:T(8,128)(2,1)S(1)}, u32[]{:S(2)}, u32[]{:S(2)}) collective-permute-start(bf16[224,1024]{1,0:T(8,128)(2,1)S(1)} %add_convert_fusion.12), channel_id=1, source_target_pairs={{0,1},{1,0},{2,3},{3,2},{4,5},{5,4},{6,7},{7,6},{8,9},{9,8},{10,11... | collective-permute-start | bytes 1376264 | tf_op jit(solution)/shard_map/ppermute | solution.py:46
  242.5 36.8 %collective-permute-start.70 = (bf16[224,1024]{1,0:T(8,128)(2,1)}, bf16[224,1024]{1,0:T(8,128)(2,1)S(1)}, u32[]{:S(2)}, u32[]{:S(2)}) collective-permute-start(bf16[224,1024]{1,0:T(8,128)(2,1)} %collective-permute-done.69.refs_3_), channel_id=1, source_target_pairs={{0,2},{2,0},{1,3},{3,1},{4,6},{6,4},{5,7},{7,5},{8,10},{10,8},{9,1... | collective-permute-start | bytes 1376264 | tf_op jit(solution)/shard_map/ppermute | solution.py:42
  268.5 42.9 %collective-permute-start.59 = (bf16[128,1024]{1,0:T(8,128)(2,1)}, bf16[128,1024]{1,0:T(8,128)(2,1)S(1)}, u32[]{:S(2)}, u32[]{:S(2)}) collective-permute-start(bf16[128,1024]{1,0:T(8,128)(2,1)} %get-tuple-element.263.refs_0_), channel_id=1, source_target_pairs={{0,4},{4,0},{8,12},{12,8},{16,20},{20,16},{24,28},{28,24},{1,5},{5... | collective-permute-start | bytes 786440 | tf_op jit(solution)/shard_map/ppermute | solution.py:50
  271.6 40.5 %collective-permute-start.58 = (bf16[128,1024]{1,0:T(8,128)(2,1)}, bf16[128,1024]{1,0:T(8,128)(2,1)}, u32[]{:S(2)}, u32[]{:S(2)}) collective-permute-start(bf16[128,1024]{1,0:T(8,128)(2,1)} %get-tuple-element.263.refs_0_), channel_id=1, source_target_pairs={{24,0},{28,4},{0,8},{4,12},{8,16},{12,20},{16,24},{20,28},{25,1},{... | collective-permute-start | bytes 786440 | tf_op jit(solution)/shard_map/ppermute | solution.py:55
  275.8 37.0 %collective-permute-start.57 = (bf16[128,1024]{1,0:T(8,128)(2,1)}, bf16[128,1024]{1,0:T(8,128)(2,1)}, u32[]{:S(2)}, u32[]{:S(2)}) collective-permute-start(bf16[128,1024]{1,0:T(8,128)(2,1)} %get-tuple-element.263.refs_0_), channel_id=1, source_target_pairs={{16,0},{20,4},{24,8},{28,12},{0,16},{4,20},{8,24},{12,28},{17,1},{... | collective-permute-start | bytes 786440 | tf_op jit(solution)/shard_map/ppermute | solution.py:55
  292.2 37.0 %collective-permute-start.71 = (bf16[448,1024]{1,0:T(8,128)(2,1)}, bf16[448,1024]{1,0:T(8,128)(2,1)}, u32[]{:S(2)}, u32[]{:S(2)}) collective-permute-start(bf16[448,1024]{1,0:T(8,128)(2,1)} %get-tuple-element.140), channel_id=1, source_target_pairs={{0,2},{2,0},{1,3},{3,1},{4,6},{6,4},{5,7},{7,5},{8,10},{10,8},{9,1... | collective-permute-start | bytes 2752520 | tf_op jit(solution)/shard_map/ppermute | solution.py:42
  293.5 19.8 %collective-permute-start.56 = (bf16[128,1024]{1,0:T(8,128)(2,1)S(1)}, bf16[128,1024]{1,0:T(8,128)(2,1)S(1)}, u32[]{:S(2)}, u32[]{:S(2)}) collective-permute-start(bf16[128,1024]{1,0:T(8,128)(2,1)S(1)} %copy-done.98), channel_id=1, source_target_pairs={{8,0},{12,4},{16,8},{20,12},{24,16},{28,20},{0,24},{4,28},{9,1},{1... | collective-permute-start | bytes 786440 | tf_op jit(solution)/shard_map/ppermute | solution.py:55
  312.1 36.3 %collective-permute-start.46 = (bf16[448,1024]{1,0:T(8,128)(2,1)}, bf16[448,1024]{1,0:T(8,128)(2,1)}, u32[]{:S(2)}, u32[]{:S(2)}) collective-permute-start(bf16[448,1024]{1,0:T(8,128)(2,1)} %get-tuple-element.127), channel_id=1, source_target_pairs={{0,2},{2,0},{1,3},{3,1},{4,6},{6,4},{5,7},{7,5},{8,10},{10,8},{9,1... | collective-permute-start | bytes 2752520 | tf_op jit(solution)/shard_map/ppermute | solution.py:42
  327.1 19.8 %collective-permute-start.50 = (bf16[128,1024]{1,0:T(8,128)(2,1)}, bf16[128,1024]{1,0:T(8,128)(2,1)S(1)}, u32[]{:S(2)}, u32[]{:S(2)}) collective-permute-start(bf16[128,1024]{1,0:T(8,128)(2,1)} %get-tuple-element.293.refs_0_), channel_id=1, source_target_pairs={{16,0},{20,4},{24,8},{28,12},{0,16},{4,20},{8,24},{12,28},{17,1},{... | collective-permute-start | bytes 786440 | tf_op jit(solution)/shard_map/ppermute | solution.py:55
  341.1 43.5 %collective-permute-start.78 = (bf16[224,1024]{1,0:T(8,128)(2,1)}, bf16[224,1024]{1,0:T(8,128)(2,1)}, u32[]{:S(2)}, u32[]{:S(2)}) collective-permute-start(bf16[224,1024]{1,0:T(8,128)(2,1)} %collective-permute-done.77), channel_id=1, source_target_pairs={{0,2},{2,0},{1,3},{3,1},{4,6},{6,4},{5,7},{7,5},{8,10},{10,8},{9,1... | collective-permute-start | bytes 1376264 | tf_op jit(solution)/shard_map/ppermute | solution.py:42
  352.3 33.9 %collective-permute-start.76 = (bf16[224,1024]{1,0:T(8,128)(2,1)}, bf16[224,1024]{1,0:T(8,128)(2,1)}, u32[]{:S(2)}, u32[]{:S(2)}) collective-permute-start(bf16[224,1024]{1,0:T(8,128)(2,1)} %fusion.74), channel_id=1, source_target_pairs={{0,2},{2,0},{1,3},{3,1},{4,6},{6,4},{5,7},{7,5},{8,10},{10,8},{9,1... | collective-permute-start | bytes 1376264 | tf_op jit(solution)/shard_map/ppermute | solution.py:42
  353.0 22.0 %collective-permute-start.53 = (bf16[128,1024]{1,0:T(8,128)(2,1)}, bf16[128,1024]{1,0:T(8,128)(2,1)}, u32[]{:S(2)}, u32[]{:S(2)}) collective-permute-start(bf16[128,1024]{1,0:T(8,128)(2,1)} %collective-permute-done.49.refs_1_), channel_id=1, source_target_pairs={{0,4},{4,0},{8,12},{12,8},{16,20},{20,16},{24,28},{28,24},{1,5},{5... | collective-permute-start | bytes 786440 | tf_op jit(solution)/shard_map/ppermute | solution.py:50
  356.2 29.5 %collective-permute-start.47 = (bf16[224,1024]{1,0:T(8,128)(2,1)}, bf16[224,1024]{1,0:T(8,128)(2,1)}, u32[]{:S(2)}, u32[]{:S(2)}) collective-permute-start(bf16[224,1024]{1,0:T(8,128)(2,1)} %add_convert_fusion.11), channel_id=1, source_target_pairs={{0,1},{1,0},{2,3},{3,2},{4,5},{5,4},{6,7},{7,6},{8,9},{9,8},{10,11... | collective-permute-start | bytes 1376264 | tf_op jit(solution)/shard_map/ppermute | solution.py:46
  366.9 24.2 %collective-permute-start.73 = (bf16[224,1024]{1,0:T(8,128)(2,1)}, bf16[224,1024]{1,0:T(8,128)(2,1)}, u32[]{:S(2)}, u32[]{:S(2)}) collective-permute-start(bf16[224,1024]{1,0:T(8,128)(2,1)} %collective-permute-done.72.s2), channel_id=1, source_target_pairs={{0,2},{2,0},{1,3},{3,1},{4,6},{6,4},{5,7},{7,5},{8,10},{10,8},{9,1... | collective-permute-start | bytes 1376264 | tf_op jit(solution)/shard_map/ppermute | solution.py:42
  385.7 23.4 %collective-permute-start.48 = (bf16[224,1024]{1,0:T(8,128)(2,1)}, bf16[224,1024]{1,0:T(8,128)(2,1)}, u32[]{:S(2)}, u32[]{:S(2)}) collective-permute-start(bf16[224,1024]{1,0:T(8,128)(2,1)} %collective-permute-done.47.s2), channel_id=1, source_target_pairs={{0,2},{2,0},{1,3},{3,1},{4,6},{6,4},{5,7},{7,5},{8,10},{10,8},{9,1... | collective-permute-start | bytes 1376264 | tf_op jit(solution)/shard_map/ppermute | solution.py:42
  406.7 21.5 %collective-permute-start.91 = (bf16[448,1024]{1,0:T(8,128)(2,1)S(1)}, bf16[448,1024]{1,0:T(8,128)(2,1)S(1)}, u32[]{:S(2)}, u32[]{:S(2)}) collective-permute-start(bf16[448,1024]{1,0:T(8,128)(2,1)S(1)} %get-tuple-element.163), channel_id=1, source_target_pairs={{0,2},{2,0},{1,3},{3,1},{4,6},{6,4},{5,7},{7,5},{8,10},{10,8},{9,1... | collective-permute-start | bytes 2752520 | tf_op jit(solution)/shard_map/ppermute | solution.py:42
  408.5 21.0 %collective-permute-start.74 = (bf16[448,1024]{1,0:T(8,128)(2,1)S(1)}, bf16[448,1024]{1,0:T(8,128)(2,1)S(1)}, u32[]{:S(2)}, u32[]{:S(2)}) collective-permute-start(bf16[448,1024]{1,0:T(8,128)(2,1)S(1)} %get-tuple-element.144), channel_id=1, source_target_pairs={{0,2},{2,0},{1,3},{3,1},{4,6},{6,4},{5,7},{7,5},{8,10},{10,8},{9,1... | collective-permute-start | bytes 2752520 | tf_op jit(solution)/shard_map/ppermute | solution.py:42
  423.6 56.1 %collective-permute-start.79 = (bf16[448,1024]{1,0:T(8,128)(2,1)S(1)}, bf16[448,1024]{1,0:T(8,128)(2,1)S(1)}, u32[]{:S(2)}, u32[]{:S(2)}) collective-permute-start(bf16[448,1024]{1,0:T(8,128)(2,1)S(1)} %get-tuple-element.147), channel_id=1, source_target_pairs={{0,2},{2,0},{1,3},{3,1},{4,6},{6,4},{5,7},{7,5},{8,10},{10,8},{9,1... | collective-permute-start | bytes 2752520 | tf_op jit(solution)/shard_map/ppermute | solution.py:42
  426.7 26.1 %collective-permute-start.137 = (bf16[4,128,1024]{2,1,0:T(8,128)(2,1)S(1)}, bf16[4,128,1024]{2,1,0:T(8,128)(2,1)S(1)}, u32[]{:S(2)}, u32[]{:S(2)}) collective-permute-start(bf16[4,128,1024]{2,1,0:T(8,128)(2,1)S(1)} %dynamic-slice_bitcast_fusion.2), channel_id=1, source_target_pairs={{0,4},{4,0},{8,12},{12,8},{16,20},{20,16},{24,28},{28,24},{1,5},{5... | collective-permute-start | bytes 3145736 | tf_op jit(solution)/shard_map/ppermute | solution.py:50
  428.3 46.1 %collective-permute-start.148 = (bf16[4,128,1024]{2,1,0:T(8,128)(2,1)S(1)}, bf16[4,128,1024]{2,1,0:T(8,128)(2,1)S(1)}, u32[]{:S(2)}, u32[]{:S(2)}) collective-permute-start(bf16[4,128,1024]{2,1,0:T(8,128)(2,1)S(1)} %dynamic-slice_bitcast_fusion), channel_id=1, source_target_pairs={{0,4},{4,0},{8,12},{12,8},{16,20},{20,16},{24,28},{28,24},{1,5},{5... | collective-permute-start | bytes 3145736 | tf_op jit(solution)/shard_map/ppermute | solution.py:50
  453.3 26.6 %collective-permute-start.138 = (bf16[128,1024]{1,0:T(8,128)(2,1)S(1)}, bf16[128,1024]{1,0:T(8,128)(2,1)S(1)}, u32[]{:S(2)}, u32[]{:S(2)}) collective-permute-start(bf16[128,1024]{1,0:T(8,128)(2,1)S(1)} %get-tuple-element.260), channel_id=1, source_target_pairs={{8,0},{12,4},{16,8},{20,12},{24,16},{28,20},{0,24},{4,28},{9,1},{1... | collective-permute-start | bytes 786440 | tf_op jit(solution)/shard_map/ppermute | solution.py:55
  457.9 23.5 %collective-permute-start.140 = (bf16[128,1024]{1,0:T(8,128)(2,1)S(1)}, bf16[128,1024]{1,0:T(8,128)(2,1)S(1)}, u32[]{:S(2)}, u32[]{:S(2)}) collective-permute-start(bf16[128,1024]{1,0:T(8,128)(2,1)S(1)} %get-tuple-element.261), channel_id=1, source_target_pairs={{24,0},{28,4},{0,8},{4,12},{8,16},{12,20},{16,24},{20,28},{25,1},{... | collective-permute-start | bytes 786440 | tf_op jit(solution)/shard_map/ppermute | solution.py:55
  457.9 24.0 %collective-permute-start.139 = (bf16[128,1024]{1,0:T(8,128)(2,1)S(1)}, bf16[128,1024]{1,0:T(8,128)(2,1)S(1)}, u32[]{:S(2)}, u32[]{:S(2)}) collective-permute-start(bf16[128,1024]{1,0:T(8,128)(2,1)S(1)} %get-tuple-element.262), channel_id=1, source_target_pairs={{16,0},{20,4},{24,8},{28,12},{0,16},{4,20},{8,24},{12,28},{17,1},{... | collective-permute-start | bytes 786440 | tf_op jit(solution)/shard_map/ppermute | solution.py:55
  479.8 24.7 %collective-permute-start.92 = (bf16[224,1024]{1,0:T(8,128)(2,1)S(1)}, bf16[224,1024]{1,0:T(8,128)(2,1)}, u32[]{:S(2)}, u32[]{:S(2)}) collective-permute-start(bf16[224,1024]{1,0:T(8,128)(2,1)S(1)} %add_convert_fusion.3), channel_id=1, source_target_pairs={{0,1},{1,0},{2,3},{3,2},{4,5},{5,4},{6,7},{7,6},{8,9},{9,8},{10,11... | collective-permute-start | bytes 1376264 | tf_op jit(solution)/shard_map/ppermute | solution.py:46
  481.4 24.7 %collective-permute-start.75 = (bf16[224,1024]{1,0:T(8,128)(2,1)S(1)}, bf16[224,1024]{1,0:T(8,128)(2,1)S(1)}, u32[]{:S(2)}, u32[]{:S(2)}) collective-permute-start(bf16[224,1024]{1,0:T(8,128)(2,1)S(1)} %fusion.65), channel_id=1, source_target_pairs={{0,1},{1,0},{2,3},{3,2},{4,5},{5,4},{6,7},{7,6},{8,9},{9,8},{10,11... | collective-permute-start | bytes 1376264 | tf_op jit(solution)/shard_map/ppermute | solution.py:46
  481.9 41.0 %collective-permute-start.64 = (bf16[224,1024]{1,0:T(8,128)(2,1)S(1)}, bf16[224,1024]{1,0:T(8,128)(2,1)S(1)}, u32[]{:S(2)}, u32[]{:S(2)}) collective-permute-start(bf16[224,1024]{1,0:T(8,128)(2,1)S(1)} %fusion.64), channel_id=1, source_target_pairs={{0,1},{1,0},{2,3},{3,2},{4,5},{5,4},{6,7},{7,6},{8,9},{9,8},{10,11... | collective-permute-start | bytes 1376264 | tf_op jit(solution)/shard_map/ppermute | solution.py:46
  486.4 36.5 %collective-permute-start.80 = (bf16[224,1024]{1,0:T(8,128)(2,1)S(1)}, bf16[224,1024]{1,0:T(8,128)(2,1)}, u32[]{:S(2)}, u32[]{:S(2)}) collective-permute-start(bf16[224,1024]{1,0:T(8,128)(2,1)S(1)} %add_convert_fusion.7), channel_id=1, source_target_pairs={{0,1},{1,0},{2,3},{3,2},{4,5},{5,4},{6,7},{7,6},{8,9},{9,8},{10,11... | collective-permute-start | bytes 1376264 | tf_op jit(solution)/shard_map/ppermute | solution.py:46
  504.4 19.9 %collective-permute-start.141 = (bf16[64,1024]{1,0:T(8,128)(2,1)S(1)}, bf16[64,1024]{1,0:T(8,128)(2,1)S(1)}, u32[]{:S(2)}, u32[]{:S(2)}) collective-permute-start(bf16[64,1024]{1,0:T(8,128)(2,1)S(1)} %fusion.105), channel_id=1, source_target_pairs={{0,2},{2,0},{1,3},{3,1},{4,6},{6,4},{5,7},{7,5},{8,10},{10,8},{9,1... | collective-permute-start | bytes 393224 | tf_op jit(solution)/shard_map/ppermute | solution.py:42
  504.6 21.8 %collective-permute-start.152 = (bf16[128,1024]{1,0:T(8,128)(2,1)S(1)}, bf16[128,1024]{1,0:T(8,128)(2,1)S(1)}, u32[]{:S(2)}, u32[]{:S(2)}) collective-permute-start(bf16[128,1024]{1,0:T(8,128)(2,1)S(1)} %get-tuple-element.237), channel_id=1, source_target_pairs={{0,1},{1,0},{2,3},{3,2},{4,5},{5,4},{6,7},{7,6},{8,9},{9,8},{10,11... | collective-permute-start | bytes 786440 | tf_op jit(solution)/shard_map/ppermute | solution.py:46
  506.2 32.3 %collective-permute-start.93 = (bf16[224,1024]{1,0:T(8,128)(2,1)}, bf16[224,1024]{1,0:T(8,128)(2,1)}, u32[]{:S(2)}, u32[]{:S(2)}) collective-permute-start(bf16[224,1024]{1,0:T(8,128)(2,1)} %collective-permute-done.92.s2), channel_id=1, source_target_pairs={{0,2},{2,0},{1,3},{3,1},{4,6},{6,4},{5,7},{7,5},{8,10},{10,8},{9,1... | collective-permute-start | bytes 1376264 | tf_op jit(solution)/shard_map/ppermute | solution.py:42
  522.9 37.7 %collective-permute-start.81 = (bf16[224,1024]{1,0:T(8,128)(2,1)}, bf16[224,1024]{1,0:T(8,128)(2,1)}, u32[]{:S(2)}, u32[]{:S(2)}) collective-permute-start(bf16[224,1024]{1,0:T(8,128)(2,1)} %collective-permute-done.80.s2), channel_id=1, source_target_pairs={{0,2},{2,0},{1,3},{3,1},{4,6},{6,4},{5,7},{7,5},{8,10},{10,8},{9,1... | collective-permute-start | bytes 1376264 | tf_op jit(solution)/shard_map/ppermute | solution.py:42
  560.5 53.3 %collective-permute-start.94 = (bf16[448,1024]{1,0:T(8,128)(2,1)}, bf16[448,1024]{1,0:T(8,128)(2,1)}, u32[]{:S(2)}, u32[]{:S(2)}) collective-permute-start(bf16[448,1024]{1,0:T(8,128)(2,1)} %get-tuple-element.167), channel_id=1, source_target_pairs={{0,2},{2,0},{1,3},{3,1},{4,6},{6,4},{5,7},{7,5},{8,10},{10,8},{9,1... | collective-permute-start | bytes 2752520 | tf_op jit(solution)/shard_map/ppermute | solution.py:42
  584.7 23.4 %collective-permute-start.115 = (bf16[4,128,768]{2,1,0:T(8,128)(2,1)}, bf16[4,128,768]{2,1,0:T(8,128)(2,1)}, u32[]{:S(2)}, u32[]{:S(2)}) collective-permute-start(bf16[4,128,768]{2,1,0:T(8,128)(2,1)} %dynamic-slice_bitcast_fusion.4), channel_id=1, source_target_pairs={{0,4},{4,0},{8,12},{12,8},{16,20},{20,16},{24,28},{28,24},{1,5},{5... | collective-permute-start | bytes 2359304 | tf_op jit(solution)/shard_map/ppermute | solution.py:50
  586.4 44.1 %collective-permute-start.82 = (bf16[448,1024]{1,0:T(8,128)(2,1)}, bf16[448,1024]{1,0:T(8,128)(2,1)S(1)}, u32[]{:S(2)}, u32[]{:S(2)}) collective-permute-start(bf16[448,1024]{1,0:T(8,128)(2,1)} %copy-done.179), channel_id=1, source_target_pairs={{0,2},{2,0},{1,3},{3,1},{4,6},{6,4},{5,7},{7,5},{8,10},{10,8},{9,1... | collective-permute-start | bytes 2752520 | tf_op jit(solution)/shard_map/ppermute | solution.py:42
  606.5 26.3 %collective-permute-start.130 = (bf16[64,1024]{1,0:T(8,128)(2,1)S(1)}, bf16[64,1024]{1,0:T(8,128)(2,1)S(1)}, u32[]{:S(2)}, u32[]{:S(2)}) collective-permute-start(bf16[64,1024]{1,0:T(8,128)(2,1)S(1)} %fusion.103), channel_id=1, source_target_pairs={{0,1},{1,0},{2,3},{3,2},{4,5},{5,4},{6,7},{7,6},{8,9},{9,8},{10,11... | collective-permute-start | bytes 393224 | tf_op jit(solution)/shard_map/ppermute | solution.py:46
  632.8 25.9 %collective-permute-start.96 = (bf16[224,1024]{1,0:T(8,128)(2,1)S(1)}, bf16[224,1024]{1,0:T(8,128)(2,1)}, u32[]{:S(2)}, u32[]{:S(2)}) collective-permute-start(bf16[224,1024]{1,0:T(8,128)(2,1)S(1)} %collective-permute-done.95.s2), channel_id=1, source_target_pairs={{0,2},{2,0},{1,3},{3,1},{4,6},{6,4},{5,7},{7,5},{8,10},{10,8},{9,1... | collective-permute-start | bytes 1376264 | tf_op jit(solution)/shard_map/ppermute | solution.py:42
  644.1 33.6 %collective-permute-start.84 = (bf16[224,1024]{1,0:T(8,128)(2,1)}, bf16[224,1024]{1,0:T(8,128)(2,1)}, u32[]{:S(2)}, u32[]{:S(2)}) collective-permute-start(bf16[224,1024]{1,0:T(8,128)(2,1)} %collective-permute-done.83.s2), channel_id=1, source_target_pairs={{0,2},{2,0},{1,3},{3,1},{4,6},{6,4},{5,7},{7,5},{8,10},{10,8},{9,1... | collective-permute-start | bytes 1376264 | tf_op jit(solution)/shard_map/ppermute | solution.py:42
  698.8 51.9 %collective-permute-start.143 = (bf16[4,128,1024]{2,1,0:T(8,128)(2,1)S(1)}, bf16[4,128,1024]{2,1,0:T(8,128)(2,1)S(1)}, u32[]{:S(2)}, u32[]{:S(2)}) collective-permute-start(bf16[4,128,1024]{2,1,0:T(8,128)(2,1)S(1)} %dynamic-slice_bitcast_fusion.1), channel_id=1, source_target_pairs={{0,4},{4,0},{8,12},{12,8},{16,20},{20,16},{24,28},{28,24},{1,5},{5... | collective-permute-start | bytes 3145736 | tf_op jit(solution)/shard_map/ppermute | solution.py:50
  702.9 43.5 %collective-permute-start.131 = (bf16[4,128,1024]{2,1,0:T(8,128)(2,1)S(1)}, bf16[4,128,1024]{2,1,0:T(8,128)(2,1)S(1)}, u32[]{:S(2)}, u32[]{:S(2)}) collective-permute-start(bf16[4,128,1024]{2,1,0:T(8,128)(2,1)S(1)} %dynamic-slice_bitcast_fusion.3), channel_id=1, source_target_pairs={{0,4},{4,0},{8,12},{12,8},{16,20},{20,16},{24,28},{28,24},{1,5},{5... | collective-permute-start | bytes 3145736 | tf_op jit(solution)/shard_map/ppermute | solution.py:50
  705.7 91.8 %collective-permute-start.98 = (bf16[224,1024]{1,0:T(8,128)(2,1)S(1)}, bf16[224,1024]{1,0:T(8,128)(2,1)S(1)}, u32[]{:S(2)}, u32[]{:S(2)}) collective-permute-start(bf16[224,1024]{1,0:T(8,128)(2,1)S(1)} %add_convert_fusion.1), channel_id=1, source_target_pairs={{0,1},{1,0},{2,3},{3,2},{4,5},{5,4},{6,7},{7,6},{8,9},{9,8},{10,11... | collective-permute-start | bytes 1376264 | tf_op jit(solution)/shard_map/ppermute | solution.py:46
  706.5 91.0 %collective-permute-start.86 = (bf16[224,1024]{1,0:T(8,128)(2,1)S(1)}, bf16[224,1024]{1,0:T(8,128)(2,1)}, u32[]{:S(2)}, u32[]{:S(2)}) collective-permute-start(bf16[224,1024]{1,0:T(8,128)(2,1)S(1)} %add_convert_fusion.5), channel_id=1, source_target_pairs={{0,1},{1,0},{2,3},{3,2},{4,5},{5,4},{6,7},{7,6},{8,9},{9,8},{10,11... | collective-permute-start | bytes 1376264 | tf_op jit(solution)/shard_map/ppermute | solution.py:46
  750.7 30.9 %collective-permute-start.133 = (bf16[128,1024]{1,0:T(8,128)(2,1)S(1)}, bf16[128,1024]{1,0:T(8,128)(2,1)S(1)}, u32[]{:S(2)}, u32[]{:S(2)}) collective-permute-start(bf16[128,1024]{1,0:T(8,128)(2,1)S(1)} %get-tuple-element.259), channel_id=1, source_target_pairs={{16,0},{20,4},{24,8},{28,12},{0,16},{4,20},{8,24},{12,28},{17,1},{... | collective-permute-start | bytes 786440 | tf_op jit(solution)/shard_map/ppermute | solution.py:55
  761.0 21.6 %collective-permute-start.144 = (bf16[128,1024]{1,0:T(8,128)(2,1)S(1)}, bf16[128,1024]{1,0:T(8,128)(2,1)S(1)}, u32[]{:S(2)}, u32[]{:S(2)}) collective-permute-start(bf16[128,1024]{1,0:T(8,128)(2,1)S(1)} %get-tuple-element.251), channel_id=1, source_target_pairs={{8,0},{12,4},{16,8},{20,12},{24,16},{28,20},{0,24},{4,28},{9,1},{1... | collective-permute-start | bytes 786440 | tf_op jit(solution)/shard_map/ppermute | solution.py:55
  797.5 20.1 %collective-permute-start.99 = (bf16[224,1024]{1,0:T(8,128)(2,1)S(1)}, bf16[224,1024]{1,0:T(8,128)(2,1)S(1)}, u32[]{:S(2)}, u32[]{:S(2)}) collective-permute-start(bf16[224,1024]{1,0:T(8,128)(2,1)S(1)} %collective-permute-done.98.s2), channel_id=1, source_target_pairs={{0,2},{2,0},{1,3},{3,1},{4,6},{6,4},{5,7},{7,5},{8,10},{10,8},{9,1... | collective-permute-start | bytes 1376264 | tf_op jit(solution)/shard_map/ppermute | solution.py:42
  797.5 39.9 %collective-permute-start.87 = (bf16[224,1024]{1,0:T(8,128)(2,1)}, bf16[224,1024]{1,0:T(8,128)(2,1)}, u32[]{:S(2)}, u32[]{:S(2)}) collective-permute-start(bf16[224,1024]{1,0:T(8,128)(2,1)} %collective-permute-done.86.s2), channel_id=1, source_target_pairs={{0,2},{2,0},{1,3},{3,1},{4,6},{6,4},{5,7},{7,5},{8,10},{10,8},{9,1... | collective-permute-start | bytes 1376264 | tf_op jit(solution)/shard_map/ppermute | solution.py:42
  837.4 55.0 %collective-permute-start.100 = (bf16[448,1024]{1,0:T(8,128)(2,1)}, bf16[448,1024]{1,0:T(8,128)(2,1)}, u32[]{:S(2)}, u32[]{:S(2)}) collective-permute-start(bf16[448,1024]{1,0:T(8,128)(2,1)} %get-tuple-element.175), channel_id=1, source_target_pairs={{0,2},{2,0},{1,3},{3,1},{4,6},{6,4},{5,7},{7,5},{8,10},{10,8},{9,1... | collective-permute-start | bytes 2752520 | tf_op jit(solution)/shard_map/ppermute | solution.py:42
  864.5 22.6 %collective-permute-start.109 = (bf16[4,128,768]{2,1,0:T(8,128)(2,1)}, bf16[4,128,768]{2,1,0:T(8,128)(2,1)}, u32[]{:S(2)}, u32[]{:S(2)}) collective-permute-start(bf16[4,128,768]{2,1,0:T(8,128)(2,1)} %dynamic-slice_bitcast_fusion.5), channel_id=1, source_target_pairs={{0,4},{4,0},{8,12},{12,8},{16,20},{20,16},{24,28},{28,24},{1,5},{5... | collective-permute-start | bytes 2359304 | tf_op jit(solution)/shard_map/ppermute | solution.py:50
  866.8 28.1 %collective-permute-start.88 = (bf16[448,1024]{1,0:T(8,128)(2,1)}, bf16[448,1024]{1,0:T(8,128)(2,1)}, u32[]{:S(2)}, u32[]{:S(2)}) collective-permute-start(bf16[448,1024]{1,0:T(8,128)(2,1)} %get-tuple-element.159), channel_id=1, source_target_pairs={{0,2},{2,0},{1,3},{3,1},{4,6},{6,4},{5,7},{7,5},{8,10},{10,8},{9,1... | collective-permute-start | bytes 2752520 | tf_op jit(solution)/shard_map/ppermute | solution.py:42
  (328 other events, 3469.3 us)

commit v2 on v1

v2 whole, which is shorter than its diff:
```python
import functools

import jax
import jax.numpy as jnp
from jax import lax
from jax.experimental import pallas as pl
from jax.experimental.pallas import tpu as pltpu
from jax.sharding import PartitionSpec as P


HEADS = 16
LAYERS = 2
norm_eps = 1e-06
bf16 = jnp.bfloat16
f32 = jnp.float32


def widen(array):
    return array.astype(f32)


def dot(a, b, dims):
    return lax.dot_general(a, b, (dims, ((), ())), preferred_element_type=f32)


def mm(a, b):
    return dot(a, b, ((1,), (0,)))


def mm_t(a, b):
    return dot(a, b, ((1,), (1,)))


def t_mm(a, b):
    return dot(a, b, ((0,), (0,)))


PAIR = [(0, 1), (1, 0)]


def core_swap(v):
    return lax.ppermute(v, "seq", PAIR)


def y_swap(v):
    return lax.ppermute(v, "replica", PAIR)


def x_swap(v, n):
    return lax.ppermute(v, "fsdp", [(f, f ^ 1) for f in range(n)])


def z_from(v, k, n):
    nz = n // 2
    return lax.ppermute(
        v, "fsdp", [(((z + k) % nz) * 2 + x, z * 2 + x) for z in range(nz) for x in range(2)]
    )


def pick(array, axis, at):
    return lax.dynamic_index_in_dim(array, at, axis, keepdims=False)


TILE = 32
COLS = 256
VMEM_LIMIT = 20 * 1024 * 1024
HBM = pltpu.MemorySpace.HBM


def call(body, outs, args, flops, transcendentals=0, scratch=(), smem=0):
    shapes = tuple(jax.ShapeDtypeStruct(o[0], o[1]) for o in outs)
    far = [i for i, o in enumerate(outs) if len(o) > 2 and o[2]]
    n_in, n_out, n_far = len(args), len(outs), len(far)

    def run(*refs):
        out_refs = list(refs[n_in : n_in + n_out])
        rest = refs[n_in + n_out :]
        sems = rest[-1] if far else None
        copies = {}
        for j, i in enumerate(far):
            copies[i] = pltpu.make_async_copy(rest[j], out_refs[i], sems.at[j])
            out_refs[i] = rest[j]
        extra = rest[n_far:-1] if far else rest[n_far:]
        body(lambda i: copies[i].start(), *refs[:n_in], *out_refs, *extra)
        for copy in copies.values():
            copy.wait()

    touched = sum(a.size * a.dtype.itemsize for a in (*args, *shapes))
    scratch = [pltpu.VMEM(*outs[i][:2]) for i in far] + list(scratch)
    if far:
        scratch.append(pltpu.SemaphoreType.DMA((n_far,)))
    spaces = [pltpu.SMEM if i < smem else pltpu.VMEM for i in range(n_in)]
    return pl.pallas_call(
        run,
        out_shape=shapes,
        in_specs=[pl.BlockSpec(memory_space=s) for s in spaces],
        out_specs=tuple(
            pl.BlockSpec(memory_space=HBM if i in far else pltpu.VMEM) for i in range(n_out)
        ),
        scratch_shapes=scratch,
        compiler_params=pltpu.CompilerParams(vmem_limit_bytes=VMEM_LIMIT),
        cost_estimate=pl.CostEstimate(
            flops=flops, bytes_accessed=touched, transcendentals=transcendentals
        ),
    )(*args)


def norm_parts(inputs):
    center = inputs - jnp.mean(inputs, axis=-1, keepdims=True)
    spread = jnp.mean(center * center, axis=-1, keepdims=True)
    scale = lax.rsqrt(spread + norm_eps)
    return center * scale, scale


def norm_grad(e, inputs, gain):
    unit, scale = norm_parts(inputs)
    eg = e * gain
    d = scale * (
        eg
        - jnp.mean(eg, axis=-1, keepdims=True)
        - unit * jnp.mean(eg * unit, axis=-1, keepdims=True)
    )
    return d, e * unit


def eight(v):
    return jnp.sum(v.reshape(v.shape[0] // 8, 8, v.shape[1]), axis=0)


def one(v):
    return jnp.sum(v, axis=0, keepdims=True)


def by_rows(half_rows, step):
    for half in range(2):

        @pl.loop(0, half_rows // TILE)
        def _(i):
            start = pl.multiple_of(i * TILE, TILE)
            step(pl.ds(half * half_rows + start, TILE), half, pl.ds(start, TILE))


def by_cols(width, step):
    @pl.loop(0, width // COLS)
    def _(i):
        step(pl.ds(pl.multiple_of(i * COLS, COLS), COLS))


def summed(sent, whole, half, part):
    rows = sent[1].shape[0] // 2
    side = pl.ds((1 - half) * rows + part.start, TILE)
    total = widen(sent[0][whole, :]) + widen(sent[1][side, :])
    return total + widen(sent[2 + half][part, :])


def put(ref, cols, value):
    ref[:, cols] = value.astype(ref.dtype)


def heads_of(ref, width, size, h):
    return [ref[:, i * width + h * size : i * width + (h + 1) * size] for i in range(3)]


GAIN_ONE, SHIFT_ONE, QUERY_B, VALUE_B, PROJ_B, GAIN_TWO, SHIFT_TWO, DOWN_B = range(8)


def row(vec, which, layer):
    at = 2 * which + layer
    return vec[at : at + 1, :]


def attend_body(layer, heads, size, flush, *refs):
    if layer == 0:
        base, vec, w_qkv, fix, w_proj, normed, qkv, attended, stat, low = refs
        sent, shift = None, 0
    else:
        base, s0, s1, s2, s3, vec, w_qkv, fix, w_proj = refs[:9]
        resid, normed, qkv, attended, stat, low = refs[9:]
        sent, shift = (s0, s1, s2, s3), 1
    width = heads * size

    def norm(whole, half, part_rows):
        value = widen(base[whole, :])
        if sent is not None:
            value = value + (summed(sent, whole, half, part_rows) + row(vec, DOWN_B, layer - 1))
            resid[whole, :] = value
        unit, _ = norm_parts(value)
        normed[whole, :] = (
            unit * row(vec, GAIN_ONE, layer) + row(vec, SHIFT_ONE, layer)
        ).astype(bf16)

    by_rows(base.shape[0] // 2, norm)
    for i in range(shift + 1):
        flush(i)

    def project(cols):
        value = mm(normed[...], w_qkv[:, cols]) + fix[2 * layer : 2 * layer + 1, cols]
        qkv[:, cols] = (value * fix[2 * layer + 1 : 2 * layer + 2, cols]).astype(bf16)

    by_cols(3 * width, project)
    flush(shift + 1)
    for h in range(heads):
        q, k, v = heads_of(qkv, width, size, h)
        s = mm_t(q, k)
        peak = jnp.max(s, axis=-1, keepdims=True)
        e = jnp.exp(s - peak)
        total = jnp.sum(e, axis=-1, keepdims=True)
        value = mm(e.astype(bf16), v) * (1.0 / total)
        attended[:, h * size : (h + 1) * size] = value.astype(bf16)
        stat[:, h : h + 1] = peak + jnp.log(total)
    flush(shift + 2)
    flush(shift + 3)
    by_cols(low.shape[1], lambda cols: put(low, cols, mm(attended[...], w_proj[:, cols])))


def attend(base, sent, vec, w_qkv, fix, w_proj, layer, heads, size):
    toks, width = base.shape
    outs = [((toks, width), bf16, True), ((toks, 3 * heads * size), bf16, True)]
    outs = outs + [((toks, heads * size), bf16, True), ((toks, 128), f32, True)]
    outs = outs + [((toks, width), bf16)]
    if layer:
        outs = [((toks, width), f32, True)] + outs
    args = [base, *(sent or ()), vec, w_qkv, fix, w_proj]
    flops = 8 * toks * width * heads * size + 4 * heads * toks * toks * size
    body = functools.partial(attend_body, layer, heads, size)
    got = call(body, outs, args, flops, heads * toks * toks)
    return got if layer else (base, *got)


ROOT_HALF = 0.7071067811865476
ROOT_TWO_PI_INV = 0.3989422804014327


def up_body(layer, flush, base, s0, s1, s2, s3, vec, w_up, up_b, mid, normed, active, slope):
    def norm(whole, half, part_rows):
        value = widen(base[whole, :])
        value = value + (
            summed((s0, s1, s2, s3), whole, half, part_rows) + row(vec, PROJ_B, layer)
        )
        mid[whole, :] = value
        unit, _ = norm_parts(value)
        normed[whole, :] = (
            unit * row(vec, GAIN_TWO, layer) + row(vec, SHIFT_TWO, layer)
        ).astype(bf16)

    by_rows(base.shape[0] // 2, norm)
    flush(0)
    flush(1)

    def up(cols):
        pre = mm(normed[...], w_up[:, cols]) + up_b[layer : layer + 1, cols]
        half = 0.5 * (1.0 + lax.erf(pre * ROOT_HALF))
        put(active, cols, pre * half)
        put(slope, cols, half + pre * (ROOT_TWO_PI_INV * jnp.exp(-0.5 * pre * pre)))

    by_cols(w_up.shape[1], up)
    flush(2)
    flush(3)


def go_up(base, sent, vec, w_up, up_b, layer):
    toks, width = base.shape
    hid = w_up.shape[1]
    outs = [((toks, width), f32, True), ((toks, width), bf16, True)]
    outs = outs + [((toks, hid), bf16, True), ((toks, hid), bf16, True)]
    args = [base, *sent, vec, w_up, up_b]
    body = functools.partial(up_body, layer)
    return call(body, outs, args, 2 * toks * width * hid, toks * hid)


def down_body(flush, active, w_down, low):
    by_cols(low.shape[1], lambda cols: put(low, cols, mm(active[...], w_down[:, cols])))


def go_down(active, w_down):
    outs = [((active.shape[0], w_down.shape[1]), bf16)]
    flops = 2 * active.size * w_down.shape[1]
    return call(down_body, outs, [active, w_down], flops)[0]


def mlp_back_tail(flush, at, d_mlp, slope, w_down, w_up, d_pre, low, up_sum):
    def back(cols):
        value = (mm_t(d_mlp[...], w_down[cols, :]) * widen(slope[:, cols])).astype(bf16)
        d_pre[:, cols] = value
        up_sum[:, cols] = eight(widen(value))

    by_cols(w_down.shape[0], back)
    flush(at)
    by_cols(low.shape[1], lambda cols: put(low, cols, mm_t(d_pre[...], w_up[cols, :])))


def mlp_back_first(flush, d_mlp, slope, w_down, w_up, d_pre, low, up_sum, sums):
    sums[...] = jnp.zeros_like(sums)

    def count(whole, half, part_rows):
        sums[16:24, :] += eight(widen(d_mlp[whole, :]))

    by_rows(d_mlp.shape[0] // 2, count)
    mlp_back_tail(flush, 0, d_mlp, slope, w_down, w_up, d_pre, low, up_sum)


def mlp_back_body(layer, flush, base, d_mid, s0, s1, s2, s3, vec, slope, w_down, w_up, *outs):
    grad, d_mlp, d_pre, low, up_sum, sums = outs
    sums[...] = jnp.zeros_like(sums)

    def norm(whole, half, part_rows):
        e = summed((s0, s1, s2, s3), whole, half, part_rows)
        d, by_gain = norm_grad(e, widen(base[whole, :]), row(vec, GAIN_ONE, layer + 1))
        value = d_mid[whole, :] + d
        grad[whole, :] = value
        low_value = value.astype(bf16)
        d_mlp[whole, :] = low_value
        sums[0:8, :] += eight(by_gain)
        sums[8:16, :] += eight(e)
        sums[16:24, :] += eight(widen(low_value))

    by_rows(base.shape[0] // 2, norm)
    flush(0)
    flush(1)
    mlp_back_tail(flush, 2, d_mlp, slope, w_down, w_up, d_pre, low, up_sum)


def mlp_back(first, base, d_mid, sent, vec, slope, w_down, w_up, layer):
    toks, hid = slope.shape
    width = w_up.shape[0]
    outs = [((toks, hid), bf16, True), ((toks, width), bf16), ((8, hid), f32), ((24, width), f32)]
    flops = 4 * toks * hid * width
    if first is not None:
        return call(mlp_back_first, outs, [first, slope, w_down, w_up], flops)
    outs = [((toks, width), f32, True), ((toks, width), bf16, True), *outs]
    args = [base, d_mid, *sent, vec, slope, w_down, w_up]
    return call(functools.partial(mlp_back_body, layer), outs, args, flops)


def attend_back_body(layer, heads, size, flush, *refs):
    grad, mid, s0, s1, s2, s3, vec, qkv, stat, w_proj, w_qkv = refs[:11]
    d_mid, d_branch, d_joined, low, sums, joined_sum, d_att = refs[11:]
    width = heads * size
    sums[...] = jnp.zeros_like(sums)

    def norm(whole, half, part_rows):
        e = summed((s0, s1, s2, s3), whole, half, part_rows)
        d, by_gain = norm_grad(e, mid[whole, :], row(vec, GAIN_TWO, layer))
        value = widen(grad[whole, :]) + d
        d_mid[whole, :] = value
        low_value = value.astype(bf16)
        d_branch[whole, :] = low_value
        sums[0:8, :] += eight(by_gain)
        sums[8:16, :] += eight(e)
        sums[16:24, :] += eight(widen(low_value))

    by_rows(mid.shape[0] // 2, norm)
    flush(0)
    flush(1)
    d_att[...] = mm_t(d_branch[...], w_proj[...]).astype(bf16)
    rows = stat[...].T
    for h in range(heads):
        q, k, v = heads_of(qkv, width, size, h)
        d = d_att[:, h * size : (h + 1) * size]
        p = jnp.exp(mm_t(k, q) - rows[h : h + 1, :])
        dv = mm(p.astype(bf16), d)
        d_p = mm_t(v, d)
        ds = (p * (d_p - jnp.sum(p * d_p, axis=0, keepdims=True))).astype(bf16)
        dk = mm(ds, q)
        dq = widen(t_mm(ds, k).astype(bf16)) * 0.125
        for i, value in enumerate((dq, dk, dv)):
            at = i * width + h * size
            d_joined[:, at : at + size] = value.astype(bf16)
    flush(2)
    joined_sum[...] = eight(widen(d_joined[...]))
    by_cols(low.shape[1], lambda cols: put(low, cols, mm_t(d_joined[...], w_qkv[cols, :])))


def attend_back(grad, mid, sent, vec, qkv, stat, w_proj, w_qkv, layer, heads, size):
    toks, width = mid.shape
    wide = 3 * heads * size
    outs = [((toks, width), f32, True), ((toks, width), bf16, True), ((toks, wide), bf16, True)]
    outs = outs + [((toks, width), bf16), ((24, width), f32), ((8, wide), f32)]
    args = [grad, mid, *sent, vec, qkv, stat, w_proj, w_qkv]
    flops = 8 * toks * width * heads * size + 10 * heads * toks * toks * size
    return call(
        functools.partial(attend_back_body, layer, heads, size),
        outs,
        args,
        flops,
        heads * toks * toks,
        [pltpu.VMEM((toks, heads * size), bf16)],
    )


def last_body(flush, where, *refs):
    streams, vec, grad, sums = (refs[0:6], refs[6:12]), refs[12], refs[13], refs[14]
    sums[...] = jnp.zeros_like(sums)
    for s, (base, d_mid, *sent) in enumerate(streams):

        def norm(whole, half, part_rows):
            e = summed(sent, whole, half, part_rows)
            d, by_gain = norm_grad(e, widen(base[whole, :]), row(vec, GAIN_ONE, 0))
            sums[0:8, :] += eight(by_gain)
            sums[8:16, :] += eight(e)
            if half == 0:

                @pl.when(where[1] == s)
                def _():
                    grad[part_rows, :] = d_mid[whole, :] + d

        by_rows(base.shape[0] // 2, norm)
    flush(0)


def last_back(where, streams, vec):
    toks, width = streams[0][0].shape
    outs = [((toks // 2, width), f32, True), ((16, width), f32)]
    args = [where, *streams[0], *streams[1], vec]
    return call(last_body, outs, args, 20 * toks * width, smem=1)


def pick_body(toks, flush, where, own, side, across, beside, *outs):
    for i in range(2):
        at = slice(i * toks, (i + 1) * toks)
        for s in range(2):
            out = outs[2 * i + s]

            @pl.when(where[1] == s)
            def _():
                out[0:toks, :] = own[at, :]
                out[toks:, :] = side[at, :]

            @pl.when(where[1] != s)
            def _():
                out[0:toks, :] = across[at, :]
                out[toks:, :] = beside[at, :]

            flush(2 * i + s)


def halves(first, second, c):
    low = lax.broadcasted_iota(jnp.int32, first.shape, 1) < first.shape[1] // 2
    half = first.shape[1] // 2
    zero = jnp.where(low, first, pltpu.roll(second, half, 1))
    other = jnp.where(low, pltpu.roll(first, half, 1), second)
    return jnp.where(c == 0, zero, other), jnp.where(c == 0, other, zero)


def units_body(rows, heads, size, flush, where, qkv, up, down, small, *outs):
    q_mine, q_theirs, u_mine, u_theirs, d_unit = outs
    c, y = where[0], where[1]
    pair = 2 * size
    for layer in range(LAYERS):
        at = slice(layer * rows, (layer + 1) * rows)
        for t in range(3):
            for h in range(0, heads, 2):
                start = (t * heads + h) * 2 * pair
                tiles = [
                    widen(qkv[layer, :, pl.ds(pl.multiple_of(start + i * 2 * pair + y * pair, pair), pair)])
                    for i in range(2)
                ]
                mine, theirs = halves(*tiles, c)
                cols = slice((t * heads + h) * size, (t * heads + h + 2) * size)
                q_mine[at, cols] = mine.astype(bf16)
                q_theirs[at, cols] = theirs.astype(bf16)
        blocks = up.shape[2] // (4 * pair)
        for f in range(blocks):
            for ref, core in ((u_mine, c), (u_theirs, 1 - c)):
                start = pl.multiple_of(f * 4 * pair + core * 2 * pair + y * pair, pair)
                ref[at, f * pair : (f + 1) * pair] = up[layer, :, pl.ds(start, pair)]
        half = down.shape[1] // 2
        d_unit[layer] = down[layer, pl.ds(pl.multiple_of(y * half, half), half), :]
    q_theirs[2 * rows :, :] = jnp.zeros((16, q_theirs.shape[1]), bf16)
    q_theirs[2 * rows :, 0:pair] = small[...]


def join_body(rows, flush, where, q_mine, q_side, u_mine, u_side, small, up_b, p_own, p_side, *outs):
    q0, q1, u0, u1, p0, p1 = outs
    c, y, x = where[0], where[1], where[2]
    pair = small.shape[1]
    here = pl.ds(pl.multiple_of(c * rows, rows), rows)
    there = pl.ds(pl.multiple_of((1 - c) * rows, rows), rows)
    for layer, (q, u, p) in enumerate(((q0, u0, p0), (q1, u1, p1))):
        at = slice(layer * rows, (layer + 1) * rows)
        q[here, :] = q_mine[at, :]
        q[there, :] = q_side[at, :]
        u[here, :] = u_mine[at, :]
        u[there, :] = u_side[at, :]

        @pl.when(x == y)
        def _():
            p[...] = p_own[layer]

        @pl.when(x != y)
        def _():
            p[...] = p_side[layer]

    low = lax.broadcasted_iota(jnp.int32, small.shape, 1) < pair // 2
    own, side = widen(small[...]), widen(q_side[2 * rows :, 0:pair])
    both = jnp.where(c == 0, jnp.where(low, own, side), jnp.where(low, side, own))
    q0[2 * rows :, :] = jnp.zeros((16, q0.shape[1]), bf16)
    q0[2 * rows :, 0:pair] = both.astype(bf16)
    ups = widen(up_b[...])
    ups = jnp.where(y == 0, ups[:, 0:pair], ups[:, pair : 2 * pair])
    q0[2 * rows :, pair : 2 * pair] = ups.astype(bf16)


def prep_body(n, heads, size, flush, where, small, vec, fix, up_b):
    c, y = where[0], where[1]
    pair = 2 * size
    for f in range(n):
        vec[:, f * pair : (f + 1) * pair] = widen(small[:, f * 2 * pair : f * 2 * pair + pair])
        up_b[:, f * pair : (f + 1) * pair] = widen(
            small[:, f * 2 * pair + pair : (f + 1) * 2 * pair]
        )
    width = heads * size
    for layer in range(LAYERS):
        for t, which in ((0, QUERY_B), (2, VALUE_B)):
            for i in range(0, heads, 2):
                tiles = [
                    widen(small[:, pl.ds(pl.multiple_of((2 * (i + j) + y) * 2 * pair, 2 * pair), pair)])
                    for j in range(2)
                ]
                mine, _ = halves(*tiles, c)
                at = 2 * which + layer
                start = t * width + i * size
                fix[2 * layer : 2 * layer + 1, start : start + pair] = mine[at : at + 1, :]
        fix[2 * layer : 2 * layer + 1, width : 2 * width] = jnp.zeros((1, width), f32)
        fix[2 * layer + 1 : 2 * layer + 2, 0:width] = jnp.full((1, width), 0.125, f32)
        fix[2 * layer + 1 : 2 * layer + 2, width:] = jnp.ones((1, 2 * width), f32)


def place_body(count, rows, extra, at_ref, *refs):
    n_out = 2 if extra else 1
    blocks, outs, sems = refs[: -1 - n_out], refs[-1 - n_out : -1], refs[-1]
    copies = []
    per = count // len(blocks)
    for i in range(count):
        source, base = blocks[i // per], (i % per) * (rows + extra)
        start = pl.multiple_of(at_ref[i] * rows, rows)
        copies.append(
            pltpu.make_async_copy(
                source.at[pl.ds(base, rows)], outs[0].at[pl.ds(start, rows)], sems.at[0, i]
            )
        )
        if extra:
            start = pl.multiple_of(at_ref[i] * 256, 256)
            copies.append(
                pltpu.make_async_copy(
                    source.at[pl.ds(base + rows, extra), pl.ds(0, 256)],
                    outs[1].at[:, pl.ds(start, 256)],
                    sems.at[1, i],
                )
            )
    for copy in copies:
        copy.start()
    for copy in copies:
        copy.wait()


def place(blocks, at, count, extra):
    total, cols = sum(b.shape[0] for b in blocks), blocks[0].shape[1]
    rows = total // count - extra
    outs = [jax.ShapeDtypeStruct((count * rows, cols), bf16)]
    if extra:
        outs.append(jax.ShapeDtypeStruct((extra, count * 256), bf16))
    return pl.pallas_call(
        functools.partial(place_body, count, rows, extra),
        in_specs=[pl.BlockSpec(memory_space=pltpu.SMEM)]
        + [pl.BlockSpec(memory_space=pltpu.VMEM)] * len(blocks),
        out_specs=tuple([pl.BlockSpec(memory_space=pl.ANY)] * len(outs)),
        scratch_shapes=[pltpu.SemaphoreType.DMA((2, count))],
        out_shape=tuple(outs),
        compiler_params=pltpu.CompilerParams(vmem_limit_bytes=VMEM_LIMIT),
        cost_estimate=pl.CostEstimate(flops=0, bytes_accessed=4 * total * cols, transcendentals=0),
        name="place",
    )(at, *blocks)


def gather_rows(unit, me, n, extra=0):
    nz = n // 2
    line = [unit] + [z_from(unit, k, n) for k in range(1, nz)]
    line = jnp.concatenate(line, axis=0)
    other = x_swap(line, n)
    z, x = me // 2, me % 2
    at = [((z + k) % nz) * 2 + x for k in range(nz)]
    at = at + [((z + k) % nz) * 2 + 1 - x for k in range(nz)]
    return place([line, other], jnp.stack(at).astype(jnp.int32), n, extra)


def gather_line(unit, me, n):
    nz = n // 2
    blocks = [unit] + [z_from(unit, k, n) for k in range(1, nz)]
    z = me // 2
    at = jnp.stack([(z + k) % nz for k in range(nz)]).astype(jnp.int32)
    return place(blocks, at, nz, 0)[0]


def split_body(nz, flush, where, *refs):
    grad, other = (refs[0], refs[1]) if len(refs) == 2 + nz else (refs[0], None)
    outs = refs[-nz:]
    x, z = where[2], where[3]
    rows = outs[0].shape[0]
    for k in range(nz):
        to = lax.rem(z - k + nz, nz)
        if other is None:
            value = grad[pl.ds(pl.multiple_of(to * rows, rows), rows), :]
        else:
            mine = grad[pl.ds(pl.multiple_of((to * 2 + x) * rows, rows), rows), :]
            value = widen(mine) + widen(other[pl.ds(pl.multiple_of(to * rows, rows), rows), :])
        outs[k][...] = value.astype(outs[k].dtype)


def scatter(grad, where, me, n, line=False):
    nz = n // 2
    count = nz if line else n
    rows, cols = grad.shape[0] // count, grad.shape[1]
    args = [where, grad]
    if not line:
        blocks = grad.reshape(nz, 2, rows, cols)
        sent = pick(blocks, 1, 1 - me % 2).reshape(nz * rows, cols)
        args.append(x_swap(sent, n))
    outs = [((rows, cols), f32)] + [((rows, cols), grad.dtype)] * (nz - 1)
    got = call(functools.partial(split_body, nz), outs, args, grad.size, smem=1)
    return [got[0]] + [z_from(got[k], k, n) for k in range(1, nz)]


def total_of(refs):
    total = widen(refs[0][...])
    for ref in refs[1:]:
        total = total + widen(ref[...])
    return total


def rows_body(rows, flush, where, *refs):
    mine, sent, total = refs[-3:]
    total[...] = total_of(refs[:-3])
    c = where[0]
    mine[...] = total[pl.ds(pl.multiple_of(c * rows, rows), rows), :]
    sent[0:rows, :] = mine[...].astype(bf16)
    other = total[pl.ds(pl.multiple_of((1 - c) * rows, rows), rows), :]
    sent[rows:, :] = other.astype(bf16)


def to_rows(pieces, where):
    rows, cols = pieces[0].shape[0] // 2, pieces[0].shape[1]
    outs = [((rows, cols), f32), ((2 * rows, cols), bf16)]
    mine, sent = call(
        functools.partial(rows_body, rows),
        outs,
        [where, *pieces],
        4 * sent_size(pieces),
        scratch=[pltpu.VMEM((2 * rows, cols), f32)],
        smem=1,
    )
    across = y_swap(sent)
    side = core_swap(sent[rows:])
    beyond = core_swap(across[rows:])
    return mine, side, across, beyond


def sent_size(pieces):
    return sum(p.size for p in pieces)


def sum_body(flush, *refs):
    total = total_of(refs[:-2])
    refs[-2][...] = total
    refs[-1][...] = total.astype(refs[-1].dtype)


def both_types(pieces):
    shape = pieces[0].shape
    return call(sum_body, [(shape, f32), (shape, bf16)], list(pieces), sent_size(pieces))


def finish_body(layer, n, heads, size, first, where, *refs):
    q, u = refs[0:4], refs[4:8]
    d_own, d_side, p_own, p_side = refs[8:12]
    outs = refs[12 if first else 16 :][:4]
    b_q, b_p, b_u, b_d, sems = refs[-5:]
    c, y, x = where[0], where[1], where[2]
    pair = 2 * size
    rows = q[0].shape[0]

    def quarters(pieces, cols):
        mine, side = pieces[0][:, cols], widen(pieces[1][:, cols])
        across, beyond = widen(pieces[2][0:rows, cols]), widen(pieces[3][:, cols])
        here = (jnp.where(c == 0, mine, side), jnp.where(c == 0, side, mine))
        there = (jnp.where(c == 0, across, beyond), jnp.where(c == 0, beyond, across))
        return [
            [jnp.where(y == at, here[core], there[core]) for core in range(2)] for at in range(2)
        ]

    def out(i, buffer):
        return pltpu.make_async_copy(buffer, outs[i].at[layer], sems.at[i])

    for t in range(3):
        for h in range(0, heads, 2):
            at = (t * heads + h) * size
            got = quarters(q, slice(at, at + pair))
            for across in range(2):
                one_head, next_head = halves(*got[across], 0)
                start = (t * heads + h) * 2 * pair + across * pair
                b_q[:, start : start + pair] = one_head
                b_q[:, start + 2 * pair : start + 3 * pair] = next_head
    out(0, b_q).start()
    for f in range(n):
        got = quarters(u, slice(f * pair, (f + 1) * pair))
        for across in range(2):
            for core in range(2):
                start = f * 4 * pair + core * 2 * pair + across * pair
                b_u[:, start : start + pair] = got[across][core]
    out(2, b_u).start()
    half = d_own.shape[0]
    b_d[pl.ds(pl.multiple_of(y * half, half), half), :] = d_own[...]
    b_d[pl.ds(pl.multiple_of((1 - y) * half, half), half), :] = widen(d_side[...])
    out(3, b_d).start()
    b_p[...] = jnp.where(x == y, p_own[...], widen(p_side[...]))
    out(1, b_p).start()
    for i, buffer in enumerate((b_q, b_p, b_u, b_d)):
        out(i, buffer).wait()


def finish(where, q, u, d, p, past, layer, n, heads, size):
    rows = q[0].shape[0]
    width = HEADS * size
    hid = n * 8 * size
    shapes = [(rows, 3 * width), (rows, width), (rows, hid), (2 * d[0].shape[0], width)]
    args = [where, *q, *u, *d, *p]
    aliases = {}
    if past is not None:
        aliases = {len(args) + i: i for i in range(4)}
        args = args + list(past)
    first = past is None
    spaces = [pltpu.SMEM] + [pltpu.VMEM] * 12 + [HBM] * (0 if first else 4)
    return pl.pallas_call(
        functools.partial(finish_body, layer, n, heads, size, first),
        out_shape=tuple(jax.ShapeDtypeStruct((LAYERS, *s), f32) for s in shapes),
        in_specs=[pl.BlockSpec(memory_space=s) for s in spaces],
        out_specs=tuple([pl.BlockSpec(memory_space=HBM)] * 4),
        scratch_shapes=[pltpu.VMEM(s, f32) for s in shapes]
        + [pltpu.SemaphoreType.DMA((4,))],
        input_output_aliases=aliases,
        compiler_params=pltpu.CompilerParams(vmem_limit_bytes=VMEM_LIMIT),
        cost_estimate=pl.CostEstimate(
            flops=0, bytes_accessed=4 << 20, transcendentals=0
        ),
        name="finish",
    )(*args)


def pack_body(n, heads, size, flush, where, *refs):
    first, upper, lower, out = refs[0], refs[1:9], refs[9:17], refs[17]
    c, y = where[0], where[1]
    pair = 2 * size
    out[...] = jnp.zeros_like(out)

    def rows_of(ref, i):
        return one(ref[8 * i : 8 * i + 8, :])

    def put_vector(which, layer, value):
        at = 2 * which + layer
        for f in range(n):
            out[f, at : at + 1, :] = 0.25 * value[:, f * pair : (f + 1) * pair]

    def both(refs_of, i):
        return rows_of(refs_of[0], i) + rows_of(refs_of[1], i)

    for layer, group in ((1, upper), (0, lower)):
        ups, mlp, att, joined = group[0:2], group[2:4], group[4:6], group[6:8]
        put_vector(DOWN_B, layer, both(mlp, 2))
        put_vector(GAIN_TWO, layer, both(att, 0))
        put_vector(SHIFT_TWO, layer, both(att, 1))
        put_vector(PROJ_B, layer, both(att, 2))
        value = one(ups[0][...]) + one(ups[1][...])
        at = 16 + 4 * layer + 2 * c + y
        for f in range(n):
            out[f, pl.ds(at, 1), :] = value[:, f * pair : (f + 1) * pair]
        value = one(joined[0][...]) + one(joined[1][...])
        low = lax.broadcasted_iota(jnp.int32, (1, pair), 1) < size
        for t, which in ((0, QUERY_B), (2, VALUE_B)):
            at = 2 * which + layer
            for i in range(0, heads, 2):
                start = (t * heads + i) * size
                tile = value[:, start : start + pair]
                turned = pltpu.roll(jnp.broadcast_to(tile, (8, pair)), size, 1)[0:1, :]
                zero = jnp.zeros_like(tile)
                even = jnp.where(c == 0, jnp.where(low, tile, zero), jnp.where(low, zero, turned))
                odd = jnp.where(c == 0, jnp.where(low, turned, zero), jnp.where(low, zero, tile))
                out[2 * i + y, at : at + 1, :] = even
                out[2 * (i + 1) + y, at : at + 1, :] = odd
    mlp = lower[2:4]
    put_vector(GAIN_ONE, 1, both(mlp, 0))
    put_vector(SHIFT_ONE, 1, both(mlp, 1))
    put_vector(GAIN_ONE, 0, rows_of(first, 0))
    put_vector(SHIFT_ONE, 0, rows_of(first, 1))


def send_part(low):
    side = core_swap(low)
    half = low.shape[0] // 2
    mine = (widen(low[:half]) + widen(side[half:])).astype(bf16)
    across = y_swap(mine)
    beside = core_swap(across)
    return low, side, across, beside


def on_device(
    clips_in,
    cotangent,
    clip_mask,
    norm1_gain,
    norm1_bias,
    qkv_weight,
    query_bias,
    value_bias,
    proj_weight,
    proj_bias,
    norm2_gain,
    norm2_bias,
    up_weight,
    up_bias,
    down_weight,
    down_bias,
    *,
    n,
):
    c, y, f = lax.axis_index("seq"), lax.axis_index("replica"), lax.axis_index("fsdp")
    quarter = 2 * y + c
    toks, width = clips_in.shape[1], clips_in.shape[2]
    rows = qkv_weight.shape[1]
    hid_rows = down_weight.shape[1]
    hidden = up_weight.shape[2]
    size = width // HEADS
    heads = HEADS // 4
    fast = n == 8 and rows == size and hid_rows == 4 * rows

    where = jnp.stack([c, y, f % 2, f // 2]).astype(jnp.int32)

    masked = (widen(cotangent[0]) * widen(clip_mask)[0]).astype(bf16)
    own = jnp.concatenate([clips_in[0], masked], axis=0)
    side = core_swap(own)
    across = y_swap(own)
    beside = core_swap(across)
    got = call(
        functools.partial(pick_body, toks),
        [((2 * toks, width), bf16, True)] * 4,
        [where, own, side, across, beside],
        0,
        smem=1,
    )
    resid, start = list(got[:2]), got[2:]

    def qkv_cols(w, at):
        w = w.reshape(*w.shape[:-1], 3, heads, 4, size)
        return pick(w, w.ndim - 2, at).reshape(*w.shape[:-4], 3 * heads * size)

    def up_cols(w, at_c, at_y):
        w = w.reshape(*w.shape[:-1], n, 2, 2, hid_rows // 2)
        w = pick(w, w.ndim - 2, at_y)
        return pick(w, w.ndim - 2, at_c).reshape(*w.shape[:-3], hidden // 4)

    flat = [
        norm1_gain,
        norm1_bias,
        query_bias,
        value_bias,
        proj_bias,
        norm2_gain,
        norm2_bias,
        down_bias,
    ]
    weights = []
    if fast:
        flat_rows = jnp.concatenate(flat, axis=0)
        small = jnp.concatenate([flat_rows, flat_rows], axis=1)
        up_b_rows = jnp.concatenate([up_bias, jnp.zeros((14, hid_rows), bf16)], axis=0)
        wide = 3 * heads * size
        outs = [((2 * rows, wide), bf16), ((2 * rows + 16, wide), bf16)]
        outs = outs + [((2 * rows, hidden // 4), bf16)] * 2
        outs = outs + [((LAYERS, hid_rows // 2, width), bf16)]
        q_mine, q_theirs, u_mine, u_theirs, down_units = call(
            functools.partial(units_body, rows, heads, size),
            outs,
            [where, qkv_weight, up_weight, down_weight, small],
            0,
            smem=1,
        )
        q_side, u_side = core_swap(q_theirs), core_swap(u_theirs)
        p_side = x_swap(proj_weight, n)
        outs = [((2 * rows + 16, wide), bf16), ((2 * rows, wide), bf16)]
        outs = outs + [((2 * rows, hidden // 4), bf16)] * 2 + [((rows, width), bf16)] * 2
        q0, q1, u0, u1, p0, p1 = call(
            functools.partial(join_body, rows),
            outs,
            [where, q_mine, q_side, u_mine, u_side, small, up_b_rows, proj_weight, p_side],
            0,
            smem=1,
        )
        for layer, (q, u, p) in enumerate(((q0, u0, p0), (q1, u1, p1))):
            extra = 16 if layer == 0 else 0
            got = gather_rows(q, f, n, extra)
            if extra:
                shapes = [((16, width), f32), ((2 * LAYERS, wide), f32), ((16, hidden // 4), f32)]
                vec, fix, up_b = call(
                    functools.partial(prep_body, n, heads, size), shapes, [where, got[1]], 0, smem=1
                )
            weights.append(
                (
                    got[0],
                    gather_line(p, f, n),
                    gather_rows(u, f, n)[0],
                    gather_rows(down_units[layer], f, n)[0],
                )
            )
    else:
        packed = jnp.concatenate(flat + [up_bias], axis=1)
        everything = lax.all_gather(packed, ("fsdp", "seq"), axis=0)
        for layer in range(LAYERS):
            full = [
                lax.all_gather(w[layer], ("fsdp", "seq"), axis=0, tiled=True)
                for w in (qkv_weight, proj_weight, up_weight, down_weight)
            ]
            by_head = full[1].reshape(heads, 4, size, width)
            by_hid = full[3].reshape(n, 2, 2, hid_rows // 2, width)
            weights.append(
                (
                    qkv_cols(full[0], quarter),
                    pick(by_head, 1, quarter).reshape(heads * size, width),
                    up_cols(full[2], c, y),
                    pick(pick(by_hid, 2, y), 1, c).reshape(hidden // 4, width),
                )
            )

        vectors = everything[:, :, : 8 * rows].reshape(2 * n, LAYERS, 8, rows)
        vectors = widen(vectors.transpose(2, 1, 0, 3).reshape(8, LAYERS, width))
        vec = vectors.reshape(8 * LAYERS, width)
        up_b = everything[:, :, 8 * rows :].reshape(n, 2, LAYERS, 2, hid_rows // 2)
        up_b = pick(pick(up_b, 3, y), 1, c).transpose(1, 0, 2)
        up_b = widen(up_b.reshape(LAYERS, hidden // 4))
        by_head = vectors.reshape(8, LAYERS, heads, 4, size)
        by_head = pick(by_head, 3, quarter).reshape(8, LAYERS, heads * size)
        zero = jnp.zeros_like(by_head[0])
        add = jnp.concatenate([by_head[QUERY_B], zero, by_head[VALUE_B]], axis=1)
        times = jnp.concatenate([zero + 0.125, zero + 1.0, zero + 1.0], axis=1)
        fix = jnp.stack([add, times], axis=1).reshape(2 * LAYERS, -1)

    streams = range(2)
    sent = [None, None]
    stash = []
    for layer in range(LAYERS):
        w_qkv, w_proj, w_up, w_down = weights[layer]
        kept = []
        for s in streams:
            before, normed, qkv, attended, stat, low = attend(
                resid[s], sent[s], vec, w_qkv, fix, w_proj, layer, heads, size
            )
            got = send_part(low)
            mid, normed_two, active, slope = go_up(before, got, vec, w_up, up_b, layer)
            kept.append((before, normed, qkv, attended, mid, normed_two, slope, active, stat))
            sent[s] = send_part(go_down(active, w_down))
            resid[s] = mid
        stash.append(kept)

    def own_rows(pair):
        return jnp.where(y == 0, pair[0], pair[1])

    last_bias = vec[2 * DOWN_B + LAYERS - 1]
    clips_out = own_rows([r[:toks] for r in resid]) + (
        widen(own_rows([p[0][:toks] for p in sent]))
        + widen(own_rows([p[1][toks:] for p in sent]))
        + widen(own_rows([p[2] for p in sent]))
        + last_bias
    )
    clips_out = clips_out.astype(bf16)[None]

    grads = [None] * LAYERS
    tallies = [None] * LAYERS
    d_mid, sent = [None, None], [None, None]

    def both_t_mm(left, right):
        return t_mm(
            jnp.concatenate(left, axis=0), jnp.concatenate(right, axis=0)
        ).astype(bf16)

    for layer in reversed(range(LAYERS)):
        w_qkv, w_proj, w_up, w_down = weights[layer]
        kept = stash[layer]
        d_mlp, d_pre, d_branch, d_joined, grad = [], [], [], [], []
        ups, mlp, att, joined = [], [], [], []
        for s in streams:
            slope = kept[s][6]
            if layer == LAYERS - 1:
                got = (start[s], start[s]) + tuple(
                    mlp_back(start[s], None, None, None, None, slope, w_down, w_up, layer)
                )
            else:
                after = stash[layer + 1][s][0]
                got = mlp_back(None, after, d_mid[s], sent[s], vec, slope, w_down, w_up, layer)
            grad.append(got[0])
            d_mlp.append(got[1])
            d_pre.append(got[2])
            ups.append(got[4])
            mlp.append(got[5])
            sent[s] = send_part(got[3])
        g_down = both_t_mm([k[7] for k in kept], d_mlp)
        g_up = both_t_mm([k[5] for k in kept], d_pre)
        for s in streams:
            _, _, qkv, _, mid, _, _, _, stat = kept[s]
            got = attend_back(
                grad[s], mid, sent[s], vec, qkv, stat, w_proj, w_qkv, layer, heads, size
            )
            d_mid[s] = got[0]
            d_branch.append(got[1])
            d_joined.append(got[2])
            att.append(got[4])
            joined.append(got[5])
            sent[s] = send_part(got[3])
        g_proj = both_t_mm([k[3] for k in kept], d_branch)
        g_qkv = both_t_mm([k[1] for k in kept], d_joined)
        grads[layer] = (g_qkv, g_proj, g_up, g_down)
        tallies[layer] = [*ups, *mlp, *att, *joined]
    ends = [(stash[0][s][0], d_mid[s], *sent[s]) for s in streams]
    input_grad, first = last_back(where, ends, vec)
    input_grad = input_grad[None]

    if fast:
        tiny = call(
            functools.partial(pack_body, n, heads, size),
            [((n, 24, 2 * rows), f32)],
            [where, first, *tallies[1], *tallies[0]],
            0,
            smem=1,
        )[0]
        tiny = scatter(tiny.reshape(n * 24, 2 * rows), where, f, n)
        tiny = (tiny[0] + tiny[1]) + (tiny[2] + tiny[3])
        tiny = tiny + core_swap(tiny)
        tiny = tiny + y_swap(tiny)
        vecs = pick(tiny[:16].reshape(8, LAYERS, 2, rows), 2, c)
        ups = pick(tiny[16:].reshape(LAYERS, 2, 2 * 2 * rows), 1, c)
        outs = None
        for layer in reversed(range(LAYERS)):
            g_qkv, g_proj, g_up, g_down = grads[layer]
            d = both_types(scatter(g_down, where, f, n))
            d = (d[0], y_swap(d[1]))
            u = to_rows(scatter(g_up, where, f, n), where)
            q = to_rows(scatter(g_qkv, where, f, n), where)
            p = both_types(scatter(g_proj, where, f, n, True))
            side = x_swap(p[1], n)
            p = both_types([p[0], side])
            p = (p[0], y_swap(p[1]))
            outs = finish(where, q, u, d, p, outs, layer, n, heads, size)
        qkv_out, proj_out, up_out, down_out = outs
    else:
        here = (jnp.arange(4) == quarter).reshape(1, 1, 4, 1)
        at_c = (jnp.arange(2) == c).reshape(1, 2, 1, 1)
        at_y = (jnp.arange(2) == y).reshape(1, 1, 2, 1)

        def rows_of(pair, i):
            return jnp.sum(pair[0][8 * i : 8 * i + 8] + pair[1][8 * i : 8 * i + 8], axis=0)

        by_owner = []
        for layer in range(LAYERS):
            tally = tallies[layer]
            ups, mlp, att, joined = [tally[2 * i : 2 * i + 2] for i in range(4)]
            if layer == 0:
                one_sums = [jnp.sum(first[8 * i : 8 * i + 8], axis=0) for i in range(2)]
            else:
                one_sums = [rows_of(tallies[layer - 1][2:4], i) for i in range(2)]
            joined = rows_of(joined, 0).reshape(3, heads, 1, size)[0::2]
            joined = jnp.where(here, joined, 0.0).reshape(2, width)
            alike = [rows_of(mlp, 2), *one_sums, rows_of(att, 2), rows_of(att, 0), rows_of(att, 1)]
            alike = [0.25 * v for v in alike]
            vecs = [alike[1], alike[2], joined[0], joined[1], alike[3], alike[4], alike[5], alike[0]]
            vecs = jnp.stack(vecs).reshape(8, 2 * n, rows).transpose(1, 0, 2)
            up = rows_of(ups, 0).reshape(n, 1, 1, hid_rows // 2)
            up = jnp.where(at_c & at_y, up, 0.0).reshape(2 * n, hid_rows)
            by_owner.append(jnp.concatenate([vecs.reshape(2 * n, 8 * rows), up], axis=1))
        total = lax.psum(jnp.stack(by_owner, axis=1), ("fsdp", "seq", "replica"))
        tiny = pick(total, 0, 2 * f + c)
        vecs = tiny[:, : 8 * rows].reshape(LAYERS, 8, rows).transpose(1, 0, 2)
        ups = tiny[:, 8 * rows :]
        axes = ("replica", "seq")

        def owned(full):
            block = lax.psum_scatter(full, "fsdp", scatter_dimension=0, tiled=True)
            half = block.shape[0] // 2
            return widen(lax.dynamic_slice_in_dim(block, c * half, half, axis=0))

        outs = []
        for layer in range(LAYERS):
            g_qkv, g_proj, g_up, g_down = grads[layer]
            g = lax.all_gather(g_qkv, axes, axis=0).reshape(4, width, 3, heads, size)
            qkv_out = owned(g.transpose(1, 2, 3, 0, 4).reshape(width, 3 * width))
            g = lax.all_gather(g_proj, axes, axis=0).reshape(4, heads, size, width)
            proj_out = owned(g.transpose(1, 0, 2, 3).reshape(width, width))
            g = lax.all_gather(g_up, axes, axis=0)
            g = g.reshape(2, 2, width, n, hid_rows // 2)
            up_out = owned(g.transpose(2, 3, 1, 0, 4).reshape(width, hidden))
            g = lax.all_gather(g_down, axes, axis=0)
            g = g.reshape(2, 2, n, hid_rows // 2, width)
            down_out = owned(g.transpose(2, 1, 0, 3, 4).reshape(hidden, width))
            outs.append((qkv_out, proj_out, up_out, down_out))
        qkv_out, proj_out, up_out, down_out = [
            jnp.stack([outs[layer][i] for layer in range(LAYERS)]) for i in range(4)
        ]
    return (
        clips_out,
        input_grad,
        vecs[GAIN_ONE],
        vecs[SHIFT_ONE],
        qkv_out,
        vecs[QUERY_B],
        vecs[VALUE_B],
        proj_out,
        vecs[PROJ_B],
        vecs[GAIN_TWO],
        vecs[SHIFT_TWO],
        up_out,
        ups,
        down_out,
        vecs[DOWN_B],
    )


def solution(mesh):
    tokens = P(("fsdp", "replica"), "seq", None)
    vector = P(None, ("fsdp", "seq"))
    matrix = P(None, ("fsdp", "seq"), None)
    kinds = [
        vector,
        vector,
        matrix,
        vector,
        vector,
        matrix,
        vector,
        vector,
        vector,
        matrix,
        vector,
        matrix,
        vector,
    ]
    return jax.shard_map(
        functools.partial(on_device, n=mesh.shape["fsdp"]),
        mesh=mesh,
        in_specs=(tokens, tokens, P(("fsdp", "replica")), *kinds),
        out_specs=(tokens, tokens, *kinds),
        check_vma=False,
    )
```

time: 961 us -> 705 us (0.73)
  local copies, waits for them, and re-layouts: 175 us -> 46 us
  waiting for transfers between devices: 355 us -> 276 us
  other arithmetic: 50 us -> 11.2 us
    ppermute x34 -> x16, waiting for transfers between devices: 147 us -> 76.7 us  [x_swap(): return lax.ppermute(v, 'fsdp', [(f, f ^ 1) for f in range(n)])]
    unnamed x490 -> x343, local copies, waits for them, and re-layouts: 99.7 us -> 40 us
    ppermute x51, waiting for transfers between devices: 149 us -> 119 us  [z_from(): lax.ppermute(v, 'fsdp', [((z + k) % nz * 2 + x, z * 2 + x) for z in range...]
    ppermute x34 -> x16, starting transfers between devices: 39.3 us -> 17 us  [x_swap(): return lax.ppermute(v, 'fsdp', [(f, f ^ 1) for f in range(n)])]
    ppermute x51, starting transfers between devices: 98.4 us -> 118 us  [z_from(): lax.ppermute(v, 'fsdp', [((z + k) % nz * 2 + x, z * 2 + x) for z in range...]
    convert_element_type x36 -> x16, other arithmetic: 22.2 us -> 3.74 us  [send_part(): mine = (widen(low[:half]) + widen(side[half:])).astype(bf16)]
    ppermute x27 -> x26, waiting for transfers between devices: 57.7 us -> 72.7 us  [y_swap(): return lax.ppermute(v, 'replica', PAIR)]
    reshape x14 -> x2, local copies, waits for them, and re-layouts: 12.9 us -> 0.09 us  [the longest x1 0.08 us: on_device(): vecs = pick(tiny[:16].reshape(8, LAYERS, 2, rows), 2, c)]
  transfers between devices with their start and end apart: 153 -> 136, of which waited for: 61 -> 44; matrix products, arithmetic and copies ran while one was open for 15% -> 5% of each run, Pallas kernels for 17% -> 26%
where the time goes in v2:
time: 705 us; the launch traced here: 699 us
  waiting for transfers between devices  276 us (39%)
  Pallas kernels  181 us (26%)
  starting transfers between devices  166 us (24%)
  local copies, waits for them, and re-layouts  46 us (7%)
  matrix products  14.9 us (2%)
  other arithmetic  11.2 us (2%)
    pallas_call x45, Pallas kernels, call(): pl.pallas_call(run, out_shape=shapes, in_specs=[pl.BlockSpec(memory_space...  162 us
    ppermute x51, waiting for transfers between devices, z_from(): lax.ppermute(v, 'fsdp', [((z + k) % nz * 2 + x, z * 2 + x) for z in range...  119 us
    ppermute x51, starting transfers between devices, z_from(): lax.ppermute(v, 'fsdp', [((z + k) % nz * 2 + x, z * 2 + x) for z in range...  118 us
    ppermute x16, waiting for transfers between devices, x_swap(): return lax.ppermute(v, 'fsdp', [(f, f ^ 1) for f in range(n)])  76.7 us
    ppermute x26, waiting for transfers between devices, y_swap(): return lax.ppermute(v, 'replica', PAIR)  72.7 us
    unnamed x343, local copies, waits for them, and re-layouts  40 us
    ppermute x26, starting transfers between devices, y_swap(): return lax.ppermute(v, 'replica', PAIR)  26.2 us
    ppermute x16, starting transfers between devices, x_swap(): return lax.ppermute(v, 'fsdp', [(f, f ^ 1) for f in range(n)])  17 us
  transfers between devices with their start and end apart: 136, of which 44 were waited for; matrix products, arithmetic and copies ran while one was open for 5% of the time, Pallas kernels for 26%

profile of v2, /device:TPU:0, one launch (start us, length us, event | category | flops | bytes accessed | tf_op | source)
XLA Modules:
  0.0 698.9 jit_solution(11547065728145523931)
XLA Ops:
  14.5 3.7 collective-permute-start.6
  19.2 4.8 collective-permute-done.6
  24.0 13.2 %collective-permute-done.7 = bf16[144,768]{1,0:T(8,128)(2,1)S(1)} collective-permute-done((bf16[144,768]{1,0:T(8,128)(2,1)S(1)}, bf16[144,768]{1,0:T(8,128)(2,1)S(1)}, u32[]{:S(2)}, u32[]{:S(2)}) %collective-permute-start.7) | collective-permute-done | bytes 221216 | tf_op jit(solution)/shard_map/ppermute | solution.py:55
  38.5 3.4 collective-permute-start.11
  41.9 4.4 collective-permute-done.12.refs_3_
  59.6 3.3 collective-permute-start.20
  62.9 3.4 place.8
  69.8 8.4 %shard_map.280 = (bf16[448,1024]{1,0:T(8,128)(2,1)S(1)}, bf16[448,768]{1,0:T(8,128)(2,1)S(1)}, bf16[448,256]{1,0:T(8,128)(2,1)S(1)}, f32[448,128]{1,0:T(8,128)S(1)}, bf16[448,1024]{1,0:T(8,128)(2,1)S(1)}) custom-call(bf16[448,1024]{1,0:T(8,128)(2,1)S(1)} %get-tuple-element.206.refs_0_.refs_7_, ...), custom_call_target="tpu_custom_call" | custom-call | flops 1145044992 | bytes 6074368 | tf_op jit(solution)/shard_map/pallas_call | solution.py:93
  83.8 10.5 %collective-permute-done.16 = bf16[128,1024]{1,0:T(8,128)(2,1)S(1)} collective-permute-done((bf16[128,1024]{1,0:T(8,128)(2,1)S(1)}, bf16[128,1024]{1,0:T(8,128)(2,1)S(1)}, u32[]{:S(2)}, u32[]{:S(2)}) %collective-permute-start.16) | collective-permute-done | bytes 262176 | tf_op jit(solution)/shard_map/ppermute | solution.py:55
  94.3 8.5 %collective-permute-done.17 = bf16[128,1024]{1,0:T(8,128)(2,1)S(1)} collective-permute-done((bf16[128,1024]{1,0:T(8,128)(2,1)S(1)}, bf16[128,1024]{1,0:T(8,128)(2,1)S(1)}, u32[]{:S(2)}, u32[]{:S(2)}) %collective-permute-start.17) | collective-permute-done | bytes 262176 | tf_op jit(solution)/shard_map/ppermute | solution.py:55
  104.1 8.4 %shard_map.275 = (bf16[448,1024]{1,0:T(8,128)(2,1)S(1)}, bf16[448,768]{1,0:T(8,128)(2,1)S(1)}, bf16[448,256]{1,0:T(8,128)(2,1)S(1)}, f32[448,128]{1,0:T(8,128)S(1)}, bf16[448,1024]{1,0:T(8,128)(2,1)S(1)}) custom-call(bf16[448,1024]{1,0:T(8,128)(2,1)S(1)} %get-tuple-element.183.refs_0_.refs_1_, ...), custom_call_target="tpu_custom_call" | custom-call | flops 1145044992 | bytes 6074368 | tf_op jit(solution)/shard_map/pallas_call | solution.py:93
  114.0 12.4 %collective-permute-done.42.refs_3_ = bf16[224,1024]{1,0:T(8,128)(2,1)S(1)} collective-permute-done((bf16[224,1024]{1,0:T(8,128)(2,1)S(1)}, bf16[224,1024]{1,0:T(8,128)(2,1)S(1)}, u32[]{:S(2)}, u32[]{:S(2)}) %collective-permute-start.42) | collective-permute-done | bytes 458784 | tf_op jit(solution)/shard_map/ppermute | solution.py:46
  131.9 6.1 shard_map.281
  147.2 3.8 collective-permute-done.27
  151.1 6.1 shard_map.276
  160.7 4.0 collective-permute-done.28
  165.4 7.7 %collective-permute-done.45.refs_3_ = bf16[224,1024]{1,0:T(8,128)(2,1)S(1)} collective-permute-done((bf16[224,1024]{1,0:T(8,128)(2,1)S(1)}, bf16[224,1024]{1,0:T(8,128)(2,1)S(1)}, u32[]{:S(2)}, u32[]{:S(2)}) %collective-permute-start.45) | collective-permute-done | bytes 458784 | tf_op jit(solution)/shard_map/ppermute | solution.py:46
  173.1 10.4 %collective-permute-start.33 = (bf16[64,1024]{1,0:T(8,128)(2,1)S(1)}, bf16[64,1024]{1,0:T(8,128)(2,1)S(1)}, u32[]{:S(2)}, u32[]{:S(2)}) collective-permute-start(bf16[64,1024]{1,0:T(8,128)(2,1)S(1)} %copy-done.91), channel_id=1, source_target_pairs={{24,0},{28,4},{0,8},{4,12},{8,16},{12,20},{16,24},{20,28},{25,1},{... | collective-permute-start | bytes 393224 | tf_op jit(solution)/shard_map/ppermute | solution.py:55
  188.0 4.7 collective-permute-done.32.refs_2_
  195.7 3.4 collective-permute-start.51
  203.2 8.8 %shard_map.283 = (f32[448,1024]{1,0:T(8,128)S(1)}, bf16[448,1024]{1,0:T(8,128)(2,1)S(1)}, bf16[448,768]{1,0:T(8,128)(2,1)S(1)}, bf16[448,256]{1,0:T(8,128)(2,1)S...) custom-call(f32[448,1024]{1,0:T(8,128)S(1)} %get-tuple-element.208.refs_0_.refs_1_, ...), custom_call_target="tpu_custom_call" | custom-call | flops 1145044992 | bytes 11579392 | tf_op jit(solution)/shard_map/pallas_call | solution.py:93
  216.3 8.1 %collective-permute-start.39 = (bf16[128,1024]{1,0:T(8,128)(2,1)S(1)}, bf16[128,1024]{1,0:T(8,128)(2,1)S(1)}, u32[]{:S(2)}, u32[]{:S(2)}) collective-permute-start(bf16[128,1024]{1,0:T(8,128)(2,1)S(1)} %copy-done.64), channel_id=1, source_target_pairs={{24,0},{28,4},{0,8},{4,12},{8,16},{12,20},{16,24},{20,28},{25,1},{... | collective-permute-start | bytes 786440 | tf_op jit(solution)/shard_map/ppermute | solution.py:55
  224.4 3.4 collective-permute-start.38
  228.7 15.6 %collective-permute-done.38 = bf16[128,1024]{1,0:T(8,128)(2,1)S(1)} collective-permute-done((bf16[128,1024]{1,0:T(8,128)(2,1)S(1)}, bf16[128,1024]{1,0:T(8,128)(2,1)S(1)}, u32[]{:S(2)}, u32[]{:S(2)}) %collective-permute-start.38) | collective-permute-done | bytes 262176 | tf_op jit(solution)/shard_map/ppermute | solution.py:55
  244.4 9.0 %shard_map.278 = (f32[448,1024]{1,0:T(8,128)S(1)}, bf16[448,1024]{1,0:T(8,128)(2,1)S(1)}, bf16[448,768]{1,0:T(8,128)(2,1)S(1)}, bf16[448,256]{1,0:T(8,128)(2,1)S...) custom-call(f32[448,1024]{1,0:T(8,128)S(1)} %get-tuple-element.197.refs_0_.refs_1_, ...), custom_call_target="tpu_custom_call" | custom-call | flops 1145044992 | bytes 11579392 | tf_op jit(solution)/shard_map/pallas_call | solution.py:93
  256.4 12.1 %collective-permute-done.48.refs_3_ = bf16[224,1024]{1,0:T(8,128)(2,1)S(1)} collective-permute-done((bf16[224,1024]{1,0:T(8,128)(2,1)S(1)}, bf16[224,1024]{1,0:T(8,128)(2,1)S(1)}, u32[]{:S(2)}, u32[]{:S(2)}) %collective-permute-start.48) | collective-permute-done | bytes 458784 | tf_op jit(solution)/shard_map/ppermute | solution.py:46
  270.1 10.4 %collective-permute-done.40.refs_1_ = bf16[512,1024]{1,0:T(8,128)(2,1)S(1)} collective-permute-done((bf16[512,1024]{1,0:T(8,128)(2,1)S(1)}, bf16[512,1024]{1,0:T(8,128)(2,1)S(1)}, u32[]{:S(2)}, u32[]{:S(2)}) %collective-permute-start.40) | collective-permute-done | bytes 1048608 | tf_op jit(solution)/shard_map/ppermute | solution.py:50
  281.4 6.1 shard_map.284
  287.5 4.0 shard_map.291
  295.6 6.0 shard_map.279
  303.6 4.0 shard_map.287
  308.6 12.3 %collective-permute-done.71.refs_4_ = bf16[224,1024]{1,0:T(8,128)(2,1)S(1)} collective-permute-done((bf16[224,1024]{1,0:T(8,128)(2,1)S(1)}, bf16[224,1024]{1,0:T(8,128)(2,1)S(1)}, u32[]{:S(2)}, u32[]{:S(2)}) %collective-permute-start.71) | collective-permute-done | bytes 458784 | tf_op jit(solution)/shard_map/ppermute | solution.py:46
  322.8 10.4 %shard_map.292 = (f32[448,1024]{1,0:T(8,128)S(1)}, bf16[448,1024]{1,0:T(8,128)(2,1)S(1)}, bf16[448,768]{1,0:T(8,128)(2,1)S(1)}, bf16[448,1024]{1,0:T(8,128)(2,1)...) custom-call(bf16[448,1024]{1,0:T(8,128)(2,1)S(1)} %get-tuple-element.229.refs_0_, ...), custom_call_target="tpu_custom_call" | custom-call | flops 1453326336 | bytes 13066240 | tf_op jit(solution)/shard_map/pallas_call | solution.py:93
  338.5 11.5 %shard_map.288 = (f32[448,1024]{1,0:T(8,128)S(1)}, bf16[448,1024]{1,0:T(8,128)(2,1)S(1)}, bf16[448,768]{1,0:T(8,128)(2,1)S(1)}, bf16[448,1024]{1,0:T(8,128)(2,1)...) custom-call(bf16[448,1024]{1,0:T(8,128)(2,1)S(1)} %get-tuple-element.215.refs_0_, ...), custom_call_target="tpu_custom_call" | custom-call | flops 1453326336 | bytes 13066240 | tf_op jit(solution)/shard_map/pallas_call | solution.py:93
  354.8 12.4 %collective-permute-done.74.refs_4_ = bf16[224,1024]{1,0:T(8,128)(2,1)} collective-permute-done((bf16[224,1024]{1,0:T(8,128)(2,1)S(1)}, bf16[224,1024]{1,0:T(8,128)(2,1)}, u32[]{:S(2)}, u32[]{:S(2)}) %collective-permute-start.74) | collective-permute-done | bytes 458784 | tf_op jit(solution)/shard_map/ppermute | solution.py:46
  377.9 9.7 %shard_map.293 = (f32[448,1024]{1,0:T(8,128)S(1)}, bf16[448,1024]{1,0:T(8,128)(2,1)S(1)}, bf16[448,1024]{1,0:T(8,128)(2,1)S(1)}, bf16[448,1024]{1,0:T(8,128)(2,1...) custom-call(f32[448,1024]{1,0:T(8,128)S(1)} %copy-done.10, f32[448,1024]{1,0:T(8,128)S(1)} %copy-done.32, ...), custom_call_target="tpu_custom_call" | custom-call | flops 1879048192 | bytes 16318464 | tf_op jit(solution)/shard_map/pallas_call | solution.py:93
  394.7 10.2 %shard_map.289 = (f32[448,1024]{1,0:T(8,128)S(1)}, bf16[448,1024]{1,0:T(8,128)(2,1)S(1)}, bf16[448,1024]{1,0:T(8,128)(2,1)S(1)}, bf16[448,1024]{1,0:T(8,128)(2,1...) custom-call(f32[448,1024]{1,0:T(8,128)S(1)} %copy-done.12, f32[448,1024]{1,0:T(8,128)S(1)} %copy-done.30, ...), custom_call_target="tpu_custom_call" | custom-call | flops 1879048192 | bytes 16318464 | tf_op jit(solution)/shard_map/pallas_call | solution.py:93
  410.3 9.1 %collective-permute-done.119.refs_2_ = bf16[512,1024]{1,0:T(8,128)(2,1)S(1)} collective-permute-done((bf16[512,1024]{1,0:T(8,128)(2,1)S(1)}, bf16[512,1024]{1,0:T(8,128)(2,1)S(1)}, u32[]{:S(2)}, u32[]{:S(2)}) %collective-permute-start.119) | collective-permute-done | bytes 1048608 | tf_op jit(solution)/shard_map/ppermute | solution.py:50
  420.3 7.7 %collective-permute-start.121 = (bf16[128,1024]{1,0:T(8,128)(2,1)S(1)}, bf16[128,1024]{1,0:T(8,128)(2,1)S(1)}, u32[]{:S(2)}, u32[]{:S(2)}) collective-permute-start(bf16[128,1024]{1,0:T(8,128)(2,1)S(1)} %get-tuple-element.321), channel_id=1, source_target_pairs={{16,0},{20,4},{24,8},{28,12},{0,16},{4,20},{8,24},{12,28},{17,1},{... | collective-permute-start | bytes 786440 | tf_op jit(solution)/shard_map/ppermute | solution.py:55
  428.2 12.7 %collective-permute-done.126.refs_2_ = bf16[512,1024]{1,0:T(8,128)(2,1)S(1)} collective-permute-done((bf16[512,1024]{1,0:T(8,128)(2,1)S(1)}, bf16[512,1024]{1,0:T(8,128)(2,1)S(1)}, u32[]{:S(2)}, u32[]{:S(2)}) %collective-permute-start.126) | collective-permute-done | bytes 1048608 | tf_op jit(solution)/shard_map/ppermute | solution.py:50
  445.6 3.7 collective-permute-done.121.refs_3_
  449.3 4.0 collective-permute-start.128
  457.3 3.3 collective-permute-start.129
  463.1 10.6 %shard_map.294 = (f32[448,1024]{1,0:T(8,128)S(1)}, bf16[448,1024]{1,0:T(8,128)(2,1)S(1)}, bf16[448,768]{1,0:T(8,128)(2,1)S(1)}, bf16[448,1024]{1,0:T(8,128)(2,1)...) custom-call(f32[448,1024]{1,0:T(8,128)S(1)} %get-tuple-element.237.refs_0_, f32[448,1024]{1,0:T(8,128)S(1)} %copy-done.8, ...), custom_call_target="tpu_custom_call" | custom-call | flops 1453326336 | bytes 13983744 | tf_op jit(solution)/shard_map/pallas_call | solution.py:93
  478.4 10.4 %shard_map.290 = (f32[448,1024]{1,0:T(8,128)S(1)}, bf16[448,1024]{1,0:T(8,128)(2,1)S(1)}, bf16[448,768]{1,0:T(8,128)(2,1)S(1)}, bf16[448,1024]{1,0:T(8,128)(2,1)...) custom-call(f32[448,1024]{1,0:T(8,128)S(1)} %get-tuple-element.223.refs_0_, f32[448,1024]{1,0:T(8,128)S(1)} %copy-done.6, ...), custom_call_target="tpu_custom_call" | custom-call | flops 1453326336 | bytes 13983744 | tf_op jit(solution)/shard_map/pallas_call | solution.py:93
  488.8 3.5 collective-permute-done.124.refs_6_
  493.3 6.0 collective-permute-done.133.refs_3_
  506.9 5.5 collective-permute-done.130.refs_9_
  513.1 22.4 %collective-permute-done.112.refs_2_ = bf16[512,768]{1,0:T(8,128)(2,1)S(1)} collective-permute-done((bf16[512,768]{1,0:T(8,128)(2,1)S(1)}, bf16[512,768]{1,0:T(8,128)(2,1)S(1)}, u32[]{:S(2)}, u32[]{:S(2)}) %collective-permute-start.112) | collective-permute-done | bytes 786464 | tf_op jit(solution)/shard_map/ppermute | solution.py:50
  540.6 3.7 collective-permute-start.113
  544.3 15.1 %collective-permute-done.134.refs_1_ = bf16[64,1024]{1,0:T(8,128)(2,1)S(1)} collective-permute-done((bf16[64,1024]{1,0:T(8,128)(2,1)S(1)}, bf16[64,1024]{1,0:T(8,128)(2,1)S(1)}, u32[]{:S(2)}, u32[]{:S(2)}) %collective-permute-start.134) | collective-permute-done | bytes 131104 | tf_op jit(solution)/shard_map/ppermute | solution.py:50
  564.9 5.9 collective-permute-done.114.refs_3_
  573.7 11.3 %collective-permute-start.98 = (bf16[128,1024]{1,0:T(8,128)(2,1)S(1)}, bf16[128,1024]{1,0:T(8,128)(2,1)S(1)}, u32[]{:S(2)}, u32[]{:S(2)}) collective-permute-start(bf16[128,1024]{1,0:T(8,128)(2,1)S(1)} %get-tuple-element.282), channel_id=1, source_target_pairs={{24,0},{28,4},{0,8},{4,12},{8,16},{12,20},{16,24},{20,28},{25,1},{... | collective-permute-start | bytes 786440 | tf_op jit(solution)/shard_map/ppermute | solution.py:55
  585.7 8.8 %collective-permute-start.103 = (bf16[128,1024]{1,0:T(8,128)(2,1)S(1)}, bf16[128,1024]{1,0:T(8,128)(2,1)S(1)}, u32[]{:S(2)}, u32[]{:S(2)}) collective-permute-start(bf16[128,1024]{1,0:T(8,128)(2,1)S(1)} %get-tuple-element.288), channel_id=1, source_target_pairs={{8,0},{12,4},{16,8},{20,12},{24,16},{28,20},{0,24},{4,28},{9,1},{1... | collective-permute-start | bytes 786440 | tf_op jit(solution)/shard_map/ppermute | solution.py:55
  597.2 7.1 %collective-permute-start.104 = (bf16[128,1024]{1,0:T(8,128)(2,1)S(1)}, bf16[128,1024]{1,0:T(8,128)(2,1)S(1)}, u32[]{:S(2)}, u32[]{:S(2)}) collective-permute-start(bf16[128,1024]{1,0:T(8,128)(2,1)S(1)} %get-tuple-element.289), channel_id=1, source_target_pairs={{16,0},{20,4},{24,8},{28,12},{0,16},{4,20},{8,24},{12,28},{17,1},{... | collective-permute-start | bytes 786440 | tf_op jit(solution)/shard_map/ppermute | solution.py:55
  607.2 8.5 %shard_map.295 = (f32[224,1024]{1,0:T(8,128)}, f32[16,1024]{1,0:T(8,128)S(1)}) custom-call(s32[4]{0:T(128)S(1)} %pad_add_fusion.refs_0_.where, bf16[448,1024]{1,0:T(8,128)(2,1)S(1)} %copy-done.22, f32[448,1024]{1,0:T(8,128)S(1)} %get-tuple-element.227.refs_2_, bf16[448,1024]{1,0:T(8,128)(2,1)S(1)} %get-tuple-element.228.refs_3_, ...), custom_call_target="tpu_custom_call" | custom-call | flops 9175040 | bytes 12058640 | tf_op jit(solution)/shard_map/pallas_call | solution.py:93
  616.5 3.9 collective-permute-done.115.refs_4_
  622.1 3.7 collective-permute-done.104.refs_2_
  625.8 4.7 collective-permute-start.108
  637.1 6.9 collective-permute-done.108.refs_2_
  651.8 6.9 collective-permute-done.90.refs_3_
  674.1 4.7 collective-permute-done.93.refs_2_
  687.7 3.2 fusion.59
  694.2 3.1 finish.3
  (671 shorter events, 213.7 us)
Async XLA Ops:
  6.7 30.6 %collective-permute-start.1 = (bf16[448,1024]{1,0:T(8,128)(2,1)S(1)}, bf16[448,1024]{1,0:T(8,128)(2,1)S(1)}, u32[]{:S(2)}, u32[]{:S(2)}) collective-permute-start(bf16[448,1024]{1,0:T(8,128)(2,1)S(1)} %pad_maximum_fusion.2.refs_1_), channel_id=1, source_target_pairs={{0,1},{1,0},{2,3},{3,2},{4,5},{5,4},{6,7},{7,6},{8,9},{9,8},{10,11... | collective-permute-start | bytes 2752520 | tf_op jit(solution)/shard_map/ppermute | solution.py:46
  18.1 48.9 %collective-permute-start = (bf16[448,1024]{1,0:T(8,128)(2,1)S(1)}, bf16[448,1024]{1,0:T(8,128)(2,1)}, u32[]{:S(2)}, u32[]{:S(2)}) collective-permute-start(bf16[448,1024]{1,0:T(8,128)(2,1)S(1)} %pad_maximum_fusion.2.refs_1_), channel_id=1, source_target_pairs={{0,2},{2,0},{1,3},{3,1},{4,6},{6,4},{5,7},{7,5},{8,10},{10,8},{9,1... | collective-permute-start | bytes 2752520 | tf_op jit(solution)/shard_map/ppermute | solution.py:42
  18.1 19.2 %collective-permute-start.8 = (bf16[144,768]{1,0:T(8,128)(2,1)S(1)}, bf16[144,768]{1,0:T(8,128)(2,1)S(1)}, u32[]{:S(2)}, u32[]{:S(2)}) collective-permute-start(bf16[144,768]{1,0:T(8,128)(2,1)S(1)} %get-tuple-element.188), channel_id=1, source_target_pairs={{24,0},{28,4},{0,8},{4,12},{8,16},{12,20},{16,24},{20,28},{25,1},{... | collective-permute-start | bytes 663560 | tf_op jit(solution)/shard_map/ppermute | solution.py:55
  18.1 19.1 %collective-permute-start.7 = (bf16[144,768]{1,0:T(8,128)(2,1)S(1)}, bf16[144,768]{1,0:T(8,128)(2,1)S(1)}, u32[]{:S(2)}, u32[]{:S(2)}) collective-permute-start(bf16[144,768]{1,0:T(8,128)(2,1)S(1)} %get-tuple-element.188), channel_id=1, source_target_pairs={{16,0},{20,4},{24,8},{28,12},{0,16},{4,20},{8,24},{12,28},{17,1},{... | collective-permute-start | bytes 663560 | tf_op jit(solution)/shard_map/ppermute | solution.py:55
  37.3 29.7 %collective-permute-start.2 = (bf16[448,1024]{1,0:T(8,128)(2,1)S(1)}, bf16[448,1024]{1,0:T(8,128)(2,1)}, u32[]{:S(2)}, u32[]{:S(2)}) collective-permute-start(bf16[448,1024]{1,0:T(8,128)(2,1)S(1)} %collective-permute-done.1.refs_3_), channel_id=1, source_target_pairs={{0,2},{2,0},{1,3},{3,1},{4,6},{6,4},{5,7},{7,5},{8,10},{10,8},{9,1... | collective-permute-start | bytes 2752520 | tf_op jit(solution)/shard_map/ppermute | solution.py:42
  37.4 22.2 %collective-permute-start.9 = (bf16[576,768]{1,0:T(8,128)(2,1)S(1)}, bf16[576,768]{1,0:T(8,128)(2,1)}, u32[]{:S(2)}, u32[]{:S(2)}) collective-permute-start(bf16[576,768]{1,0:T(8,128)(2,1)S(1)} %constant_dynamic-update-slice_fusion.refs_0_), channel_id=1, source_target_pairs={{0,4},{4,0},{8,12},{12,8},{16,20},{20,16},{24,28},{28,24},{1,5},{5... | collective-permute-start | bytes 2654216 | tf_op jit(solution)/shard_map/ppermute | solution.py:50
  51.8 27.4 %collective-permute-start.22 = (bf16[128,1024]{1,0:T(8,128)(2,1)}, bf16[128,1024]{1,0:T(8,128)(2,1)S(1)}, u32[]{:S(2)}, u32[]{:S(2)}) collective-permute-start(bf16[128,1024]{1,0:T(8,128)(2,1)} %get-tuple-element.352), channel_id=1, source_target_pairs={{24,0},{28,4},{0,8},{4,12},{8,16},{12,20},{16,24},{20,28},{25,1},{... | collective-permute-start | bytes 786440 | tf_op jit(solution)/shard_map/ppermute | solution.py:55
  54.2 27.5 %collective-permute-start.21 = (bf16[128,1024]{1,0:T(8,128)(2,1)}, bf16[128,1024]{1,0:T(8,128)(2,1)S(1)}, u32[]{:S(2)}, u32[]{:S(2)}) collective-permute-start(bf16[128,1024]{1,0:T(8,128)(2,1)} %get-tuple-element.352), channel_id=1, source_target_pairs={{16,0},{20,4},{24,8},{28,12},{0,16},{4,20},{8,24},{12,28},{17,1},{... | collective-permute-start | bytes 786440 | tf_op jit(solution)/shard_map/ppermute | solution.py:55
  59.6 22.1 %collective-permute-start.20 = (bf16[128,1024]{1,0:T(8,128)(2,1)}, bf16[128,1024]{1,0:T(8,128)(2,1)S(1)}, u32[]{:S(2)}, u32[]{:S(2)}) collective-permute-start(bf16[128,1024]{1,0:T(8,128)(2,1)} %get-tuple-element.352), channel_id=1, source_target_pairs={{8,0},{12,4},{16,8},{20,12},{24,16},{28,20},{0,24},{4,28},{9,1},{1... | collective-permute-start | bytes 786440 | tf_op jit(solution)/shard_map/ppermute | solution.py:55
  79.1 34.1 %collective-permute-start.41 = (bf16[448,1024]{1,0:T(8,128)(2,1)S(1)}, bf16[448,1024]{1,0:T(8,128)(2,1)S(1)}, u32[]{:S(2)}, u32[]{:S(2)}) collective-permute-start(bf16[448,1024]{1,0:T(8,128)(2,1)S(1)} %get-tuple-element.207.refs_1_), channel_id=1, source_target_pairs={{0,2},{2,0},{1,3},{3,1},{4,6},{6,4},{5,7},{7,5},{8,10},{10,8},{9,1... | collective-permute-start | bytes 2752520 | tf_op jit(solution)/shard_map/ppermute | solution.py:42
  79.2 23.7 %collective-permute-start.18 = (bf16[128,1024]{1,0:T(8,128)(2,1)S(1)}, bf16[128,1024]{1,0:T(8,128)(2,1)S(1)}, u32[]{:S(2)}, u32[]{:S(2)}) collective-permute-start(bf16[128,1024]{1,0:T(8,128)(2,1)S(1)} %copy-done.66), channel_id=1, source_target_pairs={{24,0},{28,4},{0,8},{4,12},{8,16},{12,20},{16,24},{20,28},{25,1},{... | collective-permute-start | bytes 786440 | tf_op jit(solution)/shard_map/ppermute | solution.py:55
  81.7 21.2 %collective-permute-start.17 = (bf16[128,1024]{1,0:T(8,128)(2,1)S(1)}, bf16[128,1024]{1,0:T(8,128)(2,1)S(1)}, u32[]{:S(2)}, u32[]{:S(2)}) collective-permute-start(bf16[128,1024]{1,0:T(8,128)(2,1)S(1)} %copy-done.66), channel_id=1, source_target_pairs={{16,0},{20,4},{24,8},{28,12},{0,16},{4,20},{8,24},{12,28},{17,1},{... | collective-permute-start | bytes 786440 | tf_op jit(solution)/shard_map/ppermute | solution.py:55
  82.8 43.6 %collective-permute-start.23 = (bf16[512,1024]{1,0:T(8,128)(2,1)S(1)}, bf16[512,1024]{1,0:T(8,128)(2,1)S(1)}, u32[]{:S(2)}, u32[]{:S(2)}) collective-permute-start(bf16[512,1024]{1,0:T(8,128)(2,1)S(1)} %pad_maximum_fusion.refs_0_), channel_id=1, source_target_pairs={{0,4},{4,0},{8,12},{12,8},{16,20},{20,16},{24,28},{28,24},{1,5},{5... | collective-permute-start | bytes 3145736 | tf_op jit(solution)/shard_map/ppermute | solution.py:50
  102.9 27.3 %collective-permute-start.19 = (bf16[512,1024]{1,0:T(8,128)(2,1)S(1)}, bf16[512,1024]{1,0:T(8,128)(2,1)S(1)}, u32[]{:S(2)}, u32[]{:S(2)}) collective-permute-start(bf16[512,1024]{1,0:T(8,128)(2,1)S(1)} %constant_dynamic-update-slice_fusion.4.refs_0_), channel_id=1, source_target_pairs={{0,4},{4,0},{8,12},{12,8},{16,20},{20,16},{24,28},{28,24},{1,5},{5... | collective-permute-start | bytes 3145736 | tf_op jit(solution)/shard_map/ppermute | solution.py:50
  140.7 19.3 %collective-permute-start.44 = (bf16[448,1024]{1,0:T(8,128)(2,1)S(1)}, bf16[448,1024]{1,0:T(8,128)(2,1)S(1)}, u32[]{:S(2)}, u32[]{:S(2)}) collective-permute-start(bf16[448,1024]{1,0:T(8,128)(2,1)S(1)} %shard_map.282.refs_1_), channel_id=1, source_target_pairs={{0,2},{2,0},{1,3},{3,1},{4,6},{6,4},{5,7},{7,5},{8,10},{10,8},{9,1... | collective-permute-start | bytes 2752520 | tf_op jit(solution)/shard_map/ppermute | solution.py:42
  159.9 23.7 %collective-permute-start.24 = (bf16[448,1024]{1,0:T(8,128)(2,1)S(1)}, bf16[448,1024]{1,0:T(8,128)(2,1)S(1)}, u32[]{:S(2)}, u32[]{:S(2)}) collective-permute-start(bf16[448,1024]{1,0:T(8,128)(2,1)S(1)} %shard_map.277.refs_1_), channel_id=1, source_target_pairs={{0,2},{2,0},{1,3},{3,1},{4,6},{6,4},{5,7},{7,5},{8,10},{10,8},{9,1... | collective-permute-start | bytes 2752520 | tf_op jit(solution)/shard_map/ppermute | solution.py:42
  164.7 35.7 %collective-permute-start.30 = (bf16[512,768]{1,0:T(8,128)(2,1)S(1)}, bf16[512,768]{1,0:T(8,128)(2,1)S(1)}, u32[]{:S(2)}, u32[]{:S(2)}) collective-permute-start(bf16[512,768]{1,0:T(8,128)(2,1)S(1)} %constant_dynamic-update-slice_fusion.8.refs_0_), channel_id=1, source_target_pairs={{0,4},{4,0},{8,12},{12,8},{16,20},{20,16},{24,28},{28,24},{1,5},{5... | collective-permute-start | bytes 2359304 | tf_op jit(solution)/shard_map/ppermute | solution.py:50
  173.1 30.1 %collective-permute-start.46 = (bf16[224,1024]{1,0:T(8,128)(2,1)S(1)}, bf16[224,1024]{1,0:T(8,128)(2,1)S(1)}, u32[]{:S(2)}, u32[]{:S(2)}) collective-permute-start(bf16[224,1024]{1,0:T(8,128)(2,1)S(1)} %collective-permute-done.45.refs_3_), channel_id=1, source_target_pairs={{0,2},{2,0},{1,3},{3,1},{4,6},{6,4},{5,7},{7,5},{8,10},{10,8},{9,1... | collective-permute-start | bytes 1376264 | tf_op jit(solution)/shard_map/ppermute | solution.py:42
  187.4 40.4 %collective-permute-start.25 = (bf16[224,1024]{1,0:T(8,128)(2,1)S(1)}, bf16[224,1024]{1,0:T(8,128)(2,1)S(1)}, u32[]{:S(2)}, u32[]{:S(2)}) collective-permute-start(bf16[224,1024]{1,0:T(8,128)(2,1)S(1)} %add_convert_fusion.15), channel_id=1, source_target_pairs={{0,1},{1,0},{2,3},{3,2},{4,5},{5,4},{6,7},{7,6},{8,9},{9,8},{10,11... | collective-permute-start | bytes 1376264 | tf_op jit(solution)/shard_map/ppermute | solution.py:46
  192.7 20.3 %collective-permute-start.52 = (bf16[128,1024]{1,0:T(8,128)(2,1)S(1)}, bf16[128,1024]{1,0:T(8,128)(2,1)S(1)}, u32[]{:S(2)}, u32[]{:S(2)}) collective-permute-start(bf16[128,1024]{1,0:T(8,128)(2,1)S(1)} %copy-done.150), channel_id=1, source_target_pairs={{24,0},{28,4},{0,8},{4,12},{8,16},{12,20},{16,24},{20,28},{25,1},{... | collective-permute-start | bytes 786440 | tf_op jit(solution)/shard_map/ppermute | solution.py:55
  195.7 20.6 %collective-permute-start.51 = (bf16[128,1024]{1,0:T(8,128)(2,1)S(1)}, bf16[128,1024]{1,0:T(8,128)(2,1)S(1)}, u32[]{:S(2)}, u32[]{:S(2)}) collective-permute-start(bf16[128,1024]{1,0:T(8,128)(2,1)S(1)} %copy-done.150), channel_id=1, source_target_pairs={{16,0},{20,4},{24,8},{28,12},{0,16},{4,20},{8,24},{12,28},{17,1},{... | collective-permute-start | bytes 786440 | tf_op jit(solution)/shard_map/ppermute | solution.py:55
  200.4 24.0 %collective-permute-start.50 = (bf16[128,1024]{1,0:T(8,128)(2,1)S(1)}, bf16[128,1024]{1,0:T(8,128)(2,1)S(1)}, u32[]{:S(2)}, u32[]{:S(2)}) collective-permute-start(bf16[128,1024]{1,0:T(8,128)(2,1)S(1)} %copy-done.150), channel_id=1, source_target_pairs={{8,0},{12,4},{16,8},{20,12},{24,16},{28,20},{0,24},{4,28},{9,1},{1... | collective-permute-start | bytes 786440 | tf_op jit(solution)/shard_map/ppermute | solution.py:55
  213.0 42.6 %collective-permute-start.47 = (bf16[448,1024]{1,0:T(8,128)(2,1)S(1)}, bf16[448,1024]{1,0:T(8,128)(2,1)S(1)}, u32[]{:S(2)}, u32[]{:S(2)}) collective-permute-start(bf16[448,1024]{1,0:T(8,128)(2,1)S(1)} %get-tuple-element.211.refs_1_), channel_id=1, source_target_pairs={{0,2},{2,0},{1,3},{3,1},{4,6},{6,4},{5,7},{7,5},{8,10},{10,8},{9,1... | collective-permute-start | bytes 2752520 | tf_op jit(solution)/shard_map/ppermute | solution.py:42
  216.3 28.0 %collective-permute-start.39 = (bf16[128,1024]{1,0:T(8,128)(2,1)S(1)}, bf16[128,1024]{1,0:T(8,128)(2,1)S(1)}, u32[]{:S(2)}, u32[]{:S(2)}) collective-permute-start(bf16[128,1024]{1,0:T(8,128)(2,1)S(1)} %copy-done.64), channel_id=1, source_target_pairs={{24,0},{28,4},{0,8},{4,12},{8,16},{12,20},{16,24},{20,28},{25,1},{... | collective-permute-start | bytes 786440 | tf_op jit(solution)/shard_map/ppermute | solution.py:55
  224.4 19.9 %collective-permute-start.38 = (bf16[128,1024]{1,0:T(8,128)(2,1)S(1)}, bf16[128,1024]{1,0:T(8,128)(2,1)S(1)}, u32[]{:S(2)}, u32[]{:S(2)}) collective-permute-start(bf16[128,1024]{1,0:T(8,128)(2,1)S(1)} %copy-done.64), channel_id=1, source_target_pairs={{16,0},{20,4},{24,8},{28,12},{0,16},{4,20},{8,24},{12,28},{17,1},{... | collective-permute-start | bytes 786440 | tf_op jit(solution)/shard_map/ppermute | solution.py:55
  227.9 40.6 %collective-permute-start.53 = (bf16[512,1024]{1,0:T(8,128)(2,1)S(1)}, bf16[512,1024]{1,0:T(8,128)(2,1)S(1)}, u32[]{:S(2)}, u32[]{:S(2)}) collective-permute-start(bf16[512,1024]{1,0:T(8,128)(2,1)S(1)} %pad_maximum_fusion.1.refs_0_), channel_id=1, source_target_pairs={{0,4},{4,0},{8,12},{12,8},{16,20},{20,16},{24,28},{28,24},{1,5},{5... | collective-permute-start | bytes 3145736 | tf_op jit(solution)/shard_map/ppermute | solution.py:50
  255.0 25.6 %collective-permute-start.40 = (bf16[512,1024]{1,0:T(8,128)(2,1)S(1)}, bf16[512,1024]{1,0:T(8,128)(2,1)S(1)}, u32[]{:S(2)}, u32[]{:S(2)}) collective-permute-start(bf16[512,1024]{1,0:T(8,128)(2,1)S(1)} %constant_dynamic-update-slice_fusion.12.refs_0_), channel_id=1, source_target_pairs={{0,4},{4,0},{8,12},{12,8},{16,20},{20,16},{24,28},{28,24},{1,5},{5... | collective-permute-start | bytes 3145736 | tf_op jit(solution)/shard_map/ppermute | solution.py:50
  269.6 23.0 %collective-permute-start.35 = (bf16[224,1024]{1,0:T(8,128)(2,1)S(1)}, bf16[224,1024]{1,0:T(8,128)(2,1)S(1)}, u32[]{:S(2)}, u32[]{:S(2)}) collective-permute-start(bf16[224,1024]{1,0:T(8,128)(2,1)S(1)} %add_convert_fusion.14), channel_id=1, source_target_pairs={{0,1},{1,0},{2,3},{3,2},{4,5},{5,4},{6,7},{7,6},{8,9},{9,8},{10,11... | collective-permute-start | bytes 1376264 | tf_op jit(solution)/shard_map/ppermute | solution.py:46
  353.1 19.1 %collective-permute-start.61 = (bf16[448,1024]{1,0:T(8,128)(2,1)}, bf16[448,1024]{1,0:T(8,128)(2,1)}, u32[]{:S(2)}, u32[]{:S(2)}) collective-permute-start(bf16[448,1024]{1,0:T(8,128)(2,1)} %get-tuple-element.221.refs_2_), channel_id=1, source_target_pairs={{0,2},{2,0},{1,3},{3,1},{4,6},{6,4},{5,7},{7,5},{8,10},{10,8},{9,1... | collective-permute-start | bytes 2752520 | tf_op jit(solution)/shard_map/ppermute | solution.py:42
  371.6 36.9 %collective-permute-start.55 = (bf16[448,1024]{1,0:T(8,128)(2,1)S(1)}, bf16[448,1024]{1,0:T(8,128)(2,1)S(1)}, u32[]{:S(2)}, u32[]{:S(2)}) collective-permute-start(bf16[448,1024]{1,0:T(8,128)(2,1)S(1)} %shard_map.286), channel_id=1, source_target_pairs={{0,2},{2,0},{1,3},{3,1},{4,6},{6,4},{5,7},{7,5},{8,10},{10,8},{9,1... | collective-permute-start | bytes 2752520 | tf_op jit(solution)/shard_map/ppermute | solution.py:42
  387.6 20.6 %collective-permute-start.76 = (bf16[448,1024]{1,0:T(8,128)(2,1)S(1)}, bf16[448,1024]{1,0:T(8,128)(2,1)S(1)}, u32[]{:S(2)}, u32[]{:S(2)}) collective-permute-start(bf16[448,1024]{1,0:T(8,128)(2,1)S(1)} %get-tuple-element.238.refs_2_), channel_id=1, source_target_pairs={{0,2},{2,0},{1,3},{3,1},{4,6},{6,4},{5,7},{7,5},{8,10},{10,8},{9,1... | collective-permute-start | bytes 2752520 | tf_op jit(solution)/shard_map/ppermute | solution.py:42
  393.3 26.1 %collective-permute-start.119 = (bf16[512,1024]{1,0:T(8,128)(2,1)S(1)}, bf16[512,1024]{1,0:T(8,128)(2,1)S(1)}, u32[]{:S(2)}, u32[]{:S(2)}) collective-permute-start(bf16[512,1024]{1,0:T(8,128)(2,1)S(1)} %bitcast.96), channel_id=1, source_target_pairs={{0,4},{4,0},{8,12},{12,8},{16,20},{20,16},{24,28},{28,24},{1,5},{5... | collective-permute-start | bytes 3145736 | tf_op jit(solution)/shard_map/ppermute | solution.py:50
  405.2 35.8 %collective-permute-start.126 = (bf16[512,1024]{1,0:T(8,128)(2,1)S(1)}, bf16[512,1024]{1,0:T(8,128)(2,1)S(1)}, u32[]{:S(2)}, u32[]{:S(2)}) collective-permute-start(bf16[512,1024]{1,0:T(8,128)(2,1)S(1)} %bitcast.95), channel_id=1, source_target_pairs={{0,4},{4,0},{8,12},{12,8},{16,20},{20,16},{24,28},{28,24},{1,5},{5... | collective-permute-start | bytes 3145736 | tf_op jit(solution)/shard_map/ppermute | solution.py:50
  408.2 19.9 %collective-permute-start.54 = (bf16[448,1024]{1,0:T(8,128)(2,1)S(1)}, bf16[448,1024]{1,0:T(8,128)(2,1)S(1)}, u32[]{:S(2)}, u32[]{:S(2)}) collective-permute-start(bf16[448,1024]{1,0:T(8,128)(2,1)S(1)} %shard_map.285), channel_id=1, source_target_pairs={{0,2},{2,0},{1,3},{3,1},{4,6},{6,4},{5,7},{7,5},{8,10},{10,8},{9,1... | collective-permute-start | bytes 2752520 | tf_op jit(solution)/shard_map/ppermute | solution.py:42
  408.5 34.0 %collective-permute-start.77 = (bf16[224,1024]{1,0:T(8,128)(2,1)S(1)}, bf16[224,1024]{1,0:T(8,128)(2,1)S(1)}, u32[]{:S(2)}, u32[]{:S(2)}) collective-permute-start(bf16[224,1024]{1,0:T(8,128)(2,1)S(1)} %add_convert_fusion.1), channel_id=1, source_target_pairs={{0,1},{1,0},{2,3},{3,2},{4,5},{5,4},{6,7},{7,6},{8,9},{9,8},{10,11... | collective-permute-start | bytes 1376264 | tf_op jit(solution)/shard_map/ppermute | solution.py:46
  420.2 24.8 %collective-permute-start.120 = (bf16[128,1024]{1,0:T(8,128)(2,1)S(1)}, bf16[128,1024]{1,0:T(8,128)(2,1)S(1)}, u32[]{:S(2)}, u32[]{:S(2)}) collective-permute-start(bf16[128,1024]{1,0:T(8,128)(2,1)S(1)} %get-tuple-element.320), channel_id=1, source_target_pairs={{8,0},{12,4},{16,8},{20,12},{24,16},{28,20},{0,24},{4,28},{9,1},{1... | collective-permute-start | bytes 786440 | tf_op jit(solution)/shard_map/ppermute | solution.py:55
  420.3 29.0 %collective-permute-start.121 = (bf16[128,1024]{1,0:T(8,128)(2,1)S(1)}, bf16[128,1024]{1,0:T(8,128)(2,1)S(1)}, u32[]{:S(2)}, u32[]{:S(2)}) collective-permute-start(bf16[128,1024]{1,0:T(8,128)(2,1)S(1)} %get-tuple-element.321), channel_id=1, source_target_pairs={{16,0},{20,4},{24,8},{28,12},{0,16},{4,20},{8,24},{12,28},{17,1},{... | collective-permute-start | bytes 786440 | tf_op jit(solution)/shard_map/ppermute | solution.py:55
  428.2 21.1 %collective-permute-start.122 = (bf16[128,1024]{1,0:T(8,128)(2,1)S(1)}, bf16[128,1024]{1,0:T(8,128)(2,1)S(1)}, u32[]{:S(2)}, u32[]{:S(2)}) collective-permute-start(bf16[128,1024]{1,0:T(8,128)(2,1)S(1)} %get-tuple-element.322), channel_id=1, source_target_pairs={{24,0},{28,4},{0,8},{4,12},{8,16},{12,20},{16,24},{20,28},{25,1},{... | collective-permute-start | bytes 786440 | tf_op jit(solution)/shard_map/ppermute | solution.py:55
  445.0 33.1 %collective-permute-start.57 = (bf16[224,1024]{1,0:T(8,128)(2,1)S(1)}, bf16[224,1024]{1,0:T(8,128)(2,1)S(1)}, u32[]{:S(2)}, u32[]{:S(2)}) collective-permute-start(bf16[224,1024]{1,0:T(8,128)(2,1)S(1)} %add_convert_fusion.9), channel_id=1, source_target_pairs={{0,1},{1,0},{2,3},{3,2},{4,5},{5,4},{6,7},{7,6},{8,9},{9,8},{10,11... | collective-permute-start | bytes 1376264 | tf_op jit(solution)/shard_map/ppermute | solution.py:46
  449.3 24.4 %collective-permute-start.127 = (bf16[128,1024]{1,0:T(8,128)(2,1)S(1)}, bf16[128,1024]{1,0:T(8,128)(2,1)S(1)}, u32[]{:S(2)}, u32[]{:S(2)}) collective-permute-start(bf16[128,1024]{1,0:T(8,128)(2,1)S(1)} %get-tuple-element.326), channel_id=1, source_target_pairs={{8,0},{12,4},{16,8},{20,12},{24,16},{28,20},{0,24},{4,28},{9,1},{1... | collective-permute-start | bytes 786440 | tf_op jit(solution)/shard_map/ppermute | solution.py:55
  449.3 27.3 %collective-permute-start.128 = (bf16[128,1024]{1,0:T(8,128)(2,1)S(1)}, bf16[128,1024]{1,0:T(8,128)(2,1)S(1)}, u32[]{:S(2)}, u32[]{:S(2)}) collective-permute-start(bf16[128,1024]{1,0:T(8,128)(2,1)S(1)} %get-tuple-element.327), channel_id=1, source_target_pairs={{16,0},{20,4},{24,8},{28,12},{0,16},{4,20},{8,24},{12,28},{17,1},{... | collective-permute-start | bytes 786440 | tf_op jit(solution)/shard_map/ppermute | solution.py:55
  457.3 20.8 %collective-permute-start.129 = (bf16[128,1024]{1,0:T(8,128)(2,1)S(1)}, bf16[128,1024]{1,0:T(8,128)(2,1)S(1)}, u32[]{:S(2)}, u32[]{:S(2)}) collective-permute-start(bf16[128,1024]{1,0:T(8,128)(2,1)S(1)} %get-tuple-element.328), channel_id=1, source_target_pairs={{24,0},{28,4},{0,8},{4,12},{8,16},{12,20},{16,24},{20,28},{25,1},{... | collective-permute-start | bytes 786440 | tf_op jit(solution)/shard_map/ppermute | solution.py:55
  473.7 27.3 %collective-permute-start.56 = (bf16[224,1024]{1,0:T(8,128)(2,1)S(1)}, bf16[224,1024]{1,0:T(8,128)(2,1)S(1)}, u32[]{:S(2)}, u32[]{:S(2)}) collective-permute-start(bf16[224,1024]{1,0:T(8,128)(2,1)S(1)} %add_convert_fusion.10), channel_id=1, source_target_pairs={{0,1},{1,0},{2,3},{3,2},{4,5},{5,4},{6,7},{7,6},{8,9},{9,8},{10,11... | collective-permute-start | bytes 1376264 | tf_op jit(solution)/shard_map/ppermute | solution.py:46
  478.1 27.2 %collective-permute-start.79 = (bf16[448,1024]{1,0:T(8,128)(2,1)S(1)}, bf16[448,1024]{1,0:T(8,128)(2,1)S(1)}, u32[]{:S(2)}, u32[]{:S(2)}) collective-permute-start(bf16[448,1024]{1,0:T(8,128)(2,1)S(1)} %get-tuple-element.242.refs_9_), channel_id=1, source_target_pairs={{0,2},{2,0},{1,3},{3,1},{4,6},{6,4},{5,7},{7,5},{8,10},{10,8},{9,1... | collective-permute-start | bytes 2752520 | tf_op jit(solution)/shard_map/ppermute | solution.py:42
  492.5 45.3 %collective-permute-start.95 = (bf16[512,1024]{1,0:T(8,128)(2,1)S(1)}, bf16[512,1024]{1,0:T(8,128)(2,1)S(1)}, u32[]{:S(2)}, u32[]{:S(2)}) collective-permute-start(bf16[512,1024]{1,0:T(8,128)(2,1)S(1)} %bitcast.93), channel_id=1, source_target_pairs={{0,4},{4,0},{8,12},{12,8},{16,20},{20,16},{24,28},{28,24},{1,5},{5... | collective-permute-start | bytes 3145736 | tf_op jit(solution)/shard_map/ppermute | solution.py:50
  493.2 42.9 %collective-permute-start.67 = (bf16[448,1024]{1,0:T(8,128)(2,1)S(1)}, bf16[448,1024]{1,0:T(8,128)(2,1)S(1)}, u32[]{:S(2)}, u32[]{:S(2)}) collective-permute-start(bf16[448,1024]{1,0:T(8,128)(2,1)S(1)} %get-tuple-element.228.refs_3_), channel_id=1, source_target_pairs={{0,2},{2,0},{1,3},{3,1},{4,6},{6,4},{5,7},{7,5},{8,10},{10,8},{9,1... | collective-permute-start | bytes 2752520 | tf_op jit(solution)/shard_map/ppermute | solution.py:42
  499.3 36.1 %collective-permute-start.112 = (bf16[512,768]{1,0:T(8,128)(2,1)S(1)}, bf16[512,768]{1,0:T(8,128)(2,1)S(1)}, u32[]{:S(2)}, u32[]{:S(2)}) collective-permute-start(bf16[512,768]{1,0:T(8,128)(2,1)S(1)} %bitcast.98), channel_id=1, source_target_pairs={{0,4},{4,0},{8,12},{12,8},{16,20},{20,16},{24,28},{28,24},{1,5},{5... | collective-permute-start | bytes 2359304 | tf_op jit(solution)/shard_map/ppermute | solution.py:50
  505.3 66.1 %collective-permute-start.102 = (bf16[512,1024]{1,0:T(8,128)(2,1)S(1)}, bf16[512,1024]{1,0:T(8,128)(2,1)S(1)}, u32[]{:S(2)}, u32[]{:S(2)}) collective-permute-start(bf16[512,1024]{1,0:T(8,128)(2,1)S(1)} %bitcast.94), channel_id=1, source_target_pairs={{0,4},{4,0},{8,12},{12,8},{16,20},{20,16},{24,28},{28,24},{1,5},{5... | collective-permute-start | bytes 3145736 | tf_op jit(solution)/shard_map/ppermute | solution.py:50
  513.1 26.9 %collective-permute-start.125 = (bf16[64,1024]{1,0:T(8,128)(2,1)S(1)}, bf16[64,1024]{1,0:T(8,128)(2,1)S(1)}, u32[]{:S(2)}, u32[]{:S(2)}) collective-permute-start(bf16[64,1024]{1,0:T(8,128)(2,1)S(1)} %slice.256), channel_id=1, source_target_pairs={{0,2},{2,0},{1,3},{3,1},{4,6},{6,4},{5,7},{7,5},{8,10},{10,8},{9,1... | collective-permute-start | bytes 393224 | tf_op jit(solution)/shard_map/ppermute | solution.py:42
  535.5 23.9 %collective-permute-start.134 = (bf16[64,1024]{1,0:T(8,128)(2,1)S(1)}, bf16[64,1024]{1,0:T(8,128)(2,1)S(1)}, u32[]{:S(2)}, u32[]{:S(2)}) collective-permute-start(bf16[64,1024]{1,0:T(8,128)(2,1)S(1)} %get-tuple-element.340), channel_id=1, source_target_pairs={{0,4},{4,0},{8,12},{12,8},{16,20},{20,16},{24,28},{28,24},{1,5},{5... | collective-permute-start | bytes 393224 | tf_op jit(solution)/shard_map/ppermute | solution.py:50
  536.1 28.7 %collective-permute-start.80 = (bf16[224,1024]{1,0:T(8,128)(2,1)S(1)}, bf16[224,1024]{1,0:T(8,128)(2,1)S(1)}, u32[]{:S(2)}, u32[]{:S(2)}) collective-permute-start(bf16[224,1024]{1,0:T(8,128)(2,1)S(1)} %add_convert_fusion), channel_id=1, source_target_pairs={{0,1},{1,0},{2,3},{3,2},{4,5},{5,4},{6,7},{7,6},{8,9},{9,8},{10,11... | collective-permute-start | bytes 1376264 | tf_op jit(solution)/shard_map/ppermute | solution.py:46
  537.9 33.6 %collective-permute-start.68 = (bf16[224,1024]{1,0:T(8,128)(2,1)S(1)}, bf16[224,1024]{1,0:T(8,128)(2,1)S(1)}, u32[]{:S(2)}, u32[]{:S(2)}) collective-permute-start(bf16[224,1024]{1,0:T(8,128)(2,1)S(1)} %add_convert_fusion.4), channel_id=1, source_target_pairs={{0,1},{1,0},{2,3},{3,2},{4,5},{5,4},{6,7},{7,6},{8,9},{9,8},{10,11... | collective-permute-start | bytes 1376264 | tf_op jit(solution)/shard_map/ppermute | solution.py:46
  540.6 22.0 %collective-permute-start.113 = (bf16[128,768]{1,0:T(8,128)(2,1)S(1)}, bf16[128,768]{1,0:T(8,128)(2,1)S(1)}, u32[]{:S(2)}, u32[]{:S(2)}) collective-permute-start(bf16[128,768]{1,0:T(8,128)(2,1)S(1)} %get-tuple-element.310), channel_id=1, source_target_pairs={{8,0},{12,4},{16,8},{20,12},{24,16},{28,20},{0,24},{4,28},{9,1},{1... | collective-permute-start | bytes 589832 | tf_op jit(solution)/shard_map/ppermute | solution.py:55
  564.8 39.5 %collective-permute-start.81 = (bf16[224,1024]{1,0:T(8,128)(2,1)S(1)}, bf16[224,1024]{1,0:T(8,128)(2,1)S(1)}, u32[]{:S(2)}, u32[]{:S(2)}) collective-permute-start(bf16[224,1024]{1,0:T(8,128)(2,1)S(1)} %collective-permute-done.80.refs_11_), channel_id=1, source_target_pairs={{0,2},{2,0},{1,3},{3,1},{4,6},{6,4},{5,7},{7,5},{8,10},{10,8},{9,1... | collective-permute-start | bytes 1376264 | tf_op jit(solution)/shard_map/ppermute | solution.py:42
  570.8 61.7 %collective-permute-start.88 = (bf16[512,768]{1,0:T(8,128)(2,1)S(1)}, bf16[512,768]{1,0:T(8,128)(2,1)S(1)}, u32[]{:S(2)}, u32[]{:S(2)}) collective-permute-start(bf16[512,768]{1,0:T(8,128)(2,1)S(1)} %bitcast.97), channel_id=1, source_target_pairs={{0,4},{4,0},{8,12},{12,8},{16,20},{20,16},{24,28},{28,24},{1,5},{5... | collective-permute-start | bytes 2359304 | tf_op jit(solution)/shard_map/ppermute | solution.py:50
  571.4 33.5 %collective-permute-start.69 = (bf16[224,1024]{1,0:T(8,128)(2,1)S(1)}, bf16[224,1024]{1,0:T(8,128)(2,1)S(1)}, u32[]{:S(2)}, u32[]{:S(2)}) collective-permute-start(bf16[224,1024]{1,0:T(8,128)(2,1)S(1)} %collective-permute-done.68.refs_5_), channel_id=1, source_target_pairs={{0,2},{2,0},{1,3},{3,1},{4,6},{6,4},{5,7},{7,5},{8,10},{10,8},{9,1... | collective-permute-start | bytes 1376264 | tf_op jit(solution)/shard_map/ppermute | solution.py:42
  573.7 23.5 %collective-permute-start.98 = (bf16[128,1024]{1,0:T(8,128)(2,1)S(1)}, bf16[128,1024]{1,0:T(8,128)(2,1)S(1)}, u32[]{:S(2)}, u32[]{:S(2)}) collective-permute-start(bf16[128,1024]{1,0:T(8,128)(2,1)S(1)} %get-tuple-element.282), channel_id=1, source_target_pairs={{24,0},{28,4},{0,8},{4,12},{8,16},{12,20},{16,24},{20,28},{25,1},{... | collective-permute-start | bytes 786440 | tf_op jit(solution)/shard_map/ppermute | solution.py:55
  585.7 34.7 %collective-permute-start.103 = (bf16[128,1024]{1,0:T(8,128)(2,1)S(1)}, bf16[128,1024]{1,0:T(8,128)(2,1)S(1)}, u32[]{:S(2)}, u32[]{:S(2)}) collective-permute-start(bf16[128,1024]{1,0:T(8,128)(2,1)S(1)} %get-tuple-element.288), channel_id=1, source_target_pairs={{8,0},{12,4},{16,8},{20,12},{24,16},{28,20},{0,24},{4,28},{9,1},{1... | collective-permute-start | bytes 786440 | tf_op jit(solution)/shard_map/ppermute | solution.py:55
  597.2 28.6 %collective-permute-start.104 = (bf16[128,1024]{1,0:T(8,128)(2,1)S(1)}, bf16[128,1024]{1,0:T(8,128)(2,1)S(1)}, u32[]{:S(2)}, u32[]{:S(2)}) collective-permute-start(bf16[128,1024]{1,0:T(8,128)(2,1)S(1)} %get-tuple-element.289), channel_id=1, source_target_pairs={{16,0},{20,4},{24,8},{28,12},{0,16},{4,20},{8,24},{12,28},{17,1},{... | collective-permute-start | bytes 786440 | tf_op jit(solution)/shard_map/ppermute | solution.py:55
  604.3 26.2 %collective-permute-start.105 = (bf16[128,1024]{1,0:T(8,128)(2,1)S(1)}, bf16[128,1024]{1,0:T(8,128)(2,1)S(1)}, u32[]{:S(2)}, u32[]{:S(2)}) collective-permute-start(bf16[128,1024]{1,0:T(8,128)(2,1)S(1)} %get-tuple-element.290), channel_id=1, source_target_pairs={{24,0},{28,4},{0,8},{4,12},{8,16},{12,20},{16,24},{20,28},{25,1},{... | collective-permute-start | bytes 786440 | tf_op jit(solution)/shard_map/ppermute | solution.py:55
  620.5 46.2 %collective-permute-start.100 = (bf16[128,1024]{1,0:T(8,128)(2,1)S(1)}, bf16[128,1024]{1,0:T(8,128)(2,1)S(1)}, u32[]{:S(2)}, u32[]{:S(2)}) collective-permute-start(bf16[128,1024]{1,0:T(8,128)(2,1)S(1)} %get-tuple-element.284), channel_id=1, source_target_pairs={{0,1},{1,0},{2,3},{3,2},{4,5},{5,4},{6,7},{7,6},{8,9},{9,8},{10,11... | collective-permute-start | bytes 786440 | tf_op jit(solution)/shard_map/ppermute | solution.py:46
  664.9 20.1 %collective-permute-start.135 = (bf16[64,1024]{1,0:T(8,128)(2,1)}, bf16[64,1024]{1,0:T(8,128)(2,1)}, u32[]{:S(2)}, u32[]{:S(2)}) collective-permute-start(bf16[64,1024]{1,0:T(8,128)(2,1)} %get-tuple-element.342), channel_id=1, source_target_pairs={{0,1},{1,0},{2,3},{3,2},{4,5},{5,4},{6,7},{7,6},{8,9},{9,8},{10,11... | collective-permute-start | bytes 393224 | tf_op jit(solution)/shard_map/ppermute | solution.py:46
  666.6 20.4 %collective-permute-start.106 = (bf16[128,1024]{1,0:T(8,128)(2,1)}, bf16[128,1024]{1,0:T(8,128)(2,1)}, u32[]{:S(2)}, u32[]{:S(2)}) collective-permute-start(bf16[128,1024]{1,0:T(8,128)(2,1)} %get-tuple-element.292), channel_id=1, source_target_pairs={{0,1},{1,0},{2,3},{3,2},{4,5},{5,4},{6,7},{7,6},{8,9},{9,8},{10,11... | collective-permute-start | bytes 786440 | tf_op jit(solution)/shard_map/ppermute | solution.py:46
  666.9 19.8 %collective-permute-start.99 = (bf16[64,1024]{1,0:T(8,128)(2,1)}, bf16[64,1024]{1,0:T(8,128)(2,1)}, u32[]{:S(2)}, u32[]{:S(2)}) collective-permute-start(bf16[64,1024]{1,0:T(8,128)(2,1)} %slice.219), channel_id=1, source_target_pairs={{0,2},{2,0},{1,3},{3,1},{4,6},{6,4},{5,7},{7,5},{8,10},{10,8},{9,1... | collective-permute-start | bytes 393224 | tf_op jit(solution)/shard_map/ppermute | solution.py:42
  (237 other events, 3161.5 us)

commit v3 on v2

--- a/solution.py
+++ b/solution.py
@@ -61,7 +61,7 @@
     return lax.dynamic_index_in_dim(array, at, axis, keepdims=False)
 
 
-TILE = 32
+TILE = 112
 COLS = 256
 VMEM_LIMIT = 20 * 1024 * 1024
 HBM = pltpu.MemorySpace.HBM
@@ -470,27 +470,17 @@
     q_theirs[2 * rows :, 0:pair] = small[...]
 
 
-def join_body(rows, flush, where, q_mine, q_side, u_mine, u_side, small, up_b, p_own, p_side, *outs):
-    q0, q1, u0, u1, p0, p1 = outs
-    c, y, x = where[0], where[1], where[2]
+def join_body(rows, flush, where, q_mine, q_side, u_mine, u_side, small, up_b, q0, q1, u0, u1):
+    c, y = where[0], where[1]
     pair = small.shape[1]
     here = pl.ds(pl.multiple_of(c * rows, rows), rows)
     there = pl.ds(pl.multiple_of((1 - c) * rows, rows), rows)
-    for layer, (q, u, p) in enumerate(((q0, u0, p0), (q1, u1, p1))):
+    for layer, (q, u) in enumerate(((q0, u0), (q1, u1))):
         at = slice(layer * rows, (layer + 1) * rows)
         q[here, :] = q_mine[at, :]
         q[there, :] = q_side[at, :]
         u[here, :] = u_mine[at, :]
         u[there, :] = u_side[at, :]
-
-        @pl.when(x == y)
-        def _():
-            p[...] = p_own[layer]
-
-        @pl.when(x != y)
-        def _():
-            p[...] = p_side[layer]
-
     low = lax.broadcasted_iota(jnp.int32, small.shape, 1) < pair // 2
     own, side = widen(small[...]), widen(q_side[2 * rows :, 0:pair])
     both = jnp.where(c == 0, jnp.where(low, own, side), jnp.where(low, side, own))
@@ -499,6 +489,19 @@
     ups = widen(up_b[...])
     ups = jnp.where(y == 0, ups[:, 0:pair], ups[:, pair : 2 * pair])
     q0[2 * rows :, pair : 2 * pair] = ups.astype(bf16)
+
+
+def choose_body(flush, where, own, side, *outs):
+    x, y = where[2], where[1]
+    for layer, out in enumerate(outs):
+
+        @pl.when(x == y)
+        def _():
+            out[...] = own[layer]
+
+        @pl.when(x != y)
+        def _():
+            out[...] = side[layer]
 
 
 def prep_body(n, heads, size, flush, where, small, vec, fix, up_b):
@@ -573,7 +576,11 @@
     )(at, *blocks)
 
 
-def gather_rows(unit, me, n, extra=0):
+def z_pair(v, bit, n):
+    return lax.ppermute(v, "fsdp", [(f, f ^ (2 * bit)) for f in range(n)])
+
+
+def gather_first(unit, me, n, extra):
     nz = n // 2
     line = [unit] + [z_from(unit, k, n) for k in range(1, nz)]
     line = jnp.concatenate(line, axis=0)
@@ -584,12 +591,26 @@
     return place([line, other], jnp.stack(at).astype(jnp.int32), n, extra)
 
 
+def along_z(unit, n):
+    pair = z_pair(unit, 1, n)
+    near = jnp.concatenate([unit, pair], axis=0)
+    return near, z_pair(near, 2, n)
+
+
+def gather_rows(unit, me, n):
+    near, far = along_z(unit, n)
+    near_x = x_swap(near, n)
+    far_x = x_swap(far, n)
+    z, x = me // 2, me % 2
+    at = [(z ^ k) * 2 + x for k in range(4)] + [(z ^ k) * 2 + 1 - x for k in range(4)]
+    at = jnp.stack(at).astype(jnp.int32)
+    return place([near, far, near_x, far_x], at, n, 0)
+
+
 def gather_line(unit, me, n):
-    nz = n // 2
-    blocks = [unit] + [z_from(unit, k, n) for k in range(1, nz)]
-    z = me // 2
-    at = jnp.stack([(z + k) % nz for k in range(nz)]).astype(jnp.int32)
-    return place(blocks, at, nz, 0)[0]
+    near, far = along_z(unit, n)
+    at = jnp.stack([(me // 2) ^ k for k in range(4)]).astype(jnp.int32)
+    return place([near, far], at, 4, 0)[0]
 
 
 def split_body(nz, flush, where, *refs):
@@ -630,7 +651,10 @@
 
 def rows_body(rows, flush, where, *refs):
     mine, sent, total = refs[-3:]
-    total[...] = total_of(refs[:-3])
+    value = refs[0][...]
+    for ref in refs[1:-3]:
+        value = value + widen(ref[ref.shape[0] - 2 * rows :, :])
+    total[...] = value
     c = where[0]
     mine[...] = total[pl.ds(pl.multiple_of(c * rows, rows), rows), :]
     sent[0:rows, :] = mine[...].astype(bf16)
@@ -884,20 +908,24 @@
             smem=1,
         )
         q_side, u_side = core_swap(q_theirs), core_swap(u_theirs)
-        p_side = x_swap(proj_weight, n)
         outs = [((2 * rows + 16, wide), bf16), ((2 * rows, wide), bf16)]
-        outs = outs + [((2 * rows, hidden // 4), bf16)] * 2 + [((rows, width), bf16)] * 2
-        q0, q1, u0, u1, p0, p1 = call(
+        outs = outs + [((2 * rows, hidden // 4), bf16)] * 2
+        q0, q1, u0, u1 = call(
             functools.partial(join_body, rows),
             outs,
-            [where, q_mine, q_side, u_mine, u_side, small, up_b_rows, proj_weight, p_side],
+            [where, q_mine, q_side, u_mine, u_side, small, up_b_rows],
             0,
             smem=1,
         )
+        p_side = x_swap(proj_weight, n)
+        p0, p1 = call(
+            choose_body, [((rows, width), bf16)] * 2, [where, proj_weight, p_side], 0, smem=1
+        )
         for layer, (q, u, p) in enumerate(((q0, u0, p0), (q1, u1, p1))):
-            extra = 16 if layer == 0 else 0
-            got = gather_rows(q, f, n, extra)
-            if extra:
+            if layer:
+                got = gather_rows(q, f, n)
+            else:
+                got = gather_first(q, f, n, 16)
                 shapes = [((16, width), f32), ((2 * LAYERS, wide), f32), ((16, hidden // 4), f32)]
                 vec, fix, up_b = call(
                     functools.partial(prep_body, n, heads, size), shapes, [where, got[1]], 0, smem=1
@@ -1040,7 +1068,8 @@
             g_qkv, g_proj, g_up, g_down = grads[layer]
             d = both_types(scatter(g_down, where, f, n))
             d = (d[0], y_swap(d[1]))
-            u = to_rows(scatter(g_up, where, f, n), where)
+            u = scatter(g_up, where, f, n)
+            u = to_rows(u, where)
             q = to_rows(scatter(g_qkv, where, f, n), where)
             p = both_types(scatter(g_proj, where, f, n, True))
             side = x_swap(p[1], n)

time: 705 us -> 746 us (1.058)
  waiting for transfers between devices: 276 us -> 373 us
  Pallas kernels: 181 us -> 152 us
  starting transfers between devices: 166 us -> 142 us
    ppermute x0 -> x14, waiting for transfers between devices: none -> 126 us  [z_pair(): return lax.ppermute(v, 'fsdp', [(f, f ^ 2 * bit) for f in range(n)])]
    ppermute x16 -> x21, waiting for transfers between devices: 76.7 us -> 133 us  [x_swap(): return lax.ppermute(v, 'fsdp', [(f, f ^ 1) for f in range(n)])]
    ppermute x51 -> x30, waiting for transfers between devices: 119 us -> 63 us  [z_from(): lax.ppermute(v, 'fsdp', [((z + k) % nz * 2 + x, z * 2 + x) for z in range...]
    ppermute x51 -> x30, starting transfers between devices: 118 us -> 64.9 us  [z_from(): lax.ppermute(v, 'fsdp', [((z + k) % nz * 2 + x, z * 2 + x) for z in range...]
    ppermute x26, waiting for transfers between devices: 72.7 us -> 42.1 us  [y_swap(): return lax.ppermute(v, 'replica', PAIR)]
    pallas_call x45 -> x46, Pallas kernels: 162 us -> 133 us  [call(): pl.pallas_call(run, out_shape=shapes, in_specs=[pl.BlockSpec(memory_space...]
    ppermute x0 -> x14, starting transfers between devices: none -> 16.1 us  [z_pair(): return lax.ppermute(v, 'fsdp', [(f, f ^ 2 * bit) for f in range(n)])]
    ppermute x16 -> x21, starting transfers between devices: 17 us -> 25.5 us  [x_swap(): return lax.ppermute(v, 'fsdp', [(f, f ^ 1) for f in range(n)])]
  transfers between devices with their start and end apart: 136 -> 134, of which waited for: 44 -> 43; matrix products, arithmetic and copies ran while one was open for 5% -> 4% of each run, Pallas kernels for 26% -> 19%
where the time goes in v3:
time: 746 us; the launch traced here: 742 us
  waiting for transfers between devices  373 us (50%)
  Pallas kernels  152 us (20%)
  starting transfers between devices  142 us (19%)
  local copies, waits for them, and re-layouts  44.8 us (6%)
  matrix products  14.8 us (2%)
  other arithmetic  11 us (1%)
    ppermute x21, waiting for transfers between devices, x_swap(): return lax.ppermute(v, 'fsdp', [(f, f ^ 1) for f in range(n)])  133 us
    pallas_call x46, Pallas kernels, call(): pl.pallas_call(run, out_shape=shapes, in_specs=[pl.BlockSpec(memory_space...  133 us
    ppermute x14, waiting for transfers between devices, z_pair(): return lax.ppermute(v, 'fsdp', [(f, f ^ 2 * bit) for f in range(n)])  126 us
    ppermute x30, starting transfers between devices, z_from(): lax.ppermute(v, 'fsdp', [((z + k) % nz * 2 + x, z * 2 + x) for z in range...  64.9 us
    ppermute x30, waiting for transfers between devices, z_from(): lax.ppermute(v, 'fsdp', [((z + k) % nz * 2 + x, z * 2 + x) for z in range...  63 us
    ppermute x26, waiting for transfers between devices, y_swap(): return lax.ppermute(v, 'replica', PAIR)  42.1 us
    unnamed x375, local copies, waits for them, and re-layouts  38.6 us
    ppermute x26, starting transfers between devices, y_swap(): return lax.ppermute(v, 'replica', PAIR)  29.9 us
  transfers between devices with their start and end apart: 134, of which 43 were waited for; matrix products, arithmetic and copies ran while one was open for 4% of the time, Pallas kernels for 19%

profile of v3, /device:TPU:0, one launch (start us, length us, event | category | flops | bytes accessed | tf_op | source)
XLA Modules:
  0.0 742.3 jit_solution(11306197100879475950)
XLA Ops:
  12.6 3.7 collective-permute-start.5
  17.2 4.8 collective-permute-done.5
  22.1 13.2 %collective-permute-done.6 = bf16[144,768]{1,0:T(8,128)(2,1)S(1)} collective-permute-done((bf16[144,768]{1,0:T(8,128)(2,1)S(1)}, bf16[144,768]{1,0:T(8,128)(2,1)S(1)}, u32[]{:S(2)}, u32[]{:S(2)}) %collective-permute-start.6) | collective-permute-done | bytes 221216 | tf_op jit(solution)/shard_map/ppermute | solution.py:55
  37.6 25.6 %collective-permute-done.9.refs_2_ = bf16[2,64,1024]{2,1,0:T(8,128)(2,1)S(1)} collective-permute-done((bf16[2,64,1024]{2,1,0:T(8,128)(2,1)S(1)}, bf16[2,64,1024]{2,1,0:T(8,128)(2,1)S(1)}, u32[]{:S(2)}, u32[]{:S(2)}) %collective-permute-start.9) | collective-permute-done | bytes 262176 | tf_op jit(solution)/shard_map/ppermute | solution.py:50
  64.3 4.5 collective-permute-done.10
  71.2 11.2 %collective-permute-done.11.refs_1_ = bf16[128,1024]{1,0:T(8,128)(2,1)S(1)} collective-permute-done((bf16[128,1024]{1,0:T(8,128)(2,1)S(1)}, bf16[128,1024]{1,0:T(8,128)(2,1)S(1)}, u32[]{:S(2)}, u32[]{:S(2)}) %collective-permute-start.11) | collective-permute-done | bytes 262176 | tf_op jit(solution)/shard_map/ppermute | solution.py:580
  89.6 3.5 shard_map.271
  94.1 6.6 shard_map.281
  106.8 6.6 shard_map.276
  116.5 4.6 collective-permute-done.15
  123.7 29.0 %collective-permute-done.20.refs_1_ = bf16[256,1024]{1,0:T(8,128)(2,1)S(1)} collective-permute-done((bf16[256,1024]{1,0:T(8,128)(2,1)S(1)}, bf16[256,1024]{1,0:T(8,128)(2,1)S(1)}, u32[]{:S(2)}, u32[]{:S(2)}) %collective-permute-start.20) | collective-permute-done | bytes 524320 | tf_op jit(solution)/shard_map/ppermute | solution.py:580
  154.2 9.3 %collective-permute-done.16.refs_1_ = bf16[256,1024]{1,0:T(8,128)(2,1)S(1)} collective-permute-done((bf16[256,1024]{1,0:T(8,128)(2,1)S(1)}, bf16[256,1024]{1,0:T(8,128)(2,1)S(1)}, u32[]{:S(2)}, u32[]{:S(2)}) %collective-permute-start.16) | collective-permute-done | bytes 524320 | tf_op jit(solution)/shard_map/ppermute | solution.py:580
  169.4 8.9 %collective-permute-done.17.refs_2_ = bf16[256,1024]{1,0:T(8,128)(2,1)} collective-permute-done((bf16[256,1024]{1,0:T(8,128)(2,1)S(1)}, bf16[256,1024]{1,0:T(8,128)(2,1)}, u32[]{:S(2)}, u32[]{:S(2)}) %collective-permute-start.17) | collective-permute-done | bytes 524320 | tf_op jit(solution)/shard_map/ppermute | solution.py:50
  178.4 9.9 %collective-permute-done.18.refs_3_ = bf16[256,1024]{1,0:T(8,128)(2,1)} collective-permute-done((bf16[256,1024]{1,0:T(8,128)(2,1)S(1)}, bf16[256,1024]{1,0:T(8,128)(2,1)}, u32[]{:S(2)}, u32[]{:S(2)}) %collective-permute-start.18) | collective-permute-done | bytes 524320 | tf_op jit(solution)/shard_map/ppermute | solution.py:50
  189.8 5.4 shard_map.282
  201.1 5.2 shard_map.277
  215.6 15.1 %collective-permute-done.27.refs_1_ = bf16[256,768]{1,0:T(8,128)(2,1)S(1)} collective-permute-done((bf16[256,768]{1,0:T(8,128)(2,1)S(1)}, bf16[256,768]{1,0:T(8,128)(2,1)S(1)}, u32[]{:S(2)}, u32[]{:S(2)}) %collective-permute-start.27) | collective-permute-done | bytes 393248 | tf_op jit(solution)/shard_map/ppermute | solution.py:580
  234.1 12.9 %collective-permute-done.31.refs_1_ = bf16[128,1024]{1,0:T(8,128)(2,1)S(1)} collective-permute-done((bf16[128,1024]{1,0:T(8,128)(2,1)S(1)}, bf16[128,1024]{1,0:T(8,128)(2,1)S(1)}, u32[]{:S(2)}, u32[]{:S(2)}) %collective-permute-start.31) | collective-permute-done | bytes 262176 | tf_op jit(solution)/shard_map/ppermute | solution.py:580
  251.1 6.9 shard_map.284
  261.9 7.0 collective-permute-done.48
  269.9 6.9 shard_map.279
  282.2 25.4 %collective-permute-done.49.refs_1_ = bf16[256,1024]{1,0:T(8,128)(2,1)S(1)} collective-permute-done((bf16[256,1024]{1,0:T(8,128)(2,1)S(1)}, bf16[256,1024]{1,0:T(8,128)(2,1)S(1)}, u32[]{:S(2)}, u32[]{:S(2)}) %collective-permute-start.49) | collective-permute-done | bytes 524320 | tf_op jit(solution)/shard_map/ppermute | solution.py:580
  309.6 7.2 collective-permute-done.36.refs_1_
  318.3 4.1 collective-permute-done.51.refs_3_
  325.1 8.6 %collective-permute-done.37.refs_2_ = bf16[256,1024]{1,0:T(8,128)(2,1)S(1)} collective-permute-done((bf16[256,1024]{1,0:T(8,128)(2,1)S(1)}, bf16[256,1024]{1,0:T(8,128)(2,1)S(1)}, u32[]{:S(2)}, u32[]{:S(2)}) %collective-permute-start.37) | collective-permute-done | bytes 524320 | tf_op jit(solution)/shard_map/ppermute | solution.py:50
  333.6 6.9 collective-permute-done.38.refs_3_
  341.4 4.2 shard_map.285
  345.6 3.9 shard_map.292
  354.3 4.4 shard_map.280
  358.8 4.0 shard_map.288
  364.7 11.3 %collective-permute-done.69.refs_4_ = bf16[224,1024]{1,0:T(8,128)(2,1)S(1)} collective-permute-done((bf16[224,1024]{1,0:T(8,128)(2,1)S(1)}, bf16[224,1024]{1,0:T(8,128)(2,1)S(1)}, u32[]{:S(2)}, u32[]{:S(2)}) %collective-permute-start.69) | collective-permute-done | bytes 458784 | tf_op jit(solution)/shard_map/ppermute | solution.py:46
  377.8 8.2 %shard_map.293 = (f32[448,1024]{1,0:T(8,128)S(1)}, bf16[448,1024]{1,0:T(8,128)(2,1)S(1)}, bf16[448,768]{1,0:T(8,128)(2,1)S(1)}, bf16[448,1024]{1,0:T(8,128)(2,1)...) custom-call(bf16[448,1024]{1,0:T(8,128)(2,1)S(1)} %copy-done.49, f32[448,1024]{1,0:T(8,128)S(1)} %get-tuple-element.212.refs_1_, ...), custom_call_target="tpu_custom_call" | custom-call | flops 1453326336 | bytes 13066240 | tf_op jit(solution)/shard_map/pallas_call | solution.py:93
  391.1 9.5 %shard_map.289 = (f32[448,1024]{1,0:T(8,128)S(1)}, bf16[448,1024]{1,0:T(8,128)(2,1)S(1)}, bf16[448,768]{1,0:T(8,128)(2,1)S(1)}, bf16[448,1024]{1,0:T(8,128)(2,1)...) custom-call(bf16[448,1024]{1,0:T(8,128)(2,1)S(1)} %copy-done.46, f32[448,1024]{1,0:T(8,128)S(1)} %get-tuple-element.205.refs_1_, ...), custom_call_target="tpu_custom_call" | custom-call | flops 1453326336 | bytes 13066240 | tf_op jit(solution)/shard_map/pallas_call | solution.py:93
  406.3 11.3 %collective-permute-done.72.refs_4_ = bf16[224,1024]{1,0:T(8,128)(2,1)S(1)} collective-permute-done((bf16[224,1024]{1,0:T(8,128)(2,1)S(1)}, bf16[224,1024]{1,0:T(8,128)(2,1)S(1)}, u32[]{:S(2)}, u32[]{:S(2)}) %collective-permute-start.72) | collective-permute-done | bytes 458784 | tf_op jit(solution)/shard_map/ppermute | solution.py:46
  429.4 7.3 shard_map.294
  444.3 7.6 %shard_map.290 = (f32[448,1024]{1,0:T(8,128)S(1)}, bf16[448,1024]{1,0:T(8,128)(2,1)S(1)}, bf16[448,1024]{1,0:T(8,128)(2,1)S(1)}, bf16[448,1024]{1,0:T(8,128)(2,1...) custom-call(f32[448,1024]{1,0:T(8,128)S(1)} %copy-done.12, f32[448,1024]{1,0:T(8,128)S(1)} %copy-done.40, ...), custom_call_target="tpu_custom_call" | custom-call | flops 1879048192 | bytes 16318464 | tf_op jit(solution)/shard_map/pallas_call | solution.py:93
  456.3 12.2 %collective-permute-done.117.refs_2_ = bf16[512,1024]{1,0:T(8,128)(2,1)S(1)} collective-permute-done((bf16[512,1024]{1,0:T(8,128)(2,1)S(1)}, bf16[512,1024]{1,0:T(8,128)(2,1)S(1)}, u32[]{:S(2)}, u32[]{:S(2)}) %collective-permute-start.117) | collective-permute-done | bytes 1048608 | tf_op jit(solution)/shard_map/ppermute | solution.py:50
  471.8 18.3 %collective-permute-done.124.refs_2_ = bf16[512,1024]{1,0:T(8,128)(2,1)S(1)} collective-permute-done((bf16[512,1024]{1,0:T(8,128)(2,1)S(1)}, bf16[512,1024]{1,0:T(8,128)(2,1)S(1)}, u32[]{:S(2)}, u32[]{:S(2)}) %collective-permute-start.124) | collective-permute-done | bytes 1048608 | tf_op jit(solution)/shard_map/ppermute | solution.py:50
  500.1 3.4 collective-permute-done.63.refs_4_
  506.0 8.2 %shard_map.295 = (f32[448,1024]{1,0:T(8,128)S(1)}, bf16[448,1024]{1,0:T(8,128)(2,1)S(1)}, bf16[448,768]{1,0:T(8,128)(2,1)S(1)}, bf16[448,1024]{1,0:T(8,128)(2,1)...) custom-call(f32[448,1024]{1,0:T(8,128)S(1)} %get-tuple-element.237.refs_0_, f32[448,1024]{1,0:T(8,128)S(1)} %copy-done.8, ...), custom_call_target="tpu_custom_call" | custom-call | flops 1453326336 | bytes 13983744 | tf_op jit(solution)/shard_map/pallas_call | solution.py:93
  514.8 3.2 collective-permute-done.126.refs_2_
  521.9 8.2 %shard_map.291 = (f32[448,1024]{1,0:T(8,128)S(1)}, bf16[448,1024]{1,0:T(8,128)(2,1)S(1)}, bf16[448,768]{1,0:T(8,128)(2,1)S(1)}, bf16[448,1024]{1,0:T(8,128)(2,1)...) custom-call(f32[448,1024]{1,0:T(8,128)S(1)} %get-tuple-element.223.refs_0_, f32[448,1024]{1,0:T(8,128)S(1)} %copy-done.6, ...), custom_call_target="tpu_custom_call" | custom-call | flops 1453326336 | bytes 13983744 | tf_op jit(solution)/shard_map/pallas_call | solution.py:93
  534.8 5.1 collective-permute-done.131.refs_3_
  546.5 7.6 %collective-permute-done.128.refs_9_ = bf16[128,1024]{1,0:T(8,128)(2,1)S(1)} collective-permute-done((bf16[128,1024]{1,0:T(8,128)(2,1)S(1)}, bf16[128,1024]{1,0:T(8,128)(2,1)S(1)}, u32[]{:S(2)}, u32[]{:S(2)}) %collective-permute-start.128) | collective-permute-done | bytes 262176 | tf_op jit(solution)/shard_map/ppermute | solution.py:46
  554.8 21.1 %collective-permute-done.110.refs_2_ = bf16[512,768]{1,0:T(8,128)(2,1)S(1)} collective-permute-done((bf16[512,768]{1,0:T(8,128)(2,1)S(1)}, bf16[512,768]{1,0:T(8,128)(2,1)S(1)}, u32[]{:S(2)}, u32[]{:S(2)}) %collective-permute-start.110) | collective-permute-done | bytes 786464 | tf_op jit(solution)/shard_map/ppermute | solution.py:50
  582.1 3.7 collective-permute-start.111
  585.8 13.9 %collective-permute-done.132.refs_1_ = bf16[64,1024]{1,0:T(8,128)(2,1)S(1)} collective-permute-done((bf16[64,1024]{1,0:T(8,128)(2,1)S(1)}, bf16[64,1024]{1,0:T(8,128)(2,1)S(1)}, u32[]{:S(2)}, u32[]{:S(2)}) %collective-permute-start.132) | collective-permute-done | bytes 131104 | tf_op jit(solution)/shard_map/ppermute | solution.py:50
  599.7 4.1 collective-permute-start.112
  606.3 5.6 collective-permute-done.112.refs_3_
  615.6 12.4 %collective-permute-start.96 = (bf16[128,1024]{1,0:T(8,128)(2,1)S(1)}, bf16[128,1024]{1,0:T(8,128)(2,1)S(1)}, u32[]{:S(2)}, u32[]{:S(2)}) collective-permute-start(bf16[128,1024]{1,0:T(8,128)(2,1)S(1)} %get-tuple-element.282), channel_id=1, source_target_pairs={{24,0},{28,4},{0,8},{4,12},{8,16},{12,20},{16,24},{20,28},{25,1},{... | collective-permute-start | bytes 786440 | tf_op jit(solution)/shard_map/ppermute | solution.py:55
  628.8 8.5 %collective-permute-start.101 = (bf16[128,1024]{1,0:T(8,128)(2,1)S(1)}, bf16[128,1024]{1,0:T(8,128)(2,1)S(1)}, u32[]{:S(2)}, u32[]{:S(2)}) collective-permute-start(bf16[128,1024]{1,0:T(8,128)(2,1)S(1)} %get-tuple-element.288), channel_id=1, source_target_pairs={{8,0},{12,4},{16,8},{20,12},{24,16},{28,20},{0,24},{4,28},{9,1},{1... | collective-permute-start | bytes 786440 | tf_op jit(solution)/shard_map/ppermute | solution.py:55
  640.0 7.1 collective-permute-start.102
  650.3 4.5 shard_map.296
  655.7 7.7 %collective-permute-done.113.refs_4_ = bf16[128,768]{1,0:T(8,128)(2,1)S(1)} collective-permute-done((bf16[128,768]{1,0:T(8,128)(2,1)S(1)}, bf16[128,768]{1,0:T(8,128)(2,1)S(1)}, u32[]{:S(2)}, u32[]{:S(2)}) %collective-permute-start.113) | collective-permute-done | bytes 196640 | tf_op jit(solution)/shard_map/ppermute | solution.py:55
  665.5 3.1 collective-permute-done.102.refs_2_
  668.7 5.4 collective-permute-start.106
  679.4 8.3 %collective-permute-done.106.refs_2_ = bf16[64,1024]{1,0:T(8,128)(2,1)S(1)} collective-permute-done((bf16[64,1024]{1,0:T(8,128)(2,1)S(1)}, bf16[64,1024]{1,0:T(8,128)(2,1)S(1)}, u32[]{:S(2)}, u32[]{:S(2)}) %collective-permute-start.106) | collective-permute-done | bytes 131104 | tf_op jit(solution)/shard_map/ppermute | solution.py:55
  687.7 3.1 collective-permute-start.89
  694.4 7.9 %collective-permute-done.88.refs_3_ = bf16[128,768]{1,0:T(8,128)(2,1)S(1)} collective-permute-done((bf16[128,768]{1,0:T(8,128)(2,1)S(1)}, bf16[128,768]{1,0:T(8,128)(2,1)S(1)}, u32[]{:S(2)}, u32[]{:S(2)}) %collective-permute-start.88) | collective-permute-done | bytes 196640 | tf_op jit(solution)/shard_map/ppermute | solution.py:55
  712.3 3.9 collective-permute-done.108.refs_1_
  717.6 4.7 collective-permute-done.91.refs_2_
  731.1 3.2 fusion.59
  734.4 3.1 finish.2
  737.6 3.1 finish.3
  (703 shorter events, 212.6 us)
Async XLA Ops:
  3.7 31.6 %collective-permute-start.1 = (bf16[448,1024]{1,0:T(8,128)(2,1)S(1)}, bf16[448,1024]{1,0:T(8,128)(2,1)}, u32[]{:S(2)}, u32[]{:S(2)}) collective-permute-start(bf16[448,1024]{1,0:T(8,128)(2,1)S(1)} %pad_maximum_fusion.refs_1_), channel_id=1, source_target_pairs={{0,1},{1,0},{2,3},{3,2},{4,5},{5,4},{6,7},{7,6},{8,9},{9,8},{10,11... | collective-permute-start | bytes 2752520 | tf_op jit(solution)/shard_map/ppermute | solution.py:46
  16.2 73.4 %collective-permute-start = (bf16[448,1024]{1,0:T(8,128)(2,1)S(1)}, bf16[448,1024]{1,0:T(8,128)(2,1)}, u32[]{:S(2)}, u32[]{:S(2)}) collective-permute-start(bf16[448,1024]{1,0:T(8,128)(2,1)S(1)} %pad_maximum_fusion.refs_1_), channel_id=1, source_target_pairs={{0,2},{2,0},{1,3},{3,1},{4,6},{6,4},{5,7},{7,5},{8,10},{10,8},{9,1... | collective-permute-start | bytes 2752520 | tf_op jit(solution)/shard_map/ppermute | solution.py:42
  16.2 19.2 %collective-permute-start.7 = (bf16[144,768]{1,0:T(8,128)(2,1)S(1)}, bf16[144,768]{1,0:T(8,128)(2,1)S(1)}, u32[]{:S(2)}, u32[]{:S(2)}) collective-permute-start(bf16[144,768]{1,0:T(8,128)(2,1)S(1)} %get-tuple-element.188), channel_id=1, source_target_pairs={{24,0},{28,4},{0,8},{4,12},{8,16},{12,20},{16,24},{20,28},{25,1},{... | collective-permute-start | bytes 663560 | tf_op jit(solution)/shard_map/ppermute | solution.py:55
  16.2 19.1 %collective-permute-start.6 = (bf16[144,768]{1,0:T(8,128)(2,1)S(1)}, bf16[144,768]{1,0:T(8,128)(2,1)S(1)}, u32[]{:S(2)}, u32[]{:S(2)}) collective-permute-start(bf16[144,768]{1,0:T(8,128)(2,1)S(1)} %get-tuple-element.188), channel_id=1, source_target_pairs={{16,0},{20,4},{24,8},{28,12},{0,16},{4,20},{8,24},{12,28},{17,1},{... | collective-permute-start | bytes 663560 | tf_op jit(solution)/shard_map/ppermute | solution.py:55
  35.3 54.3 %collective-permute-start.2 = (bf16[448,1024]{1,0:T(8,128)(2,1)}, bf16[448,1024]{1,0:T(8,128)(2,1)}, u32[]{:S(2)}, u32[]{:S(2)}) collective-permute-start(bf16[448,1024]{1,0:T(8,128)(2,1)} %collective-permute-done.1.refs_3_), channel_id=1, source_target_pairs={{0,2},{2,0},{1,3},{3,1},{4,6},{6,4},{5,7},{7,5},{8,10},{10,8},{9,1... | collective-permute-start | bytes 2752520 | tf_op jit(solution)/shard_map/ppermute | solution.py:42
  35.5 50.5 %collective-permute-start.8 = (bf16[576,768]{1,0:T(8,128)(2,1)S(1)}, bf16[576,768]{1,0:T(8,128)(2,1)S(1)}, u32[]{:S(2)}, u32[]{:S(2)}) collective-permute-start(bf16[576,768]{1,0:T(8,128)(2,1)S(1)} %constant_dynamic-update-slice_fusion.refs_0_), channel_id=1, source_target_pairs={{0,4},{4,0},{8,12},{12,8},{16,20},{20,16},{24,28},{28,24},{1,5},{5... | collective-permute-start | bytes 2654216 | tf_op jit(solution)/shard_map/ppermute | solution.py:50
  37.0 26.2 %collective-permute-start.9 = (bf16[2,64,1024]{2,1,0:T(8,128)(2,1)S(1)}, bf16[2,64,1024]{2,1,0:T(8,128)(2,1)S(1)}, u32[]{:S(2)}, u32[]{:S(2)}) collective-permute-start(bf16[2,64,1024]{2,1,0:T(8,128)(2,1)S(1)} %copy-done.79), channel_id=1, source_target_pairs={{0,4},{4,0},{8,12},{12,8},{16,20},{20,16},{24,28},{28,24},{1,5},{5... | collective-permute-start | bytes 786440 | tf_op jit(solution)/shard_map/ppermute | solution.py:50
  114.3 50.6 %collective-permute-start.12 = (bf16[448,1024]{1,0:T(8,128)(2,1)S(1)}, bf16[448,1024]{1,0:T(8,128)(2,1)S(1)}, u32[]{:S(2)}, u32[]{:S(2)}) collective-permute-start(bf16[448,1024]{1,0:T(8,128)(2,1)S(1)} %get-tuple-element.194.refs_1_), channel_id=1, source_target_pairs={{0,2},{2,0},{1,3},{3,1},{4,6},{6,4},{5,7},{7,5},{8,10},{10,8},{9,1... | collective-permute-start | bytes 2752520 | tf_op jit(solution)/shard_map/ppermute | solution.py:42
  114.4 38.3 %collective-permute-start.20 = (bf16[256,1024]{1,0:T(8,128)(2,1)S(1)}, bf16[256,1024]{1,0:T(8,128)(2,1)S(1)}, u32[]{:S(2)}, u32[]{:S(2)}) collective-permute-start(bf16[256,1024]{1,0:T(8,128)(2,1)S(1)} %pad_maximum_fusion.1.refs_0_), channel_id=1, source_target_pairs={{0,16},{4,20},{8,24},{12,28},{16,0},{20,4},{24,8},{28,12},{1,17},{... | collective-permute-start | bytes 1572872 | tf_op jit(solution)/shard_map/ppermute | solution.py:580
  121.2 42.3 %collective-permute-start.16 = (bf16[256,1024]{1,0:T(8,128)(2,1)S(1)}, bf16[256,1024]{1,0:T(8,128)(2,1)S(1)}, u32[]{:S(2)}, u32[]{:S(2)}) collective-permute-start(bf16[256,1024]{1,0:T(8,128)(2,1)S(1)} %constant_dynamic-update-slice_fusion.6.refs_0_), channel_id=1, source_target_pairs={{0,16},{4,20},{8,24},{12,28},{16,0},{20,4},{24,8},{28,12},{1,17},{... | collective-permute-start | bytes 1572872 | tf_op jit(solution)/shard_map/ppermute | solution.py:580
  121.7 44.6 %collective-permute-start.40 = (bf16[224,1024]{1,0:T(8,128)(2,1)S(1)}, bf16[224,1024]{1,0:T(8,128)(2,1)}, u32[]{:S(2)}, u32[]{:S(2)}) collective-permute-start(bf16[224,1024]{1,0:T(8,128)(2,1)S(1)} %add_convert_fusion.13), channel_id=1, source_target_pairs={{0,1},{1,0},{2,3},{3,2},{4,5},{5,4},{6,7},{7,6},{8,9},{9,8},{10,11... | collective-permute-start | bytes 1376264 | tf_op jit(solution)/shard_map/ppermute | solution.py:46
  122.2 45.0 %collective-permute-start.21 = (bf16[256,1024]{1,0:T(8,128)(2,1)S(1)}, bf16[256,1024]{1,0:T(8,128)(2,1)S(1)}, u32[]{:S(2)}, u32[]{:S(2)}) collective-permute-start(bf16[256,1024]{1,0:T(8,128)(2,1)S(1)} %pad_maximum_fusion.1.refs_0_), channel_id=1, source_target_pairs={{0,4},{4,0},{8,12},{12,8},{16,20},{20,16},{24,28},{28,24},{1,5},{5... | collective-permute-start | bytes 1572872 | tf_op jit(solution)/shard_map/ppermute | solution.py:50
  165.0 23.3 %collective-permute-start.18 = (bf16[256,1024]{1,0:T(8,128)(2,1)S(1)}, bf16[256,1024]{1,0:T(8,128)(2,1)}, u32[]{:S(2)}, u32[]{:S(2)}) collective-permute-start(bf16[256,1024]{1,0:T(8,128)(2,1)S(1)} %collective-permute-done.16.refs_1_), channel_id=1, source_target_pairs={{0,4},{4,0},{8,12},{12,8},{16,20},{20,16},{24,28},{28,24},{1,5},{5... | collective-permute-start | bytes 1572872 | tf_op jit(solution)/shard_map/ppermute | solution.py:50
  166.3 23.5 %collective-permute-start.41 = (bf16[224,1024]{1,0:T(8,128)(2,1)}, bf16[224,1024]{1,0:T(8,128)(2,1)}, u32[]{:S(2)}, u32[]{:S(2)}) collective-permute-start(bf16[224,1024]{1,0:T(8,128)(2,1)} %collective-permute-done.40.refs_3_), channel_id=1, source_target_pairs={{0,2},{2,0},{1,3},{3,1},{4,6},{6,4},{5,7},{7,5},{8,10},{10,8},{9,1... | collective-permute-start | bytes 1376264 | tf_op jit(solution)/shard_map/ppermute | solution.py:42
  167.3 30.7 %collective-permute-start.13 = (bf16[224,1024]{1,0:T(8,128)(2,1)}, bf16[224,1024]{1,0:T(8,128)(2,1)}, u32[]{:S(2)}, u32[]{:S(2)}) collective-permute-start(bf16[224,1024]{1,0:T(8,128)(2,1)} %add_convert_fusion.16), channel_id=1, source_target_pairs={{0,1},{1,0},{2,3},{3,2},{4,5},{5,4},{6,7},{7,6},{8,9},{9,8},{10,11... | collective-permute-start | bytes 1376264 | tf_op jit(solution)/shard_map/ppermute | solution.py:46
  209.2 23.1 %collective-permute-start.23 = (bf16[448,1024]{1,0:T(8,128)(2,1)S(1)}, bf16[448,1024]{1,0:T(8,128)(2,1)S(1)}, u32[]{:S(2)}, u32[]{:S(2)}) collective-permute-start(bf16[448,1024]{1,0:T(8,128)(2,1)S(1)} %shard_map.278.refs_1_), channel_id=1, source_target_pairs={{0,2},{2,0},{1,3},{3,1},{4,6},{6,4},{5,7},{7,5},{8,10},{10,8},{9,1... | collective-permute-start | bytes 2752520 | tf_op jit(solution)/shard_map/ppermute | solution.py:42
  209.6 22.6 %collective-permute-start.43 = (bf16[224,1024]{1,0:T(8,128)(2,1)S(1)}, bf16[224,1024]{1,0:T(8,128)(2,1)S(1)}, u32[]{:S(2)}, u32[]{:S(2)}) collective-permute-start(bf16[224,1024]{1,0:T(8,128)(2,1)S(1)} %add_convert_fusion.12), channel_id=1, source_target_pairs={{0,1},{1,0},{2,3},{3,2},{4,5},{5,4},{6,7},{7,6},{8,9},{9,8},{10,11... | collective-permute-start | bytes 1376264 | tf_op jit(solution)/shard_map/ppermute | solution.py:46
  210.2 20.5 %collective-permute-start.27 = (bf16[256,768]{1,0:T(8,128)(2,1)S(1)}, bf16[256,768]{1,0:T(8,128)(2,1)S(1)}, u32[]{:S(2)}, u32[]{:S(2)}) collective-permute-start(bf16[256,768]{1,0:T(8,128)(2,1)S(1)} %constant_dynamic-update-slice_fusion.8.refs_0_), channel_id=1, source_target_pairs={{0,16},{4,20},{8,24},{12,28},{16,0},{20,4},{24,8},{28,12},{1,17},{... | collective-permute-start | bytes 1179656 | tf_op jit(solution)/shard_map/ppermute | solution.py:580
  211.3 20.9 %collective-permute-start.30 = (bf16[64,1024]{1,0:T(8,128)(2,1)S(1)}, bf16[64,1024]{1,0:T(8,128)(2,1)S(1)}, u32[]{:S(2)}, u32[]{:S(2)}) collective-permute-start(bf16[64,1024]{1,0:T(8,128)(2,1)S(1)} %copy-done.111), channel_id=1, source_target_pairs={{0,8},{4,12},{8,0},{12,4},{16,24},{20,28},{24,16},{28,20},{1,9},{5... | collective-permute-start | bytes 393224 | tf_op jit(solution)/shard_map/ppermute | solution.py:580
  214.1 34.2 %collective-permute-start.28 = (bf16[256,768]{1,0:T(8,128)(2,1)S(1)}, bf16[256,768]{1,0:T(8,128)(2,1)S(1)}, u32[]{:S(2)}, u32[]{:S(2)}) collective-permute-start(bf16[256,768]{1,0:T(8,128)(2,1)S(1)} %constant_dynamic-update-slice_fusion.8.refs_0_), channel_id=1, source_target_pairs={{0,4},{4,0},{8,12},{12,8},{16,20},{20,16},{24,28},{28,24},{1,5},{5... | collective-permute-start | bytes 1179656 | tf_op jit(solution)/shard_map/ppermute | solution.py:50
  232.5 27.3 %collective-permute-start.24 = (bf16[224,1024]{1,0:T(8,128)(2,1)S(1)}, bf16[224,1024]{1,0:T(8,128)(2,1)S(1)}, u32[]{:S(2)}, u32[]{:S(2)}) collective-permute-start(bf16[224,1024]{1,0:T(8,128)(2,1)S(1)} %add_convert_fusion.15), channel_id=1, source_target_pairs={{0,1},{1,0},{2,3},{3,2},{4,5},{5,4},{6,7},{7,6},{8,9},{9,8},{10,11... | collective-permute-start | bytes 1376264 | tf_op jit(solution)/shard_map/ppermute | solution.py:46
  259.7 20.8 %collective-permute-start.45 = (bf16[448,1024]{1,0:T(8,128)(2,1)S(1)}, bf16[448,1024]{1,0:T(8,128)(2,1)S(1)}, u32[]{:S(2)}, u32[]{:S(2)}) collective-permute-start(bf16[448,1024]{1,0:T(8,128)(2,1)S(1)} %get-tuple-element.211.refs_1_), channel_id=1, source_target_pairs={{0,2},{2,0},{1,3},{3,1},{4,6},{6,4},{5,7},{7,5},{8,10},{10,8},{9,1... | collective-permute-start | bytes 2752520 | tf_op jit(solution)/shard_map/ppermute | solution.py:42
  269.0 39.3 %collective-permute-start.50 = (bf16[256,1024]{1,0:T(8,128)(2,1)S(1)}, bf16[256,1024]{1,0:T(8,128)(2,1)S(1)}, u32[]{:S(2)}, u32[]{:S(2)}) collective-permute-start(bf16[256,1024]{1,0:T(8,128)(2,1)S(1)} %pad_maximum_fusion.2.refs_0_), channel_id=1, source_target_pairs={{0,4},{4,0},{8,12},{12,8},{16,20},{20,16},{24,28},{28,24},{1,5},{5... | collective-permute-start | bytes 1572872 | tf_op jit(solution)/shard_map/ppermute | solution.py:50
  269.6 38.0 %collective-permute-start.49 = (bf16[256,1024]{1,0:T(8,128)(2,1)S(1)}, bf16[256,1024]{1,0:T(8,128)(2,1)S(1)}, u32[]{:S(2)}, u32[]{:S(2)}) collective-permute-start(bf16[256,1024]{1,0:T(8,128)(2,1)S(1)} %pad_maximum_fusion.2.refs_0_), channel_id=1, source_target_pairs={{0,16},{4,20},{8,24},{12,28},{16,0},{20,4},{24,8},{28,12},{1,17},{... | collective-permute-start | bytes 1572872 | tf_op jit(solution)/shard_map/ppermute | solution.py:580
  277.8 45.5 %collective-permute-start.32 = (bf16[448,1024]{1,0:T(8,128)(2,1)S(1)}, bf16[448,1024]{1,0:T(8,128)(2,1)S(1)}, u32[]{:S(2)}, u32[]{:S(2)}) collective-permute-start(bf16[448,1024]{1,0:T(8,128)(2,1)S(1)} %get-tuple-element.203.refs_1_), channel_id=1, source_target_pairs={{0,2},{2,0},{1,3},{3,1},{4,6},{6,4},{5,7},{7,5},{8,10},{10,8},{9,1... | collective-permute-start | bytes 2752520 | tf_op jit(solution)/shard_map/ppermute | solution.py:42
  277.8 39.0 %collective-permute-start.36 = (bf16[256,1024]{1,0:T(8,128)(2,1)S(1)}, bf16[256,1024]{1,0:T(8,128)(2,1)S(1)}, u32[]{:S(2)}, u32[]{:S(2)}) collective-permute-start(bf16[256,1024]{1,0:T(8,128)(2,1)S(1)} %constant_dynamic-update-slice_fusion.12.refs_0_), channel_id=1, source_target_pairs={{0,16},{4,20},{8,24},{12,28},{16,0},{20,4},{24,8},{28,12},{1,17},{... | collective-permute-start | bytes 1572872 | tf_op jit(solution)/shard_map/ppermute | solution.py:580
  280.7 37.7 %collective-permute-start.46 = (bf16[224,1024]{1,0:T(8,128)(2,1)S(1)}, bf16[224,1024]{1,0:T(8,128)(2,1)S(1)}, u32[]{:S(2)}, u32[]{:S(2)}) collective-permute-start(bf16[224,1024]{1,0:T(8,128)(2,1)S(1)} %add_convert_fusion.11), channel_id=1, source_target_pairs={{0,1},{1,0},{2,3},{3,2},{4,5},{5,4},{6,7},{7,6},{8,9},{9,8},{10,11... | collective-permute-start | bytes 1376264 | tf_op jit(solution)/shard_map/ppermute | solution.py:46
  308.3 25.4 %collective-permute-start.37 = (bf16[256,1024]{1,0:T(8,128)(2,1)S(1)}, bf16[256,1024]{1,0:T(8,128)(2,1)S(1)}, u32[]{:S(2)}, u32[]{:S(2)}) collective-permute-start(bf16[256,1024]{1,0:T(8,128)(2,1)S(1)} %constant_dynamic-update-slice_fusion.12.refs_0_), channel_id=1, source_target_pairs={{0,4},{4,0},{8,12},{12,8},{16,20},{20,16},{24,28},{28,24},{1,5},{5... | collective-permute-start | bytes 1572872 | tf_op jit(solution)/shard_map/ppermute | solution.py:50
  316.8 23.7 %collective-permute-start.38 = (bf16[256,1024]{1,0:T(8,128)(2,1)S(1)}, bf16[256,1024]{1,0:T(8,128)(2,1)S(1)}, u32[]{:S(2)}, u32[]{:S(2)}) collective-permute-start(bf16[256,1024]{1,0:T(8,128)(2,1)S(1)} %collective-permute-done.36.refs_1_), channel_id=1, source_target_pairs={{0,4},{4,0},{8,12},{12,8},{16,20},{20,16},{24,28},{28,24},{1,5},{5... | collective-permute-start | bytes 1572872 | tf_op jit(solution)/shard_map/ppermute | solution.py:50
  318.3 23.1 %collective-permute-start.47 = (bf16[224,1024]{1,0:T(8,128)(2,1)S(1)}, bf16[224,1024]{1,0:T(8,128)(2,1)S(1)}, u32[]{:S(2)}, u32[]{:S(2)}) collective-permute-start(bf16[224,1024]{1,0:T(8,128)(2,1)S(1)} %collective-permute-done.46.refs_3_), channel_id=1, source_target_pairs={{0,2},{2,0},{1,3},{3,1},{4,6},{6,4},{5,7},{7,5},{8,10},{10,8},{9,1... | collective-permute-start | bytes 1376264 | tf_op jit(solution)/shard_map/ppermute | solution.py:42
  323.5 27.7 %collective-permute-start.33 = (bf16[224,1024]{1,0:T(8,128)(2,1)S(1)}, bf16[224,1024]{1,0:T(8,128)(2,1)S(1)}, u32[]{:S(2)}, u32[]{:S(2)}) collective-permute-start(bf16[224,1024]{1,0:T(8,128)(2,1)S(1)} %add_convert_fusion.14), channel_id=1, source_target_pairs={{0,1},{1,0},{2,3},{3,2},{4,5},{5,4},{6,7},{7,6},{8,9},{9,8},{10,11... | collective-permute-start | bytes 1376264 | tf_op jit(solution)/shard_map/ppermute | solution.py:46
  422.1 33.5 %collective-permute-start.53 = (bf16[448,1024]{1,0:T(8,128)(2,1)S(1)}, bf16[448,1024]{1,0:T(8,128)(2,1)S(1)}, u32[]{:S(2)}, u32[]{:S(2)}) collective-permute-start(bf16[448,1024]{1,0:T(8,128)(2,1)S(1)} %shard_map.287), channel_id=1, source_target_pairs={{0,2},{2,0},{1,3},{3,1},{4,6},{6,4},{5,7},{7,5},{8,10},{10,8},{9,1... | collective-permute-start | bytes 2752520 | tf_op jit(solution)/shard_map/ppermute | solution.py:42
  442.4 26.1 %collective-permute-start.117 = (bf16[512,1024]{1,0:T(8,128)(2,1)S(1)}, bf16[512,1024]{1,0:T(8,128)(2,1)S(1)}, u32[]{:S(2)}, u32[]{:S(2)}) collective-permute-start(bf16[512,1024]{1,0:T(8,128)(2,1)S(1)} %bitcast.103), channel_id=1, source_target_pairs={{0,4},{4,0},{8,12},{12,8},{16,20},{20,16},{24,28},{28,24},{1,5},{5... | collective-permute-start | bytes 3145736 | tf_op jit(solution)/shard_map/ppermute | solution.py:50
  452.1 38.0 %collective-permute-start.124 = (bf16[512,1024]{1,0:T(8,128)(2,1)S(1)}, bf16[512,1024]{1,0:T(8,128)(2,1)S(1)}, u32[]{:S(2)}, u32[]{:S(2)}) collective-permute-start(bf16[512,1024]{1,0:T(8,128)(2,1)S(1)} %bitcast.102), channel_id=1, source_target_pairs={{0,4},{4,0},{8,12},{12,8},{16,20},{20,16},{24,28},{28,24},{1,5},{5... | collective-permute-start | bytes 3145736 | tf_op jit(solution)/shard_map/ppermute | solution.py:50
  455.6 35.0 %collective-permute-start.75 = (bf16[224,1024]{1,0:T(8,128)(2,1)S(1)}, bf16[224,1024]{1,0:T(8,128)(2,1)S(1)}, u32[]{:S(2)}, u32[]{:S(2)}) collective-permute-start(bf16[224,1024]{1,0:T(8,128)(2,1)S(1)} %add_convert_fusion.1), channel_id=1, source_target_pairs={{0,1},{1,0},{2,3},{3,2},{4,5},{5,4},{6,7},{7,6},{8,9},{9,8},{10,11... | collective-permute-start | bytes 1376264 | tf_op jit(solution)/shard_map/ppermute | solution.py:46
  469.3 23.8 %collective-permute-start.118 = (bf16[128,1024]{1,0:T(8,128)(2,1)S(1)}, bf16[128,1024]{1,0:T(8,128)(2,1)S(1)}, u32[]{:S(2)}, u32[]{:S(2)}) collective-permute-start(bf16[128,1024]{1,0:T(8,128)(2,1)S(1)} %get-tuple-element.320), channel_id=1, source_target_pairs={{8,0},{12,4},{16,8},{20,12},{24,16},{28,20},{0,24},{4,28},{9,1},{1... | collective-permute-start | bytes 786440 | tf_op jit(solution)/shard_map/ppermute | solution.py:55
  470.7 24.0 %collective-permute-start.119 = (bf16[128,1024]{1,0:T(8,128)(2,1)S(1)}, bf16[128,1024]{1,0:T(8,128)(2,1)S(1)}, u32[]{:S(2)}, u32[]{:S(2)}) collective-permute-start(bf16[128,1024]{1,0:T(8,128)(2,1)S(1)} %get-tuple-element.321), channel_id=1, source_target_pairs={{16,0},{20,4},{24,8},{28,12},{0,16},{4,20},{8,24},{12,28},{17,1},{... | collective-permute-start | bytes 786440 | tf_op jit(solution)/shard_map/ppermute | solution.py:55
  470.9 25.2 %collective-permute-start.120 = (bf16[128,1024]{1,0:T(8,128)(2,1)S(1)}, bf16[128,1024]{1,0:T(8,128)(2,1)S(1)}, u32[]{:S(2)}, u32[]{:S(2)}) collective-permute-start(bf16[128,1024]{1,0:T(8,128)(2,1)S(1)} %get-tuple-element.322), channel_id=1, source_target_pairs={{24,0},{28,4},{0,8},{4,12},{8,16},{12,20},{16,24},{20,28},{25,1},{... | collective-permute-start | bytes 786440 | tf_op jit(solution)/shard_map/ppermute | solution.py:55
  493.1 25.5 %collective-permute-start.55 = (bf16[224,1024]{1,0:T(8,128)(2,1)S(1)}, bf16[224,1024]{1,0:T(8,128)(2,1)S(1)}, u32[]{:S(2)}, u32[]{:S(2)}) collective-permute-start(bf16[224,1024]{1,0:T(8,128)(2,1)S(1)} %add_convert_fusion.9), channel_id=1, source_target_pairs={{0,1},{1,0},{2,3},{3,2},{4,5},{5,4},{6,7},{7,6},{8,9},{9,8},{10,11... | collective-permute-start | bytes 1376264 | tf_op jit(solution)/shard_map/ppermute | solution.py:46
  494.7 19.5 %collective-permute-start.125 = (bf16[128,1024]{1,0:T(8,128)(2,1)S(1)}, bf16[128,1024]{1,0:T(8,128)(2,1)S(1)}, u32[]{:S(2)}, u32[]{:S(2)}) collective-permute-start(bf16[128,1024]{1,0:T(8,128)(2,1)S(1)} %get-tuple-element.326), channel_id=1, source_target_pairs={{8,0},{12,4},{16,8},{20,12},{24,16},{28,20},{0,24},{4,28},{9,1},{1... | collective-permute-start | bytes 786440 | tf_op jit(solution)/shard_map/ppermute | solution.py:55
  496.1 21.9 %collective-permute-start.126 = (bf16[128,1024]{1,0:T(8,128)(2,1)S(1)}, bf16[128,1024]{1,0:T(8,128)(2,1)S(1)}, u32[]{:S(2)}, u32[]{:S(2)}) collective-permute-start(bf16[128,1024]{1,0:T(8,128)(2,1)S(1)} %get-tuple-element.327), channel_id=1, source_target_pairs={{16,0},{20,4},{24,8},{28,12},{0,16},{4,20},{8,24},{12,28},{17,1},{... | collective-permute-start | bytes 786440 | tf_op jit(solution)/shard_map/ppermute | solution.py:55
  514.3 28.5 %collective-permute-start.54 = (bf16[224,1024]{1,0:T(8,128)(2,1)S(1)}, bf16[224,1024]{1,0:T(8,128)(2,1)S(1)}, u32[]{:S(2)}, u32[]{:S(2)}) collective-permute-start(bf16[224,1024]{1,0:T(8,128)(2,1)S(1)} %add_convert_fusion.10), channel_id=1, source_target_pairs={{0,1},{1,0},{2,3},{3,2},{4,5},{5,4},{6,7},{7,6},{8,9},{9,8},{10,11... | collective-permute-start | bytes 1376264 | tf_op jit(solution)/shard_map/ppermute | solution.py:46
  518.5 27.4 %collective-permute-start.77 = (bf16[448,1024]{1,0:T(8,128)(2,1)S(1)}, bf16[448,1024]{1,0:T(8,128)(2,1)S(1)}, u32[]{:S(2)}, u32[]{:S(2)}) collective-permute-start(bf16[448,1024]{1,0:T(8,128)(2,1)S(1)} %get-tuple-element.242.refs_9_), channel_id=1, source_target_pairs={{0,2},{2,0},{1,3},{3,1},{4,6},{6,4},{5,7},{7,5},{8,10},{10,8},{9,1... | collective-permute-start | bytes 2752520 | tf_op jit(solution)/shard_map/ppermute | solution.py:42
  533.0 45.3 %collective-permute-start.93 = (bf16[512,1024]{1,0:T(8,128)(2,1)S(1)}, bf16[512,1024]{1,0:T(8,128)(2,1)S(1)}, u32[]{:S(2)}, u32[]{:S(2)}) collective-permute-start(bf16[512,1024]{1,0:T(8,128)(2,1)S(1)} %bitcast.100), channel_id=1, source_target_pairs={{0,4},{4,0},{8,12},{12,8},{16,20},{20,16},{24,28},{28,24},{1,5},{5... | collective-permute-start | bytes 3145736 | tf_op jit(solution)/shard_map/ppermute | solution.py:50
  534.8 42.9 %collective-permute-start.65 = (bf16[448,1024]{1,0:T(8,128)(2,1)S(1)}, bf16[448,1024]{1,0:T(8,128)(2,1)S(1)}, u32[]{:S(2)}, u32[]{:S(2)}) collective-permute-start(bf16[448,1024]{1,0:T(8,128)(2,1)S(1)} %get-tuple-element.228.refs_3_), channel_id=1, source_target_pairs={{0,2},{2,0},{1,3},{3,1},{4,6},{6,4},{5,7},{7,5},{8,10},{10,8},{9,1... | collective-permute-start | bytes 2752520 | tf_op jit(solution)/shard_map/ppermute | solution.py:42
  540.0 35.9 %collective-permute-start.110 = (bf16[512,768]{1,0:T(8,128)(2,1)S(1)}, bf16[512,768]{1,0:T(8,128)(2,1)S(1)}, u32[]{:S(2)}, u32[]{:S(2)}) collective-permute-start(bf16[512,768]{1,0:T(8,128)(2,1)S(1)} %bitcast.105), channel_id=1, source_target_pairs={{0,4},{4,0},{8,12},{12,8},{16,20},{20,16},{24,28},{28,24},{1,5},{5... | collective-permute-start | bytes 2359304 | tf_op jit(solution)/shard_map/ppermute | solution.py:50
  545.9 67.7 %collective-permute-start.100 = (bf16[512,1024]{1,0:T(8,128)(2,1)S(1)}, bf16[512,1024]{1,0:T(8,128)(2,1)S(1)}, u32[]{:S(2)}, u32[]{:S(2)}) collective-permute-start(bf16[512,1024]{1,0:T(8,128)(2,1)S(1)} %bitcast.101), channel_id=1, source_target_pairs={{0,4},{4,0},{8,12},{12,8},{16,20},{20,16},{24,28},{28,24},{1,5},{5... | collective-permute-start | bytes 3145736 | tf_op jit(solution)/shard_map/ppermute | solution.py:50
  554.8 26.7 %collective-permute-start.123 = (bf16[64,1024]{1,0:T(8,128)(2,1)S(1)}, bf16[64,1024]{1,0:T(8,128)(2,1)S(1)}, u32[]{:S(2)}, u32[]{:S(2)}) collective-permute-start(bf16[64,1024]{1,0:T(8,128)(2,1)S(1)} %slice.256), channel_id=1, source_target_pairs={{0,2},{2,0},{1,3},{3,1},{4,6},{6,4},{5,7},{7,5},{8,10},{10,8},{9,1... | collective-permute-start | bytes 393224 | tf_op jit(solution)/shard_map/ppermute | solution.py:42
  575.9 23.8 %collective-permute-start.132 = (bf16[64,1024]{1,0:T(8,128)(2,1)S(1)}, bf16[64,1024]{1,0:T(8,128)(2,1)S(1)}, u32[]{:S(2)}, u32[]{:S(2)}) collective-permute-start(bf16[64,1024]{1,0:T(8,128)(2,1)S(1)} %get-tuple-element.340), channel_id=1, source_target_pairs={{0,4},{4,0},{8,12},{12,8},{16,20},{20,16},{24,28},{28,24},{1,5},{5... | collective-permute-start | bytes 393224 | tf_op jit(solution)/shard_map/ppermute | solution.py:50
  577.6 28.6 %collective-permute-start.78 = (bf16[224,1024]{1,0:T(8,128)(2,1)S(1)}, bf16[224,1024]{1,0:T(8,128)(2,1)S(1)}, u32[]{:S(2)}, u32[]{:S(2)}) collective-permute-start(bf16[224,1024]{1,0:T(8,128)(2,1)S(1)} %add_convert_fusion), channel_id=1, source_target_pairs={{0,1},{1,0},{2,3},{3,2},{4,5},{5,4},{6,7},{7,6},{8,9},{9,8},{10,11... | collective-permute-start | bytes 1376264 | tf_op jit(solution)/shard_map/ppermute | solution.py:46
  578.3 35.3 %collective-permute-start.66 = (bf16[224,1024]{1,0:T(8,128)(2,1)S(1)}, bf16[224,1024]{1,0:T(8,128)(2,1)S(1)}, u32[]{:S(2)}, u32[]{:S(2)}) collective-permute-start(bf16[224,1024]{1,0:T(8,128)(2,1)S(1)} %add_convert_fusion.4), channel_id=1, source_target_pairs={{0,1},{1,0},{2,3},{3,2},{4,5},{5,4},{6,7},{7,6},{8,9},{9,8},{10,11... | collective-permute-start | bytes 1376264 | tf_op jit(solution)/shard_map/ppermute | solution.py:46
  582.1 23.5 %collective-permute-start.111 = (bf16[128,768]{1,0:T(8,128)(2,1)S(1)}, bf16[128,768]{1,0:T(8,128)(2,1)S(1)}, u32[]{:S(2)}, u32[]{:S(2)}) collective-permute-start(bf16[128,768]{1,0:T(8,128)(2,1)S(1)} %get-tuple-element.310), channel_id=1, source_target_pairs={{8,0},{12,4},{16,8},{20,12},{24,16},{28,20},{0,24},{4,28},{9,1},{1... | collective-permute-start | bytes 589832 | tf_op jit(solution)/shard_map/ppermute | solution.py:55
  606.2 40.9 %collective-permute-start.79 = (bf16[224,1024]{1,0:T(8,128)(2,1)S(1)}, bf16[224,1024]{1,0:T(8,128)(2,1)S(1)}, u32[]{:S(2)}, u32[]{:S(2)}) collective-permute-start(bf16[224,1024]{1,0:T(8,128)(2,1)S(1)} %collective-permute-done.78.refs_11_), channel_id=1, source_target_pairs={{0,2},{2,0},{1,3},{3,1},{4,6},{6,4},{5,7},{7,5},{8,10},{10,8},{9,1... | collective-permute-start | bytes 1376264 | tf_op jit(solution)/shard_map/ppermute | solution.py:42
  611.9 64.1 %collective-permute-start.86 = (bf16[512,768]{1,0:T(8,128)(2,1)S(1)}, bf16[512,768]{1,0:T(8,128)(2,1)S(1)}, u32[]{:S(2)}, u32[]{:S(2)}) collective-permute-start(bf16[512,768]{1,0:T(8,128)(2,1)S(1)} %bitcast.104), channel_id=1, source_target_pairs={{0,4},{4,0},{8,12},{12,8},{16,20},{20,16},{24,28},{28,24},{1,5},{5... | collective-permute-start | bytes 2359304 | tf_op jit(solution)/shard_map/ppermute | solution.py:50
  613.6 34.4 %collective-permute-start.67 = (bf16[224,1024]{1,0:T(8,128)(2,1)S(1)}, bf16[224,1024]{1,0:T(8,128)(2,1)S(1)}, u32[]{:S(2)}, u32[]{:S(2)}) collective-permute-start(bf16[224,1024]{1,0:T(8,128)(2,1)S(1)} %collective-permute-done.66.refs_5_), channel_id=1, source_target_pairs={{0,2},{2,0},{1,3},{3,1},{4,6},{6,4},{5,7},{7,5},{8,10},{10,8},{9,1... | collective-permute-start | bytes 1376264 | tf_op jit(solution)/shard_map/ppermute | solution.py:42
  615.6 24.4 %collective-permute-start.96 = (bf16[128,1024]{1,0:T(8,128)(2,1)S(1)}, bf16[128,1024]{1,0:T(8,128)(2,1)S(1)}, u32[]{:S(2)}, u32[]{:S(2)}) collective-permute-start(bf16[128,1024]{1,0:T(8,128)(2,1)S(1)} %get-tuple-element.282), channel_id=1, source_target_pairs={{24,0},{28,4},{0,8},{4,12},{8,16},{12,20},{16,24},{20,28},{25,1},{... | collective-permute-start | bytes 786440 | tf_op jit(solution)/shard_map/ppermute | solution.py:55
  628.8 35.1 %collective-permute-start.101 = (bf16[128,1024]{1,0:T(8,128)(2,1)S(1)}, bf16[128,1024]{1,0:T(8,128)(2,1)S(1)}, u32[]{:S(2)}, u32[]{:S(2)}) collective-permute-start(bf16[128,1024]{1,0:T(8,128)(2,1)S(1)} %get-tuple-element.288), channel_id=1, source_target_pairs={{8,0},{12,4},{16,8},{20,12},{24,16},{28,20},{0,24},{4,28},{9,1},{1... | collective-permute-start | bytes 786440 | tf_op jit(solution)/shard_map/ppermute | solution.py:55
  640.0 28.6 %collective-permute-start.102 = (bf16[128,1024]{1,0:T(8,128)(2,1)S(1)}, bf16[128,1024]{1,0:T(8,128)(2,1)S(1)}, u32[]{:S(2)}, u32[]{:S(2)}) collective-permute-start(bf16[128,1024]{1,0:T(8,128)(2,1)S(1)} %get-tuple-element.289), channel_id=1, source_target_pairs={{16,0},{20,4},{24,8},{28,12},{0,16},{4,20},{8,24},{12,28},{17,1},{... | collective-permute-start | bytes 786440 | tf_op jit(solution)/shard_map/ppermute | solution.py:55
  647.2 26.9 %collective-permute-start.103 = (bf16[128,1024]{1,0:T(8,128)(2,1)S(1)}, bf16[128,1024]{1,0:T(8,128)(2,1)S(1)}, u32[]{:S(2)}, u32[]{:S(2)}) collective-permute-start(bf16[128,1024]{1,0:T(8,128)(2,1)S(1)} %get-tuple-element.290), channel_id=1, source_target_pairs={{24,0},{28,4},{0,8},{4,12},{8,16},{12,20},{16,24},{20,28},{25,1},{... | collective-permute-start | bytes 786440 | tf_op jit(solution)/shard_map/ppermute | solution.py:55
  663.4 46.5 %collective-permute-start.98 = (bf16[128,1024]{1,0:T(8,128)(2,1)S(1)}, bf16[128,1024]{1,0:T(8,128)(2,1)S(1)}, u32[]{:S(2)}, u32[]{:S(2)}) collective-permute-start(bf16[128,1024]{1,0:T(8,128)(2,1)S(1)} %get-tuple-element.284), channel_id=1, source_target_pairs={{0,1},{1,0},{2,3},{3,2},{4,5},{5,4},{6,7},{7,6},{8,9},{9,8},{10,11... | collective-permute-start | bytes 786440 | tf_op jit(solution)/shard_map/ppermute | solution.py:46
  668.7 19.0 %collective-permute-start.106 = (bf16[64,1024]{1,0:T(8,128)(2,1)S(1)}, bf16[64,1024]{1,0:T(8,128)(2,1)S(1)}, u32[]{:S(2)}, u32[]{:S(2)}) collective-permute-start(bf16[64,1024]{1,0:T(8,128)(2,1)S(1)} %get-tuple-element.299), channel_id=1, source_target_pairs={{16,0},{20,4},{24,8},{28,12},{0,16},{4,20},{8,24},{12,28},{17,1},{... | collective-permute-start | bytes 393224 | tf_op jit(solution)/shard_map/ppermute | solution.py:55
  708.3 20.1 %collective-permute-start.133 = (bf16[64,1024]{1,0:T(8,128)(2,1)}, bf16[64,1024]{1,0:T(8,128)(2,1)}, u32[]{:S(2)}, u32[]{:S(2)}) collective-permute-start(bf16[64,1024]{1,0:T(8,128)(2,1)} %get-tuple-element.342), channel_id=1, source_target_pairs={{0,1},{1,0},{2,3},{3,2},{4,5},{5,4},{6,7},{7,6},{8,9},{9,8},{10,11... | collective-permute-start | bytes 393224 | tf_op jit(solution)/shard_map/ppermute | solution.py:46
  709.9 20.6 %collective-permute-start.104 = (bf16[128,1024]{1,0:T(8,128)(2,1)}, bf16[128,1024]{1,0:T(8,128)(2,1)}, u32[]{:S(2)}, u32[]{:S(2)}) collective-permute-start(bf16[128,1024]{1,0:T(8,128)(2,1)} %get-tuple-element.292), channel_id=1, source_target_pairs={{0,1},{1,0},{2,3},{3,2},{4,5},{5,4},{6,7},{7,6},{8,9},{9,8},{10,11... | collective-permute-start | bytes 786440 | tf_op jit(solution)/shard_map/ppermute | solution.py:46
  710.3 19.8 %collective-permute-start.97 = (bf16[64,1024]{1,0:T(8,128)(2,1)}, bf16[64,1024]{1,0:T(8,128)(2,1)}, u32[]{:S(2)}, u32[]{:S(2)}) collective-permute-start(bf16[64,1024]{1,0:T(8,128)(2,1)} %slice.219), channel_id=1, source_target_pairs={{0,2},{2,0},{1,3},{3,1},{4,6},{6,4},{5,7},{7,5},{8,10},{10,8},{9,1... | collective-permute-start | bytes 393224 | tf_op jit(solution)/shard_map/ppermute | solution.py:42
  (253 other events, 2932.6 us)

commit v4 on v3

--- a/solution.py
+++ b/solution.py
@@ -61,7 +61,7 @@
     return lax.dynamic_index_in_dim(array, at, axis, keepdims=False)
 
 
-TILE = 112
+TILE = 224
 COLS = 256
 VMEM_LIMIT = 20 * 1024 * 1024
 HBM = pltpu.MemorySpace.HBM
@@ -146,15 +146,18 @@
         step(pl.ds(pl.multiple_of(i * COLS, COLS), COLS))
 
 
-def summed(sent, whole, half, part):
-    rows = sent[1].shape[0] // 2
-    side = pl.ds((1 - half) * rows + part.start, TILE)
-    total = widen(sent[0][whole, :]) + widen(sent[1][side, :])
-    return total + widen(sent[2 + half][part, :])
+def summed(sent, half, part):
+    return sum(widen(sent[2 * i + half][part, :]) for i in range(3))
 
 
 def put(ref, cols, value):
     ref[:, cols] = value.astype(ref.dtype)
+
+
+def put_halves(refs, cols, value):
+    rows = refs[0].shape[0]
+    for i, ref in enumerate(refs):
+        ref[:, cols] = value[i * rows : (i + 1) * rows].astype(ref.dtype)
 
 
 def heads_of(ref, width, size, h):
@@ -171,18 +174,20 @@
 
 def attend_body(layer, heads, size, flush, *refs):
     if layer == 0:
-        base, vec, w_qkv, fix, w_proj, normed, qkv, attended, stat, low = refs
+        base, vec, w_qkv, fix, w_proj = refs[:5]
+        normed, qkv, attended, stat = refs[5:9]
         sent, shift = None, 0
     else:
-        base, s0, s1, s2, s3, vec, w_qkv, fix, w_proj = refs[:9]
-        resid, normed, qkv, attended, stat, low = refs[9:]
-        sent, shift = (s0, s1, s2, s3), 1
+        base, sent, (vec, w_qkv, fix, w_proj) = refs[0], refs[1:7], refs[7:11]
+        resid, normed, qkv, attended, stat = refs[11:16]
+        shift = 1
+    low = refs[-2:]
     width = heads * size
 
     def norm(whole, half, part_rows):
         value = widen(base[whole, :])
         if sent is not None:
-            value = value + (summed(sent, whole, half, part_rows) + row(vec, DOWN_B, layer - 1))
+            value = value + (summed(sent, half, part_rows) + row(vec, DOWN_B, layer - 1))
             resid[whole, :] = value
         unit, _ = norm_parts(value)
         normed[whole, :] = (
@@ -210,14 +215,14 @@
         stat[:, h : h + 1] = peak + jnp.log(total)
     flush(shift + 2)
     flush(shift + 3)
-    by_cols(low.shape[1], lambda cols: put(low, cols, mm(attended[...], w_proj[:, cols])))
+    by_cols(base.shape[1], lambda cols: put_halves(low, cols, mm(attended[...], w_proj[:, cols])))
 
 
 def attend(base, sent, vec, w_qkv, fix, w_proj, layer, heads, size):
     toks, width = base.shape
     outs = [((toks, width), bf16, True), ((toks, 3 * heads * size), bf16, True)]
     outs = outs + [((toks, heads * size), bf16, True), ((toks, 128), f32, True)]
-    outs = outs + [((toks, width), bf16)]
+    outs = outs + [((toks // 2, width), bf16)] * 2
     if layer:
         outs = [((toks, width), f32, True)] + outs
     args = [base, *(sent or ()), vec, w_qkv, fix, w_proj]
@@ -231,11 +236,13 @@
 ROOT_TWO_PI_INV = 0.3989422804014327
 
 
-def up_body(layer, flush, base, s0, s1, s2, s3, vec, w_up, up_b, mid, normed, active, slope):
+def up_body(layer, flush, base, *refs):
+    sent, (vec, w_up, up_b, mid, normed, active, slope) = refs[:6], refs[6:]
+
     def norm(whole, half, part_rows):
         value = widen(base[whole, :])
         value = value + (
-            summed((s0, s1, s2, s3), whole, half, part_rows) + row(vec, PROJ_B, layer)
+            summed(sent, half, part_rows) + row(vec, PROJ_B, layer)
         )
         mid[whole, :] = value
         unit, _ = norm_parts(value)
@@ -268,14 +275,16 @@
     return call(body, outs, args, 2 * toks * width * hid, toks * hid)
 
 
-def down_body(flush, active, w_down, low):
-    by_cols(low.shape[1], lambda cols: put(low, cols, mm(active[...], w_down[:, cols])))
+def down_body(flush, active, w_down, *low):
+    by_cols(
+        w_down.shape[1], lambda cols: put_halves(low, cols, mm(active[...], w_down[:, cols]))
+    )
 
 
 def go_down(active, w_down):
-    outs = [((active.shape[0], w_down.shape[1]), bf16)]
+    outs = [((active.shape[0] // 2, w_down.shape[1]), bf16)] * 2
     flops = 2 * active.size * w_down.shape[1]
-    return call(down_body, outs, [active, w_down], flops)[0]
+    return call(down_body, outs, [active, w_down], flops)
 
 
 def mlp_back_tail(flush, at, d_mlp, slope, w_down, w_up, d_pre, low, up_sum):
@@ -286,25 +295,26 @@
 
     by_cols(w_down.shape[0], back)
     flush(at)
-    by_cols(low.shape[1], lambda cols: put(low, cols, mm_t(d_pre[...], w_up[cols, :])))
-
-
-def mlp_back_first(flush, d_mlp, slope, w_down, w_up, d_pre, low, up_sum, sums):
+    by_cols(w_up.shape[0], lambda cols: put_halves(low, cols, mm_t(d_pre[...], w_up[cols, :])))
+
+
+def mlp_back_first(flush, d_mlp, slope, w_down, w_up, d_pre, near, far, up_sum, sums):
     sums[...] = jnp.zeros_like(sums)
 
     def count(whole, half, part_rows):
         sums[16:24, :] += eight(widen(d_mlp[whole, :]))
 
     by_rows(d_mlp.shape[0] // 2, count)
-    mlp_back_tail(flush, 0, d_mlp, slope, w_down, w_up, d_pre, low, up_sum)
-
-
-def mlp_back_body(layer, flush, base, d_mid, s0, s1, s2, s3, vec, slope, w_down, w_up, *outs):
-    grad, d_mlp, d_pre, low, up_sum, sums = outs
+    mlp_back_tail(flush, 0, d_mlp, slope, w_down, w_up, d_pre, (near, far), up_sum)
+
+
+def mlp_back_body(layer, flush, base, d_mid, *refs):
+    sent, (vec, slope, w_down, w_up) = refs[:6], refs[6:10]
+    grad, d_mlp, d_pre, near, far, up_sum, sums = refs[10:]
     sums[...] = jnp.zeros_like(sums)
 
     def norm(whole, half, part_rows):
-        e = summed((s0, s1, s2, s3), whole, half, part_rows)
+        e = summed(sent, half, part_rows)
         d, by_gain = norm_grad(e, widen(base[whole, :]), row(vec, GAIN_ONE, layer + 1))
         value = d_mid[whole, :] + d
         grad[whole, :] = value
@@ -317,13 +327,14 @@
     by_rows(base.shape[0] // 2, norm)
     flush(0)
     flush(1)
-    mlp_back_tail(flush, 2, d_mlp, slope, w_down, w_up, d_pre, low, up_sum)
+    mlp_back_tail(flush, 2, d_mlp, slope, w_down, w_up, d_pre, (near, far), up_sum)
 
 
 def mlp_back(first, base, d_mid, sent, vec, slope, w_down, w_up, layer):
     toks, hid = slope.shape
     width = w_up.shape[0]
-    outs = [((toks, hid), bf16, True), ((toks, width), bf16), ((8, hid), f32), ((24, width), f32)]
+    outs = [((toks, hid), bf16, True)] + [((toks // 2, width), bf16)] * 2
+    outs = outs + [((8, hid), f32), ((24, width), f32)]
     flops = 4 * toks * hid * width
     if first is not None:
         return call(mlp_back_first, outs, [first, slope, w_down, w_up], flops)
@@ -333,13 +344,13 @@
 
 
 def attend_back_body(layer, heads, size, flush, *refs):
-    grad, mid, s0, s1, s2, s3, vec, qkv, stat, w_proj, w_qkv = refs[:11]
-    d_mid, d_branch, d_joined, low, sums, joined_sum, d_att = refs[11:]
+    grad, mid, sent, (vec, qkv, stat, w_proj, w_qkv) = *refs[:2], refs[2:8], refs[8:13]
+    d_mid, d_branch, d_joined, near, far, sums, joined_sum, d_att = refs[13:]
     width = heads * size
     sums[...] = jnp.zeros_like(sums)
 
     def norm(whole, half, part_rows):
-        e = summed((s0, s1, s2, s3), whole, half, part_rows)
+        e = summed(sent, half, part_rows)
         d, by_gain = norm_grad(e, mid[whole, :], row(vec, GAIN_TWO, layer))
         value = widen(grad[whole, :]) + d
         d_mid[whole, :] = value
@@ -368,14 +379,17 @@
             d_joined[:, at : at + size] = value.astype(bf16)
     flush(2)
     joined_sum[...] = eight(widen(d_joined[...]))
-    by_cols(low.shape[1], lambda cols: put(low, cols, mm_t(d_joined[...], w_qkv[cols, :])))
+    by_cols(
+        w_qkv.shape[0],
+        lambda cols: put_halves((near, far), cols, mm_t(d_joined[...], w_qkv[cols, :])),
+    )
 
 
 def attend_back(grad, mid, sent, vec, qkv, stat, w_proj, w_qkv, layer, heads, size):
     toks, width = mid.shape
     wide = 3 * heads * size
     outs = [((toks, width), f32, True), ((toks, width), bf16, True), ((toks, wide), bf16, True)]
-    outs = outs + [((toks, width), bf16), ((24, width), f32), ((8, wide), f32)]
+    outs = outs + [((toks // 2, width), bf16)] * 2 + [((24, width), f32), ((8, wide), f32)]
     args = [grad, mid, *sent, vec, qkv, stat, w_proj, w_qkv]
     flops = 8 * toks * width * heads * size + 10 * heads * toks * toks * size
     return call(
@@ -389,12 +403,12 @@
 
 
 def last_body(flush, where, *refs):
-    streams, vec, grad, sums = (refs[0:6], refs[6:12]), refs[12], refs[13], refs[14]
+    streams, vec, grad, sums = (refs[0:8], refs[8:16]), refs[16], refs[17], refs[18]
     sums[...] = jnp.zeros_like(sums)
     for s, (base, d_mid, *sent) in enumerate(streams):
 
         def norm(whole, half, part_rows):
-            e = summed(sent, whole, half, part_rows)
+            e = summed(sent, half, part_rows)
             d, by_gain = norm_grad(e, widen(base[whole, :]), row(vec, GAIN_ONE, 0))
             sums[0:8, :] += eight(by_gain)
             sums[8:16, :] += eight(e)
@@ -416,22 +430,19 @@
 
 
 def pick_body(toks, flush, where, own, side, across, beside, *outs):
-    for i in range(2):
-        at = slice(i * toks, (i + 1) * toks)
-        for s in range(2):
-            out = outs[2 * i + s]
-
-            @pl.when(where[1] == s)
-            def _():
-                out[0:toks, :] = own[at, :]
-                out[toks:, :] = side[at, :]
-
-            @pl.when(where[1] != s)
-            def _():
-                out[0:toks, :] = across[at, :]
-                out[toks:, :] = beside[at, :]
-
-            flush(2 * i + s)
+    for s, out in enumerate(outs):
+
+        @pl.when(where[1] == s)
+        def _():
+            out[0:toks, :] = own[...]
+            out[toks:, :] = side[...]
+
+        @pl.when(where[1] != s)
+        def _():
+            out[0:toks, :] = across[...]
+            out[toks:, :] = beside[...]
+
+        flush(s)
 
 
 def halves(first, second, c):
@@ -442,45 +453,47 @@
     return jnp.where(c == 0, zero, other), jnp.where(c == 0, other, zero)
 
 
-def units_body(rows, heads, size, flush, where, qkv, up, down, small, *outs):
-    q_mine, q_theirs, u_mine, u_theirs, d_unit = outs
+def units_q_body(rows, heads, size, flush, where, qkv, *refs):
+    vectors, (q_mine, q_theirs, small, wide) = refs[:-4], refs[-4:]
     c, y = where[0], where[1]
     pair = 2 * size
+    for i, vector in enumerate(vectors):
+        for at in (0, size):
+            wide[2 * i : 2 * i + 2, at : at + size] = widen(vector[...])
+    small[...] = wide[...].astype(bf16)
     for layer in range(LAYERS):
         at = slice(layer * rows, (layer + 1) * rows)
         for t in range(3):
             for h in range(0, heads, 2):
-                start = (t * heads + h) * 2 * pair
-                tiles = [
-                    widen(qkv[layer, :, pl.ds(pl.multiple_of(start + i * 2 * pair + y * pair, pair), pair)])
-                    for i in range(2)
-                ]
+                tiles = []
+                for i in range(2):
+                    start = ((t * heads + h + i) * 2 + y) * pair
+                    tiles.append(widen(qkv[layer, :, pl.ds(pl.multiple_of(start, pair), pair)]))
                 mine, theirs = halves(*tiles, c)
                 cols = slice((t * heads + h) * size, (t * heads + h + 2) * size)
                 q_mine[at, cols] = mine.astype(bf16)
                 q_theirs[at, cols] = theirs.astype(bf16)
-        blocks = up.shape[2] // (4 * pair)
-        for f in range(blocks):
+    q_theirs[2 * rows :, :] = jnp.zeros((16, q_theirs.shape[1]), bf16)
+    q_theirs[2 * rows :, 0:pair] = wide[...].astype(bf16)
+
+
+def units_u_body(rows, pair, flush, where, up, down, u_mine, u_theirs, d_unit):
+    c, y = where[0], where[1]
+    for layer in range(LAYERS):
+        at = slice(layer * rows, (layer + 1) * rows)
+        for f in range(up.shape[2] // (4 * pair)):
             for ref, core in ((u_mine, c), (u_theirs, 1 - c)):
                 start = pl.multiple_of(f * 4 * pair + core * 2 * pair + y * pair, pair)
                 ref[at, f * pair : (f + 1) * pair] = up[layer, :, pl.ds(start, pair)]
         half = down.shape[1] // 2
         d_unit[layer] = down[layer, pl.ds(pl.multiple_of(y * half, half), half), :]
-    q_theirs[2 * rows :, :] = jnp.zeros((16, q_theirs.shape[1]), bf16)
-    q_theirs[2 * rows :, 0:pair] = small[...]
-
-
-def join_body(rows, flush, where, q_mine, q_side, u_mine, u_side, small, up_b, q0, q1, u0, u1):
+
+
+def join_q_body(rows, flush, where, q_mine, q_side, small, up_b, q0, q1):
     c, y = where[0], where[1]
     pair = small.shape[1]
-    here = pl.ds(pl.multiple_of(c * rows, rows), rows)
-    there = pl.ds(pl.multiple_of((1 - c) * rows, rows), rows)
-    for layer, (q, u) in enumerate(((q0, u0), (q1, u1))):
-        at = slice(layer * rows, (layer + 1) * rows)
-        q[here, :] = q_mine[at, :]
-        q[there, :] = q_side[at, :]
-        u[here, :] = u_mine[at, :]
-        u[there, :] = u_side[at, :]
+    for layer, q in enumerate((q0, q1)):
+        join_rows(c, rows, q, layer, q_mine, q_side)
     low = lax.broadcasted_iota(jnp.int32, small.shape, 1) < pair // 2
     own, side = widen(small[...]), widen(q_side[2 * rows :, 0:pair])
     both = jnp.where(c == 0, jnp.where(low, own, side), jnp.where(low, side, own))
@@ -491,9 +504,16 @@
     q0[2 * rows :, pair : 2 * pair] = ups.astype(bf16)
 
 
-def choose_body(flush, where, own, side, *outs):
-    x, y = where[2], where[1]
-    for layer, out in enumerate(outs):
+def join_rows(c, rows, out, layer, mine, side):
+    at = slice(layer * rows, (layer + 1) * rows)
+    out[pl.ds(pl.multiple_of(c * rows, rows), rows), :] = mine[at, :]
+    out[pl.ds(pl.multiple_of((1 - c) * rows, rows), rows), :] = side[at, :]
+
+
+def join_u_body(rows, flush, where, u_mine, u_side, own, side, u0, u1, *outs):
+    c, y, x = where[0], where[1], where[2]
+    for layer, (u, out) in enumerate(zip((u0, u1), outs)):
+        join_rows(c, rows, u, layer, u_mine, u_side)
 
         @pl.when(x == y)
         def _():
@@ -572,7 +592,6 @@
         out_shape=tuple(outs),
         compiler_params=pltpu.CompilerParams(vmem_limit_bytes=VMEM_LIMIT),
         cost_estimate=pl.CostEstimate(flops=0, bytes_accessed=4 * total * cols, transcendentals=0),
-        name="place",
     )(at, *blocks)
 
 
@@ -766,7 +785,6 @@
         cost_estimate=pl.CostEstimate(
             flops=0, bytes_accessed=4 << 20, transcendentals=0
         ),
-        name="finish",
     )(*args)
 
 
@@ -817,13 +835,12 @@
     put_vector(SHIFT_ONE, 0, rows_of(first, 1))
 
 
-def send_part(low):
-    side = core_swap(low)
-    half = low.shape[0] // 2
-    mine = (widen(low[:half]) + widen(side[half:])).astype(bf16)
+def send_part(near, far):
+    near_side, far_side = core_swap(far), core_swap(near)
+    mine = (widen(near) + widen(near_side)).astype(bf16)
     across = y_swap(mine)
     beside = core_swap(across)
-    return low, side, across, beside
+    return near, far, near_side, far_side, across, beside
 
 
 def on_device(
@@ -858,19 +875,20 @@
 
     where = jnp.stack([c, y, f % 2, f // 2]).astype(jnp.int32)
 
+    def pair_tokens(own):
+        across = y_swap(own)
+        side, beside = core_swap(own), core_swap(across)
+        return call(
+            functools.partial(pick_body, toks),
+            [((2 * toks, width), bf16, True)] * 2,
+            [where, own, side, across, beside],
+            0,
+            smem=1,
+        )
+
+    resid = list(pair_tokens(clips_in[0]))
     masked = (widen(cotangent[0]) * widen(clip_mask)[0]).astype(bf16)
-    own = jnp.concatenate([clips_in[0], masked], axis=0)
-    side = core_swap(own)
-    across = y_swap(own)
-    beside = core_swap(across)
-    got = call(
-        functools.partial(pick_body, toks),
-        [((2 * toks, width), bf16, True)] * 4,
-        [where, own, side, across, beside],
-        0,
-        smem=1,
-    )
-    resid, start = list(got[:2]), got[2:]
+    start = pair_tokens(masked)
 
     def qkv_cols(w, at):
         w = w.reshape(*w.shape[:-1], 3, heads, 4, size)
@@ -893,33 +911,40 @@
     ]
     weights = []
     if fast:
-        flat_rows = jnp.concatenate(flat, axis=0)
-        small = jnp.concatenate([flat_rows, flat_rows], axis=1)
         up_b_rows = jnp.concatenate([up_bias, jnp.zeros((14, hid_rows), bf16)], axis=0)
         wide = 3 * heads * size
         outs = [((2 * rows, wide), bf16), ((2 * rows + 16, wide), bf16)]
-        outs = outs + [((2 * rows, hidden // 4), bf16)] * 2
-        outs = outs + [((LAYERS, hid_rows // 2, width), bf16)]
-        q_mine, q_theirs, u_mine, u_theirs, down_units = call(
-            functools.partial(units_body, rows, heads, size),
-            outs,
-            [where, qkv_weight, up_weight, down_weight, small],
+        q_mine, q_theirs, small = call(
+            functools.partial(units_q_body, rows, heads, size),
+            [*outs, ((16, 2 * size), bf16)],
+            [where, qkv_weight, *flat],
+            0,
+            scratch=[pltpu.VMEM((16, 2 * size), f32)],
+            smem=1,
+        )
+        q_side = core_swap(q_theirs)
+        q0, q1 = call(
+            functools.partial(join_q_body, rows),
+            [((2 * rows + 16, wide), bf16), ((2 * rows, wide), bf16)],
+            [where, q_mine, q_side, small, up_b_rows],
             0,
             smem=1,
         )
-        q_side, u_side = core_swap(q_theirs), core_swap(u_theirs)
-        outs = [((2 * rows + 16, wide), bf16), ((2 * rows, wide), bf16)]
-        outs = outs + [((2 * rows, hidden // 4), bf16)] * 2
-        q0, q1, u0, u1 = call(
-            functools.partial(join_body, rows),
-            outs,
-            [where, q_mine, q_side, u_mine, u_side, small, up_b_rows],
+        outs = [((2 * rows, hidden // 4), bf16)] * 2
+        u_mine, u_theirs, down_units = call(
+            functools.partial(units_u_body, rows, 2 * size),
+            [*outs, ((LAYERS, hid_rows // 2, width), bf16)],
+            [where, up_weight, down_weight],
             0,
             smem=1,
         )
         p_side = x_swap(proj_weight, n)
-        p0, p1 = call(
-            choose_body, [((rows, width), bf16)] * 2, [where, proj_weight, p_side], 0, smem=1
+        u0, u1, p0, p1 = call(
+            functools.partial(join_u_body, rows),
+            [*outs, *[((rows, width), bf16)] * 2],
+            [where, u_mine, core_swap(u_theirs), proj_weight, p_side],
+            0,
+            smem=1,
         )
         for layer, (q, u, p) in enumerate(((q0, u0, p0), (q1, u1, p1))):
             if layer:
@@ -977,13 +1002,13 @@
         w_qkv, w_proj, w_up, w_down = weights[layer]
         kept = []
         for s in streams:
-            before, normed, qkv, attended, stat, low = attend(
+            before, normed, qkv, attended, stat, *low = attend(
                 resid[s], sent[s], vec, w_qkv, fix, w_proj, layer, heads, size
             )
-            got = send_part(low)
+            got = send_part(*low)
             mid, normed_two, active, slope = go_up(before, got, vec, w_up, up_b, layer)
             kept.append((before, normed, qkv, attended, mid, normed_two, slope, active, stat))
-            sent[s] = send_part(go_down(active, w_down))
+            sent[s] = send_part(*go_down(active, w_down))
             resid[s] = mid
         stash.append(kept)
 
@@ -992,9 +1017,9 @@
 
     last_bias = vec[2 * DOWN_B + LAYERS - 1]
     clips_out = own_rows([r[:toks] for r in resid]) + (
-        widen(own_rows([p[0][:toks] for p in sent]))
-        + widen(own_rows([p[1][toks:] for p in sent]))
+        widen(own_rows([p[0] for p in sent]))
         + widen(own_rows([p[2] for p in sent]))
+        + widen(own_rows([p[4] for p in sent]))
         + last_bias
     )
     clips_out = clips_out.astype(bf16)[None]
@@ -1025,9 +1050,9 @@
             grad.append(got[0])
             d_mlp.append(got[1])
             d_pre.append(got[2])
-            ups.append(got[4])
-            mlp.append(got[5])
-            sent[s] = send_part(got[3])
+            ups.append(got[5])
+            mlp.append(got[6])
+            sent[s] = send_part(got[3], got[4])
         g_down = both_t_mm([k[7] for k in kept], d_mlp)
         g_up = both_t_mm([k[5] for k in kept], d_pre)
         for s in streams:
@@ -1038,9 +1063,9 @@
             d_mid[s] = got[0]
             d_branch.append(got[1])
             d_joined.append(got[2])
-            att.append(got[4])
-            joined.append(got[5])
-            sent[s] = send_part(got[3])
+            att.append(got[5])
+            joined.append(got[6])
+            sent[s] = send_part(got[3], got[4])
         g_proj = both_t_mm([k[3] for k in kept], d_branch)
         g_qkv = both_t_mm([k[1] for k in kept], d_joined)
         grads[layer] = (g_qkv, g_proj, g_up, g_down)

time: 746 us -> 667 us (0.89)
  waiting for transfers between devices: 373 us -> 293 us
    ppermute x14, waiting for transfers between devices: 126 us -> 73 us  [z_pair(): return lax.ppermute(v, 'fsdp', [(f, f ^ 2 * bit) for f in range(n)])]
    ppermute x21, waiting for transfers between devices: 133 us -> 88.4 us  [x_swap(): return lax.ppermute(v, 'fsdp', [(f, f ^ 1) for f in range(n)])]
    ppermute x30, waiting for transfers between devices: 63 us -> 88.7 us  [z_from(): lax.ppermute(v, 'fsdp', [((z + k) % nz * 2 + x, z * 2 + x) for z in range...]
    ppermute x43 -> x59, waiting for transfers between devices: 8.18 us -> 0.57 us  [core_swap(): return lax.ppermute(v, 'seq', PAIR)]
    unnamed x375 -> x337, local copies, waits for them, and re-layouts: 38.6 us -> 42.1 us
    ppermute x26 -> x27, starting transfers between devices: 29.9 us -> 30.4 us  [y_swap(): return lax.ppermute(v, 'replica', PAIR)]
    pallas_call x46 -> x48, Pallas kernels: 133 us -> 133 us  [call(): pl.pallas_call(run, out_shape=shapes, in_specs=[pl.BlockSpec(memory_space...]
    ppermute x26 -> x27, waiting for transfers between devices: 42.1 us -> 42 us  [y_swap(): return lax.ppermute(v, 'replica', PAIR)]
  transfers between devices with their start and end apart: 134 -> 151, of which waited for: 43 -> 40; matrix products, arithmetic and copies ran while one was open for 4% -> 5% of each run, Pallas kernels for 19% -> 23%
where the time goes in v4:
time: 667 us; the launch traced here: 663 us
  waiting for transfers between devices  293 us (44%)
  Pallas kernels  152 us (23%)
  starting transfers between devices  141 us (21%)
  local copies, waits for them, and re-layouts  48.8 us (7%)
  matrix products  16.2 us (2%)
  other arithmetic  9.45 us (1%)
    pallas_call x48, Pallas kernels, call(): pl.pallas_call(run, out_shape=shapes, in_specs=[pl.BlockSpec(memory_space...  133 us
    ppermute x30, waiting for transfers between devices, z_from(): lax.ppermute(v, 'fsdp', [((z + k) % nz * 2 + x, z * 2 + x) for z in range...  88.7 us
    ppermute x21, waiting for transfers between devices, x_swap(): return lax.ppermute(v, 'fsdp', [(f, f ^ 1) for f in range(n)])  88.4 us
    ppermute x14, waiting for transfers between devices, z_pair(): return lax.ppermute(v, 'fsdp', [(f, f ^ 2 * bit) for f in range(n)])  73 us
    ppermute x30, starting transfers between devices, z_from(): lax.ppermute(v, 'fsdp', [((z + k) % nz * 2 + x, z * 2 + x) for z in range...  60.6 us
    unnamed x337, local copies, waits for them, and re-layouts  42.1 us
    ppermute x27, waiting for transfers between devices, y_swap(): return lax.ppermute(v, 'replica', PAIR)  42 us
    ppermute x27, starting transfers between devices, y_swap(): return lax.ppermute(v, 'replica', PAIR)  30.4 us
  transfers between devices with their start and end apart: 151, of which 40 were waited for; matrix products, arithmetic and copies ran while one was open for 5% of the time, Pallas kernels for 23%

profile of v4, /device:TPU:0, one launch (start us, length us, event | category | flops | bytes accessed | tf_op | source)
XLA Modules:
  0.0 663.5 jit_solution(10303971141127403491)
XLA Ops:
  10.9 5.0 collective-permute-start.4
  22.1 14.9 %collective-permute-done.5 = bf16[144,768]{1,0:T(8,128)(2,1)S(1)} collective-permute-done((bf16[144,768]{1,0:T(8,128)(2,1)S(1)}, bf16[144,768]{1,0:T(8,128)(2,1)S(1)}, u32[]{:S(2)}, u32[]{:S(2)}) %collective-permute-start.5) | collective-permute-done | bytes 221216 | tf_op jit(solution)/shard_map/ppermute | solution.py:55
  41.8 3.5 collective-permute-done.10
  48.0 6.8 %collective-permute-done.20 = bf16[128,1024]{1,0:T(8,128)(2,1)S(1)} collective-permute-done((bf16[128,1024]{1,0:T(8,128)(2,1)S(1)}, bf16[128,1024]{1,0:T(8,128)(2,1)S(1)}, u32[]{:S(2)}, u32[]{:S(2)}) %collective-permute-start.20) | collective-permute-done | bytes 262176 | tf_op jit(solution)/shard_map/ppermute | solution.py:599
  54.9 5.7 collective-permute-done.11.refs_1_
  64.3 3.0 shard_map.274
  68.0 7.0 %shard_map.289 = (bf16[448,1024]{1,0:T(8,128)(2,1)S(1)}, bf16[448,768]{1,0:T(8,128)(2,1)S(1)}, bf16[448,256]{1,0:T(8,128)(2,1)S(1)}, f32[448,128]{1,0:T(8,128)S(...) custom-call(bf16[448,1024]{1,0:T(8,128)(2,1)S(1)} %get-tuple-element.232.refs_0_.refs_9_, ...), custom_call_target="tpu_custom_call" | custom-call | flops 1145044992 | bytes 6074368 | tf_op jit(solution)/shard_map/pallas_call | solution.py:93
  78.5 3.0 collective-permute-start.17
  81.5 6.2 shard_map.279
  95.7 9.4 %collective-permute-done.17.refs_1_ = bf16[256,1024]{1,0:T(8,128)(2,1)S(1)} collective-permute-done((bf16[256,1024]{1,0:T(8,128)(2,1)S(1)}, bf16[256,1024]{1,0:T(8,128)(2,1)S(1)}, u32[]{:S(2)}, u32[]{:S(2)}) %collective-permute-start.17) | collective-permute-done | bytes 524320 | tf_op jit(solution)/shard_map/ppermute | solution.py:599
  108.8 8.1 %collective-permute-done.18.refs_2_ = bf16[256,1024]{1,0:T(8,128)(2,1)S(1)} collective-permute-done((bf16[256,1024]{1,0:T(8,128)(2,1)S(1)}, bf16[256,1024]{1,0:T(8,128)(2,1)S(1)}, u32[]{:S(2)}, u32[]{:S(2)}) %collective-permute-start.18) | collective-permute-done | bytes 524320 | tf_op jit(solution)/shard_map/ppermute | solution.py:50
  118.3 9.9 %collective-permute-done.23.refs_3_ = bf16[256,1024]{1,0:T(8,128)(2,1)S(1)} collective-permute-done((bf16[256,1024]{1,0:T(8,128)(2,1)S(1)}, bf16[256,1024]{1,0:T(8,128)(2,1)S(1)}, u32[]{:S(2)}, u32[]{:S(2)}) %collective-permute-start.23) | collective-permute-done | bytes 524320 | tf_op jit(solution)/shard_map/ppermute | solution.py:50
  130.2 8.7 %collective-permute-done.19.refs_3_ = bf16[256,1024]{1,0:T(8,128)(2,1)} collective-permute-done((bf16[256,1024]{1,0:T(8,128)(2,1)S(1)}, bf16[256,1024]{1,0:T(8,128)(2,1)}, u32[]{:S(2)}, u32[]{:S(2)}) %collective-permute-start.19) | collective-permute-done | bytes 524320 | tf_op jit(solution)/shard_map/ppermute | solution.py:50
  148.4 5.4 shard_map.290
  158.8 5.3 shard_map.281
  168.2 15.7 %collective-permute-done.29.refs_1_ = bf16[256,768]{1,0:T(8,128)(2,1)S(1)} collective-permute-done((bf16[256,768]{1,0:T(8,128)(2,1)S(1)}, bf16[256,768]{1,0:T(8,128)(2,1)S(1)}, u32[]{:S(2)}, u32[]{:S(2)}) %collective-permute-start.29) | collective-permute-done | bytes 393248 | tf_op jit(solution)/shard_map/ppermute | solution.py:599
  190.5 5.4 collective-permute-done.30.refs_2_
  195.9 3.7 collective-permute-done.48.refs_5_
  199.6 2.9 collective-permute-done.31.refs_3_
  202.5 6.9 %collective-permute-done.26.refs_5_ = bf16[224,1024]{1,0:T(8,128)(2,1)S(1)} collective-permute-done((bf16[224,1024]{1,0:T(8,128)(2,1)S(1)}, bf16[224,1024]{1,0:T(8,128)(2,1)S(1)}, u32[]{:S(2)}, u32[]{:S(2)}) %collective-permute-start.26) | collective-permute-done | bytes 458784 | tf_op jit(solution)/shard_map/ppermute | solution.py:46
  210.8 2.7 shard_map.284.refs_8_.refs_12_
  213.5 3.3 collective-permute-done.63.refs_3_
  217.5 6.7 %shard_map.292 = (f32[448,1024]{1,0:T(8,128)S(1)}, bf16[448,1024]{1,0:T(8,128)(2,1)S(1)}, bf16[448,768]{1,0:T(8,128)(2,1)S(1)}, bf16[448,256]{1,0:T(8,128)(2,1)S...) custom-call(f32[448,1024]{1,0:T(8,128)S(1)} %get-tuple-element.235.refs_0_.refs_1_, ...), custom_call_target="tpu_custom_call" | custom-call | flops 1145044992 | bytes 11579392 | tf_op jit(solution)/shard_map/pallas_call | solution.py:93
  229.7 7.2 %shard_map.286 = (f32[448,1024]{1,0:T(8,128)S(1)}, bf16[448,1024]{1,0:T(8,128)(2,1)S(1)}, bf16[448,768]{1,0:T(8,128)(2,1)S(1)}, bf16[448,256]{1,0:T(8,128)(2,1)S...) custom-call(f32[448,1024]{1,0:T(8,128)S(1)} %get-tuple-element.220.refs_0_.refs_1_, ...), custom_call_target="tpu_custom_call" | custom-call | flops 1145044992 | bytes 11579392 | tf_op jit(solution)/shard_map/pallas_call | solution.py:93
  241.1 24.6 %collective-permute-done.55.refs_1_ = bf16[256,1024]{1,0:T(8,128)(2,1)S(1)} collective-permute-done((bf16[256,1024]{1,0:T(8,128)(2,1)S(1)}, bf16[256,1024]{1,0:T(8,128)(2,1)S(1)}, u32[]{:S(2)}, u32[]{:S(2)}) %collective-permute-start.55) | collective-permute-done | bytes 524320 | tf_op jit(solution)/shard_map/ppermute | solution.py:599
  269.6 6.7 %collective-permute-done.39.refs_1_ = bf16[256,1024]{1,0:T(8,128)(2,1)S(1)} collective-permute-done((bf16[256,1024]{1,0:T(8,128)(2,1)S(1)}, bf16[256,1024]{1,0:T(8,128)(2,1)S(1)}, u32[]{:S(2)}, u32[]{:S(2)}) %collective-permute-start.39) | collective-permute-done | bytes 524320 | tf_op jit(solution)/shard_map/ppermute | solution.py:599
  281.0 5.8 collective-permute-done.36.refs_5_
  291.9 3.9 shard_map.293
  295.8 4.7 shard_map.302
  302.4 3.9 shard_map.288
  309.5 4.9 shard_map.298
  323.0 3.7 convolution_convert_fusion.1.refs_1_
  326.7 6.2 collective-permute-done.83.refs_6_
  334.7 7.0 %collective-permute-done.67.refs_6_ = bf16[224,1024]{1,0:T(8,128)(2,1)S(1)} collective-permute-done((bf16[224,1024]{1,0:T(8,128)(2,1)S(1)}, bf16[224,1024]{1,0:T(8,128)(2,1)S(1)}, u32[]{:S(2)}, u32[]{:S(2)}) %collective-permute-start.67) | collective-permute-done | bytes 458784 | tf_op jit(solution)/shard_map/ppermute | solution.py:46
  344.3 9.6 %shard_map.303 = (f32[448,1024]{1,0:T(8,128)S(1)}, bf16[448,1024]{1,0:T(8,128)(2,1)S(1)}, bf16[448,768]{1,0:T(8,128)(2,1)S(1)}, bf16[224,1024]{1,0:T(8,128)(2,1)...) custom-call(bf16[448,1024]{1,0:T(8,128)(2,1)S(1)} %copy-done.48, ...), custom_call_target="tpu_custom_call" | custom-call | flops 1453326336 | bytes 13066240 | tf_op jit(solution)/shard_map/pallas_call | solution.py:93
  356.2 9.3 %shard_map.299 = (f32[448,1024]{1,0:T(8,128)S(1)}, bf16[448,1024]{1,0:T(8,128)(2,1)S(1)}, bf16[448,768]{1,0:T(8,128)(2,1)S(1)}, bf16[224,1024]{1,0:T(8,128)(2,1)...) custom-call(bf16[448,1024]{1,0:T(8,128)(2,1)S(1)} %copy-done.46, ...), custom_call_target="tpu_custom_call" | custom-call | flops 1453326336 | bytes 13066240 | tf_op jit(solution)/shard_map/pallas_call | solution.py:93
  374.8 6.3 collective-permute-done.141.refs_2_
  381.3 2.8 collective-permute-done.87.refs_6_
  384.2 10.8 %collective-permute-done.136.refs_3_ = bf16[128,1024]{1,0:T(8,128)(2,1)S(1)} collective-permute-done((bf16[128,1024]{1,0:T(8,128)(2,1)S(1)}, bf16[128,1024]{1,0:T(8,128)(2,1)S(1)}, u32[]{:S(2)}, u32[]{:S(2)}) %collective-permute-start.136) | collective-permute-done | bytes 262176 | tf_op jit(solution)/shard_map/ppermute | solution.py:55
  399.5 6.2 shard_map.304
  407.8 6.0 shard_map.300
  415.8 2.8 collective-permute-start.143
  424.0 13.2 %collective-permute-done.143.refs_2_ = bf16[128,1024]{1,0:T(8,128)(2,1)S(1)} collective-permute-done((bf16[128,1024]{1,0:T(8,128)(2,1)S(1)}, bf16[128,1024]{1,0:T(8,128)(2,1)S(1)}, u32[]{:S(2)}, u32[]{:S(2)}) %collective-permute-start.143) | collective-permute-done | bytes 262176 | tf_op jit(solution)/shard_map/ppermute | solution.py:55
  438.7 3.1 collective-permute-start.147
  445.5 5.6 collective-permute-done.147.refs_2_
  457.8 8.2 %shard_map.305 = (f32[448,1024]{1,0:T(8,128)S(1)}, bf16[448,1024]{1,0:T(8,128)(2,1)S(1)}, bf16[448,768]{1,0:T(8,128)(2,1)S(1)}, bf16[224,1024]{1,0:T(8,128)(2,1)...) custom-call(f32[448,1024]{1,0:T(8,128)S(1)} %get-tuple-element.277.refs_0_, ...), custom_call_target="tpu_custom_call" | custom-call | flops 1453326336 | bytes 13983744 | tf_op jit(solution)/shard_map/pallas_call | solution.py:93
  468.1 8.0 %shard_map.301 = (f32[448,1024]{1,0:T(8,128)S(1)}, bf16[448,1024]{1,0:T(8,128)(2,1)S(1)}, bf16[448,768]{1,0:T(8,128)(2,1)S(1)}, bf16[224,1024]{1,0:T(8,128)(2,1)...) custom-call(f32[448,1024]{1,0:T(8,128)S(1)} %get-tuple-element.259.refs_0_, ...), custom_call_target="tpu_custom_call" | custom-call | flops 1453326336 | bytes 13983744 | tf_op jit(solution)/shard_map/pallas_call | solution.py:93
  478.8 39.4 %collective-permute-done.149.refs_1_ = bf16[64,1024]{1,0:T(8,128)(2,1)S(1)} collective-permute-done((bf16[64,1024]{1,0:T(8,128)(2,1)S(1)}, bf16[64,1024]{1,0:T(8,128)(2,1)S(1)}, u32[]{:S(2)}, u32[]{:S(2)}) %collective-permute-start.149) | collective-permute-done | bytes 131104 | tf_op jit(solution)/shard_map/ppermute | solution.py:50
  521.9 3.3 collective-permute-done.128.refs_2_
  525.3 2.6 collective-permute-start.111
  527.9 3.5 collective-permute-done.129.refs_3_
  531.3 15.3 %collective-permute-start.113 = (bf16[128,1024]{1,0:T(8,128)(2,1)S(1)}, bf16[128,1024]{1,0:T(8,128)(2,1)S(1)}, u32[]{:S(2)}, u32[]{:S(2)}) collective-permute-start(bf16[128,1024]{1,0:T(8,128)(2,1)S(1)} %get-tuple-element.324), channel_id=1, source_target_pairs={{24,0},{28,4},{0,8},{4,12},{8,16},{12,20},{16,24},{20,28},{25,1},{... | collective-permute-start | bytes 786440 | tf_op jit(solution)/shard_map/ppermute | solution.py:55
  549.3 8.5 %collective-permute-done.113.refs_4_ = bf16[128,1024]{1,0:T(8,128)(2,1)S(1)} collective-permute-done((bf16[128,1024]{1,0:T(8,128)(2,1)S(1)}, bf16[128,1024]{1,0:T(8,128)(2,1)S(1)}, u32[]{:S(2)}, u32[]{:S(2)}) %collective-permute-start.113) | collective-permute-done | bytes 262176 | tf_op jit(solution)/shard_map/ppermute | solution.py:55
  567.3 3.9 shard_map.306
  572.0 13.0 %collective-permute-done.130.refs_4_ = bf16[128,768]{1,0:T(8,128)(2,1)S(1)} collective-permute-done((bf16[128,768]{1,0:T(8,128)(2,1)S(1)}, bf16[128,768]{1,0:T(8,128)(2,1)S(1)}, u32[]{:S(2)}, u32[]{:S(2)}) %collective-permute-start.130) | collective-permute-done | bytes 196640 | tf_op jit(solution)/shard_map/ppermute | solution.py:55
  589.3 7.0 %collective-permute-start.123 = (bf16[64,1024]{1,0:T(8,128)(2,1)S(1)}, bf16[64,1024]{1,0:T(8,128)(2,1)S(1)}, u32[]{:S(2)}, u32[]{:S(2)}) collective-permute-start(bf16[64,1024]{1,0:T(8,128)(2,1)S(1)} %get-tuple-element.341), channel_id=1, source_target_pairs={{16,0},{20,4},{24,8},{28,12},{0,16},{4,20},{8,24},{12,28},{17,1},{... | collective-permute-start | bytes 393224 | tf_op jit(solution)/shard_map/ppermute | solution.py:55
  602.3 6.7 %collective-permute-done.123.refs_2_ = bf16[64,1024]{1,0:T(8,128)(2,1)S(1)} collective-permute-done((bf16[64,1024]{1,0:T(8,128)(2,1)S(1)}, bf16[64,1024]{1,0:T(8,128)(2,1)S(1)}, u32[]{:S(2)}, u32[]{:S(2)}) %collective-permute-start.123) | collective-permute-done | bytes 131104 | tf_op jit(solution)/shard_map/ppermute | solution.py:55
  609.0 5.5 collective-permute-start.106
  616.9 8.2 %collective-permute-done.105.refs_3_ = bf16[128,768]{1,0:T(8,128)(2,1)S(1)} collective-permute-done((bf16[128,768]{1,0:T(8,128)(2,1)S(1)}, bf16[128,768]{1,0:T(8,128)(2,1)S(1)}, u32[]{:S(2)}, u32[]{:S(2)}) %collective-permute-start.105) | collective-permute-done | bytes 196640 | tf_op jit(solution)/shard_map/ppermute | solution.py:55
  634.8 3.7 collective-permute-done.125.refs_1_
  639.8 5.1 collective-permute-done.108.refs_2_
  652.7 3.0 fusion.58
  655.7 3.1 shard_map.327
  658.9 3.0 shard_map.328
  (698 shorter events, 204.5 us)
Async XLA Ops:
  15.9 21.8 %collective-permute-start.9 = (bf16[2,64,1024]{2,1,0:T(8,128)(2,1)}, bf16[2,64,1024]{2,1,0:T(8,128)(2,1)S(1)}, u32[]{:S(2)}, u32[]{:S(2)}) collective-permute-start(bf16[2,64,1024]{2,1,0:T(8,128)(2,1)} %refs_3_.3), channel_id=1, source_target_pairs={{0,4},{4,0},{8,12},{12,8},{16,20},{20,16},{24,28},{28,24},{1,5},{5... | collective-permute-start | bytes 786440 | tf_op jit(solution)/shard_map/ppermute | solution.py:50
  17.4 24.4 %collective-permute-start.1 = (bf16[224,1024]{1,0:T(8,128)(2,1)}, bf16[224,1024]{1,0:T(8,128)(2,1)}, u32[]{:S(2)}, u32[]{:S(2)}) collective-permute-start(bf16[224,1024]{1,0:T(8,128)(2,1)} %bitcast.4.refs_1_), channel_id=1, source_target_pairs={{0,1},{1,0},{2,3},{3,2},{4,5},{5,4},{6,7},{7,6},{8,9},{9,8},{10,11... | collective-permute-start | bytes 1376264 | tf_op jit(solution)/shard_map/ppermute | solution.py:46
  37.0 27.2 %collective-permute-start.7 = (bf16[576,768]{1,0:T(8,128)(2,1)S(1)}, bf16[576,768]{1,0:T(8,128)(2,1)S(1)}, u32[]{:S(2)}, u32[]{:S(2)}) collective-permute-start(bf16[576,768]{1,0:T(8,128)(2,1)S(1)} %constant_dynamic-update-slice_fusion.refs_0_), channel_id=1, source_target_pairs={{0,4},{4,0},{8,12},{12,8},{16,20},{20,16},{24,28},{28,24},{1,5},{5... | collective-permute-start | bytes 2654216 | tf_op jit(solution)/shard_map/ppermute | solution.py:50
  37.6 24.2 %collective-permute-start = (bf16[224,1024]{1,0:T(8,128)(2,1)}, bf16[224,1024]{1,0:T(8,128)(2,1)}, u32[]{:S(2)}, u32[]{:S(2)}) collective-permute-start(bf16[224,1024]{1,0:T(8,128)(2,1)} %bitcast.4.refs_1_), channel_id=1, source_target_pairs={{0,2},{2,0},{1,3},{3,1},{4,6},{6,4},{5,7},{7,5},{8,10},{10,8},{9,1... | collective-permute-start | bytes 1376264 | tf_op jit(solution)/shard_map/ppermute | solution.py:42
  41.8 20.1 %collective-permute-start.2 = (bf16[224,1024]{1,0:T(8,128)(2,1)}, bf16[224,1024]{1,0:T(8,128)(2,1)}, u32[]{:S(2)}, u32[]{:S(2)}) collective-permute-start(bf16[224,1024]{1,0:T(8,128)(2,1)} %collective-permute-done.1.refs_3_), channel_id=1, source_target_pairs={{0,2},{2,0},{1,3},{3,1},{4,6},{6,4},{5,7},{7,5},{8,10},{10,8},{9,1... | collective-permute-start | bytes 1376264 | tf_op jit(solution)/shard_map/ppermute | solution.py:42
  54.8 23.6 %collective-permute-start.16 = (bf16[128,1024]{1,0:T(8,128)(2,1)}, bf16[128,1024]{1,0:T(8,128)(2,1)S(1)}, u32[]{:S(2)}, u32[]{:S(2)}) collective-permute-start(bf16[128,1024]{1,0:T(8,128)(2,1)} %get-tuple-element.218), channel_id=1, source_target_pairs={{0,8},{4,12},{8,0},{12,4},{16,24},{20,28},{24,16},{28,20},{1,9},{5... | collective-permute-start | bytes 786440 | tf_op jit(solution)/shard_map/ppermute | solution.py:599
  60.6 33.6 %collective-permute-start.21 = (bf16[256,1024]{1,0:T(8,128)(2,1)S(1)}, bf16[256,1024]{1,0:T(8,128)(2,1)S(1)}, u32[]{:S(2)}, u32[]{:S(2)}) collective-permute-start(bf16[256,1024]{1,0:T(8,128)(2,1)S(1)} %pad_maximum_fusion.refs_0_), channel_id=1, source_target_pairs={{0,16},{4,20},{8,24},{12,28},{16,0},{20,4},{24,8},{28,12},{1,17},{... | collective-permute-start | bytes 1572872 | tf_op jit(solution)/shard_map/ppermute | solution.py:599
  78.5 26.6 %collective-permute-start.17 = (bf16[256,1024]{1,0:T(8,128)(2,1)S(1)}, bf16[256,1024]{1,0:T(8,128)(2,1)S(1)}, u32[]{:S(2)}, u32[]{:S(2)}) collective-permute-start(bf16[256,1024]{1,0:T(8,128)(2,1)S(1)} %constant_dynamic-update-slice_fusion.6.refs_0_), channel_id=1, source_target_pairs={{0,16},{4,20},{8,24},{12,28},{16,0},{20,4},{24,8},{28,12},{1,17},{... | collective-permute-start | bytes 1572872 | tf_op jit(solution)/shard_map/ppermute | solution.py:599
  91.3 25.6 %collective-permute-start.18 = (bf16[256,1024]{1,0:T(8,128)(2,1)S(1)}, bf16[256,1024]{1,0:T(8,128)(2,1)S(1)}, u32[]{:S(2)}, u32[]{:S(2)}) collective-permute-start(bf16[256,1024]{1,0:T(8,128)(2,1)S(1)} %constant_dynamic-update-slice_fusion.6.refs_0_), channel_id=1, source_target_pairs={{0,4},{4,0},{8,12},{12,8},{16,20},{20,16},{24,28},{28,24},{1,5},{5... | collective-permute-start | bytes 1572872 | tf_op jit(solution)/shard_map/ppermute | solution.py:50
  94.2 23.5 %collective-permute-start.44 = (bf16[224,1024]{1,0:T(8,128)(2,1)S(1)}, bf16[224,1024]{1,0:T(8,128)(2,1)}, u32[]{:S(2)}, u32[]{:S(2)}) collective-permute-start(bf16[224,1024]{1,0:T(8,128)(2,1)S(1)} %add_convert_fusion.13), channel_id=1, source_target_pairs={{0,1},{1,0},{2,3},{3,2},{4,5},{5,4},{6,7},{7,6},{8,9},{9,8},{10,11... | collective-permute-start | bytes 1376264 | tf_op jit(solution)/shard_map/ppermute | solution.py:46
  105.1 23.1 %collective-permute-start.23 = (bf16[256,1024]{1,0:T(8,128)(2,1)S(1)}, bf16[256,1024]{1,0:T(8,128)(2,1)S(1)}, u32[]{:S(2)}, u32[]{:S(2)}) collective-permute-start(bf16[256,1024]{1,0:T(8,128)(2,1)S(1)} %collective-permute-done.21.refs_1_), channel_id=1, source_target_pairs={{0,4},{4,0},{8,12},{12,8},{16,20},{20,16},{24,28},{28,24},{1,5},{5... | collective-permute-start | bytes 1572872 | tf_op jit(solution)/shard_map/ppermute | solution.py:50
  107.6 31.4 %collective-permute-start.19 = (bf16[256,1024]{1,0:T(8,128)(2,1)S(1)}, bf16[256,1024]{1,0:T(8,128)(2,1)}, u32[]{:S(2)}, u32[]{:S(2)}) collective-permute-start(bf16[256,1024]{1,0:T(8,128)(2,1)S(1)} %collective-permute-done.17.refs_1_), channel_id=1, source_target_pairs={{0,4},{4,0},{8,12},{12,8},{16,20},{20,16},{24,28},{28,24},{1,5},{5... | collective-permute-start | bytes 1572872 | tf_op jit(solution)/shard_map/ppermute | solution.py:50
  107.8 21.2 %collective-permute-start.14 = (bf16[224,1024]{1,0:T(8,128)(2,1)S(1)}, bf16[224,1024]{1,0:T(8,128)(2,1)}, u32[]{:S(2)}, u32[]{:S(2)}) collective-permute-start(bf16[224,1024]{1,0:T(8,128)(2,1)S(1)} %add_convert_fusion.16), channel_id=1, source_target_pairs={{0,1},{1,0},{2,3},{3,2},{4,5},{5,4},{6,7},{7,6},{8,9},{9,8},{10,11... | collective-permute-start | bytes 1376264 | tf_op jit(solution)/shard_map/ppermute | solution.py:46
  117.7 28.4 %collective-permute-start.43 = (bf16[224,1024]{1,0:T(8,128)(2,1)}, bf16[224,1024]{1,0:T(8,128)(2,1)}, u32[]{:S(2)}, u32[]{:S(2)}) collective-permute-start(bf16[224,1024]{1,0:T(8,128)(2,1)} %get-tuple-element.233.refs_1_), channel_id=1, source_target_pairs={{0,2},{2,0},{1,3},{3,1},{4,6},{6,4},{5,7},{7,5},{8,10},{10,8},{9,1... | collective-permute-start | bytes 1376264 | tf_op jit(solution)/shard_map/ppermute | solution.py:42
  117.8 30.6 %collective-permute-start.45 = (bf16[224,1024]{1,0:T(8,128)(2,1)}, bf16[224,1024]{1,0:T(8,128)(2,1)}, u32[]{:S(2)}, u32[]{:S(2)}) collective-permute-start(bf16[224,1024]{1,0:T(8,128)(2,1)} %collective-permute-done.44.refs_5_), channel_id=1, source_target_pairs={{0,2},{2,0},{1,3},{3,1},{4,6},{6,4},{5,7},{7,5},{8,10},{10,8},{9,1... | collective-permute-start | bytes 1376264 | tf_op jit(solution)/shard_map/ppermute | solution.py:42
  129.0 27.9 %collective-permute-start.13 = (bf16[224,1024]{1,0:T(8,128)(2,1)S(1)}, bf16[224,1024]{1,0:T(8,128)(2,1)}, u32[]{:S(2)}, u32[]{:S(2)}) collective-permute-start(bf16[224,1024]{1,0:T(8,128)(2,1)S(1)} %get-tuple-element.216.refs_1_), channel_id=1, source_target_pairs={{0,2},{2,0},{1,3},{3,1},{4,6},{6,4},{5,7},{7,5},{8,10},{10,8},{9,1... | collective-permute-start | bytes 1376264 | tf_op jit(solution)/shard_map/ppermute | solution.py:42
  129.0 29.8 %collective-permute-start.15 = (bf16[224,1024]{1,0:T(8,128)(2,1)}, bf16[224,1024]{1,0:T(8,128)(2,1)}, u32[]{:S(2)}, u32[]{:S(2)}) collective-permute-start(bf16[224,1024]{1,0:T(8,128)(2,1)} %collective-permute-done.14.refs_5_), channel_id=1, source_target_pairs={{0,2},{2,0},{1,3},{3,1},{4,6},{6,4},{5,7},{7,5},{8,10},{10,8},{9,1... | collective-permute-start | bytes 1376264 | tf_op jit(solution)/shard_map/ppermute | solution.py:42
  146.2 41.6 %collective-permute-start.54 = (bf16[128,1024]{1,0:T(8,128)(2,1)S(1)}, bf16[128,1024]{1,0:T(8,128)(2,1)S(1)}, u32[]{:S(2)}, u32[]{:S(2)}) collective-permute-start(bf16[128,1024]{1,0:T(8,128)(2,1)S(1)} %copy-done.160), channel_id=1, source_target_pairs={{0,8},{4,12},{8,0},{12,4},{16,24},{20,28},{24,16},{28,20},{1,9},{5... | collective-permute-start | bytes 786440 | tf_op jit(solution)/shard_map/ppermute | solution.py:599
  156.8 27.6 %collective-permute-start.46 = (bf16[224,1024]{1,0:T(8,128)(2,1)S(1)}, bf16[224,1024]{1,0:T(8,128)(2,1)S(1)}, u32[]{:S(2)}, u32[]{:S(2)}) collective-permute-start(bf16[224,1024]{1,0:T(8,128)(2,1)S(1)} %get-tuple-element.238.refs_2_), channel_id=1, source_target_pairs={{0,2},{2,0},{1,3},{3,1},{4,6},{6,4},{5,7},{7,5},{8,10},{10,8},{9,1... | collective-permute-start | bytes 1376264 | tf_op jit(solution)/shard_map/ppermute | solution.py:42
  156.9 27.0 %collective-permute-start.29 = (bf16[256,768]{1,0:T(8,128)(2,1)S(1)}, bf16[256,768]{1,0:T(8,128)(2,1)S(1)}, u32[]{:S(2)}, u32[]{:S(2)}) collective-permute-start(bf16[256,768]{1,0:T(8,128)(2,1)S(1)} %constant_dynamic-update-slice_fusion.8.refs_0_), channel_id=1, source_target_pairs={{0,16},{4,20},{8,24},{12,28},{16,0},{20,4},{24,8},{28,12},{1,17},{... | collective-permute-start | bytes 1179656 | tf_op jit(solution)/shard_map/ppermute | solution.py:599
  167.1 22.0 %collective-permute-start.33 = (bf16[128,1024]{1,0:T(8,128)(2,1)S(1)}, bf16[128,1024]{1,0:T(8,128)(2,1)S(1)}, u32[]{:S(2)}, u32[]{:S(2)}) collective-permute-start(bf16[128,1024]{1,0:T(8,128)(2,1)S(1)} %constant_dynamic-update-slice_fusion.10.refs_0_), channel_id=1, source_target_pairs={{0,16},{4,20},{8,24},{12,28},{16,0},{20,4},{24,8},{28,12},{1,17},{... | collective-permute-start | bytes 786440 | tf_op jit(solution)/shard_map/ppermute | solution.py:599
  187.8 21.6 %collective-permute-start.26 = (bf16[224,1024]{1,0:T(8,128)(2,1)S(1)}, bf16[224,1024]{1,0:T(8,128)(2,1)S(1)}, u32[]{:S(2)}, u32[]{:S(2)}) collective-permute-start(bf16[224,1024]{1,0:T(8,128)(2,1)S(1)} %add_convert_fusion.15), channel_id=1, source_target_pairs={{0,1},{1,0},{2,3},{3,2},{4,5},{5,4},{6,7},{7,6},{8,9},{9,8},{10,11... | collective-permute-start | bytes 1376264 | tf_op jit(solution)/shard_map/ppermute | solution.py:46
  189.0 27.8 %collective-permute-start.63 = (bf16[224,1024]{1,0:T(8,128)(2,1)S(1)}, bf16[224,1024]{1,0:T(8,128)(2,1)S(1)}, u32[]{:S(2)}, u32[]{:S(2)}) collective-permute-start(bf16[224,1024]{1,0:T(8,128)(2,1)S(1)} %fusion.59.refs_1_), channel_id=1, source_target_pairs={{0,1},{1,0},{2,3},{3,2},{4,5},{5,4},{6,7},{7,6},{8,9},{9,8},{10,11... | collective-permute-start | bytes 1376264 | tf_op jit(solution)/shard_map/ppermute | solution.py:46
  195.9 21.0 %collective-permute-start.47 = (bf16[224,1024]{1,0:T(8,128)(2,1)S(1)}, bf16[224,1024]{1,0:T(8,128)(2,1)S(1)}, u32[]{:S(2)}, u32[]{:S(2)}) collective-permute-start(bf16[224,1024]{1,0:T(8,128)(2,1)S(1)} %get-tuple-element.237.refs_1_), channel_id=1, source_target_pairs={{0,2},{2,0},{1,3},{3,1},{4,6},{6,4},{5,7},{7,5},{8,10},{10,8},{9,1... | collective-permute-start | bytes 1376264 | tf_op jit(solution)/shard_map/ppermute | solution.py:42
  202.5 24.9 %collective-permute-start.25 = (bf16[224,1024]{1,0:T(8,128)(2,1)S(1)}, bf16[224,1024]{1,0:T(8,128)(2,1)S(1)}, u32[]{:S(2)}, u32[]{:S(2)}) collective-permute-start(bf16[224,1024]{1,0:T(8,128)(2,1)S(1)} %get-tuple-element.223.refs_1_), channel_id=1, source_target_pairs={{0,2},{2,0},{1,3},{3,1},{4,6},{6,4},{5,7},{7,5},{8,10},{10,8},{9,1... | collective-permute-start | bytes 1376264 | tf_op jit(solution)/shard_map/ppermute | solution.py:42
  216.9 21.2 %collective-permute-start.62 = (bf16[224,1024]{1,0:T(8,128)(2,1)S(1)}, bf16[224,1024]{1,0:T(8,128)(2,1)S(1)}, u32[]{:S(2)}, u32[]{:S(2)}) collective-permute-start(bf16[224,1024]{1,0:T(8,128)(2,1)S(1)} %fusion.59.refs_1_), channel_id=1, source_target_pairs={{0,2},{2,0},{1,3},{3,1},{4,6},{6,4},{5,7},{7,5},{8,10},{10,8},{9,1... | collective-permute-start | bytes 1376264 | tf_op jit(solution)/shard_map/ppermute | solution.py:42
  216.9 20.9 %collective-permute-start.38 = (bf16[128,1024]{1,0:T(8,128)(2,1)S(1)}, bf16[128,1024]{1,0:T(8,128)(2,1)S(1)}, u32[]{:S(2)}, u32[]{:S(2)}) collective-permute-start(bf16[128,1024]{1,0:T(8,128)(2,1)S(1)} %copy-done.83), channel_id=1, source_target_pairs={{0,8},{4,12},{8,0},{12,4},{16,24},{20,28},{24,16},{28,20},{1,9},{5... | collective-permute-start | bytes 786440 | tf_op jit(solution)/shard_map/ppermute | solution.py:599
  217.0 21.5 %collective-permute-start.56 = (bf16[256,1024]{1,0:T(8,128)(2,1)S(1)}, bf16[256,1024]{1,0:T(8,128)(2,1)S(1)}, u32[]{:S(2)}, u32[]{:S(2)}) collective-permute-start(bf16[256,1024]{1,0:T(8,128)(2,1)S(1)} %pad_maximum_fusion.1.refs_0_), channel_id=1, source_target_pairs={{0,4},{4,0},{8,12},{12,8},{16,20},{20,16},{24,28},{28,24},{1,5},{5... | collective-permute-start | bytes 1572872 | tf_op jit(solution)/shard_map/ppermute | solution.py:50
  227.5 38.2 %collective-permute-start.55 = (bf16[256,1024]{1,0:T(8,128)(2,1)S(1)}, bf16[256,1024]{1,0:T(8,128)(2,1)S(1)}, u32[]{:S(2)}, u32[]{:S(2)}) collective-permute-start(bf16[256,1024]{1,0:T(8,128)(2,1)S(1)} %pad_maximum_fusion.1.refs_0_), channel_id=1, source_target_pairs={{0,16},{4,20},{8,24},{12,28},{16,0},{20,4},{24,8},{28,12},{1,17},{... | collective-permute-start | bytes 1572872 | tf_op jit(solution)/shard_map/ppermute | solution.py:599
  237.8 29.5 %collective-permute-start.34 = (bf16[224,1024]{1,0:T(8,128)(2,1)S(1)}, bf16[224,1024]{1,0:T(8,128)(2,1)S(1)}, u32[]{:S(2)}, u32[]{:S(2)}) collective-permute-start(bf16[224,1024]{1,0:T(8,128)(2,1)S(1)} %get-tuple-element.229.refs_2_), channel_id=1, source_target_pairs={{0,2},{2,0},{1,3},{3,1},{4,6},{6,4},{5,7},{7,5},{8,10},{10,8},{9,1... | collective-permute-start | bytes 1376264 | tf_op jit(solution)/shard_map/ppermute | solution.py:42
  238.1 30.9 %collective-permute-start.64 = (bf16[224,1024]{1,0:T(8,128)(2,1)S(1)}, bf16[224,1024]{1,0:T(8,128)(2,1)S(1)}, u32[]{:S(2)}, u32[]{:S(2)}) collective-permute-start(bf16[224,1024]{1,0:T(8,128)(2,1)S(1)} %collective-permute-done.63.refs_3_), channel_id=1, source_target_pairs={{0,2},{2,0},{1,3},{3,1},{4,6},{6,4},{5,7},{7,5},{8,10},{10,8},{9,1... | collective-permute-start | bytes 1376264 | tf_op jit(solution)/shard_map/ppermute | solution.py:42
  238.5 39.4 %collective-permute-start.40 = (bf16[256,1024]{1,0:T(8,128)(2,1)S(1)}, bf16[256,1024]{1,0:T(8,128)(2,1)S(1)}, u32[]{:S(2)}, u32[]{:S(2)}) collective-permute-start(bf16[256,1024]{1,0:T(8,128)(2,1)S(1)} %constant_dynamic-update-slice_fusion.12.refs_0_), channel_id=1, source_target_pairs={{0,4},{4,0},{8,12},{12,8},{16,20},{20,16},{24,28},{28,24},{1,5},{5... | collective-permute-start | bytes 1572872 | tf_op jit(solution)/shard_map/ppermute | solution.py:50
  240.2 36.1 %collective-permute-start.39 = (bf16[256,1024]{1,0:T(8,128)(2,1)S(1)}, bf16[256,1024]{1,0:T(8,128)(2,1)S(1)}, u32[]{:S(2)}, u32[]{:S(2)}) collective-permute-start(bf16[256,1024]{1,0:T(8,128)(2,1)S(1)} %constant_dynamic-update-slice_fusion.12.refs_0_), channel_id=1, source_target_pairs={{0,16},{4,20},{8,24},{12,28},{16,0},{20,4},{24,8},{28,12},{1,17},{... | collective-permute-start | bytes 1572872 | tf_op jit(solution)/shard_map/ppermute | solution.py:599
  281.0 20.6 %collective-permute-start.35 = (bf16[224,1024]{1,0:T(8,128)(2,1)S(1)}, bf16[224,1024]{1,0:T(8,128)(2,1)S(1)}, u32[]{:S(2)}, u32[]{:S(2)}) collective-permute-start(bf16[224,1024]{1,0:T(8,128)(2,1)S(1)} %get-tuple-element.228.refs_1_), channel_id=1, source_target_pairs={{0,2},{2,0},{1,3},{3,1},{4,6},{6,4},{5,7},{7,5},{8,10},{10,8},{9,1... | collective-permute-start | bytes 1376264 | tf_op jit(solution)/shard_map/ppermute | solution.py:42
  317.4 26.9 %collective-permute-start.82 = (bf16[224,1024]{1,0:T(8,128)(2,1)}, bf16[224,1024]{1,0:T(8,128)(2,1)S(1)}, u32[]{:S(2)}, u32[]{:S(2)}) collective-permute-start(bf16[224,1024]{1,0:T(8,128)(2,1)} %copy-done.35), channel_id=1, source_target_pairs={{0,2},{2,0},{1,3},{3,1},{4,6},{6,4},{5,7},{7,5},{8,10},{10,8},{9,1... | collective-permute-start | bytes 1376264 | tf_op jit(solution)/shard_map/ppermute | solution.py:42
  321.3 20.4 %collective-permute-start.67 = (bf16[224,1024]{1,0:T(8,128)(2,1)S(1)}, bf16[224,1024]{1,0:T(8,128)(2,1)S(1)}, u32[]{:S(2)}, u32[]{:S(2)}) collective-permute-start(bf16[224,1024]{1,0:T(8,128)(2,1)S(1)} %add_convert_fusion.7), channel_id=1, source_target_pairs={{0,1},{1,0},{2,3},{3,2},{4,5},{5,4},{6,7},{7,6},{8,9},{9,8},{10,11... | collective-permute-start | bytes 1376264 | tf_op jit(solution)/shard_map/ppermute | solution.py:46
  333.0 36.5 %collective-permute-start.134 = (bf16[512,1024]{1,0:T(8,128)(2,1)S(1)}, bf16[512,1024]{1,0:T(8,128)(2,1)S(1)}, u32[]{:S(2)}, u32[]{:S(2)}) collective-permute-start(bf16[512,1024]{1,0:T(8,128)(2,1)S(1)} %bitcast.103), channel_id=1, source_target_pairs={{0,4},{4,0},{8,12},{12,8},{16,20},{20,16},{24,28},{28,24},{1,5},{5... | collective-permute-start | bytes 3145736 | tf_op jit(solution)/shard_map/ppermute | solution.py:50
  334.5 21.6 %collective-permute-start.66 = (bf16[224,1024]{1,0:T(8,128)(2,1)S(1)}, bf16[224,1024]{1,0:T(8,128)(2,1)S(1)}, u32[]{:S(2)}, u32[]{:S(2)}) collective-permute-start(bf16[224,1024]{1,0:T(8,128)(2,1)S(1)} %copy-done.34), channel_id=1, source_target_pairs={{0,2},{2,0},{1,3},{3,1},{4,6},{6,4},{5,7},{7,5},{8,10},{10,8},{9,1... | collective-permute-start | bytes 1376264 | tf_op jit(solution)/shard_map/ppermute | solution.py:42
  354.6 26.5 %collective-permute-start.141 = (bf16[512,1024]{1,0:T(8,128)(2,1)S(1)}, bf16[512,1024]{1,0:T(8,128)(2,1)S(1)}, u32[]{:S(2)}, u32[]{:S(2)}) collective-permute-start(bf16[512,1024]{1,0:T(8,128)(2,1)S(1)} %bitcast.102), channel_id=1, source_target_pairs={{0,4},{4,0},{8,12},{12,8},{16,20},{20,16},{24,28},{28,24},{1,5},{5... | collective-permute-start | bytes 3145736 | tf_op jit(solution)/shard_map/ppermute | solution.py:50
  373.3 21.7 %collective-permute-start.71 = (bf16[224,1024]{1,0:T(8,128)(2,1)S(1)}, bf16[224,1024]{1,0:T(8,128)(2,1)S(1)}, u32[]{:S(2)}, u32[]{:S(2)}) collective-permute-start(bf16[224,1024]{1,0:T(8,128)(2,1)S(1)} %add_convert_fusion.6), channel_id=1, source_target_pairs={{0,1},{1,0},{2,3},{3,2},{4,5},{5,4},{6,7},{7,6},{8,9},{9,8},{10,11... | collective-permute-start | bytes 1376264 | tf_op jit(solution)/shard_map/ppermute | solution.py:46
  374.8 20.2 %collective-permute-start.136 = (bf16[128,1024]{1,0:T(8,128)(2,1)S(1)}, bf16[128,1024]{1,0:T(8,128)(2,1)S(1)}, u32[]{:S(2)}, u32[]{:S(2)}) collective-permute-start(bf16[128,1024]{1,0:T(8,128)(2,1)S(1)} %get-tuple-element.363), channel_id=1, source_target_pairs={{16,0},{20,4},{24,8},{28,12},{0,16},{4,20},{8,24},{12,28},{17,1},{... | collective-permute-start | bytes 786440 | tf_op jit(solution)/shard_map/ppermute | solution.py:55
  398.8 21.7 %collective-permute-start.60 = (bf16[224,1024]{1,0:T(8,128)(2,1)S(1)}, bf16[224,1024]{1,0:T(8,128)(2,1)S(1)}, u32[]{:S(2)}, u32[]{:S(2)}) collective-permute-start(bf16[224,1024]{1,0:T(8,128)(2,1)S(1)} %add_convert_fusion.10), channel_id=1, source_target_pairs={{0,1},{1,0},{2,3},{3,2},{4,5},{5,4},{6,7},{7,6},{8,9},{9,8},{10,11... | collective-permute-start | bytes 1376264 | tf_op jit(solution)/shard_map/ppermute | solution.py:46
  415.8 21.4 %collective-permute-start.143 = (bf16[128,1024]{1,0:T(8,128)(2,1)S(1)}, bf16[128,1024]{1,0:T(8,128)(2,1)S(1)}, u32[]{:S(2)}, u32[]{:S(2)}) collective-permute-start(bf16[128,1024]{1,0:T(8,128)(2,1)S(1)} %get-tuple-element.369), channel_id=1, source_target_pairs={{16,0},{20,4},{24,8},{28,12},{0,16},{4,20},{8,24},{12,28},{17,1},{... | collective-permute-start | bytes 786440 | tf_op jit(solution)/shard_map/ppermute | solution.py:55
  418.6 20.1 %collective-permute-start.144 = (bf16[128,1024]{1,0:T(8,128)(2,1)S(1)}, bf16[128,1024]{1,0:T(8,128)(2,1)S(1)}, u32[]{:S(2)}, u32[]{:S(2)}) collective-permute-start(bf16[128,1024]{1,0:T(8,128)(2,1)S(1)} %get-tuple-element.370), channel_id=1, source_target_pairs={{24,0},{28,4},{0,8},{4,12},{8,16},{12,20},{16,24},{20,28},{25,1},{... | collective-permute-start | bytes 786440 | tf_op jit(solution)/shard_map/ppermute | solution.py:55
  420.5 21.3 %collective-permute-start.138 = (bf16[64,1024]{1,0:T(8,128)(2,1)S(1)}, bf16[64,1024]{1,0:T(8,128)(2,1)S(1)}, u32[]{:S(2)}, u32[]{:S(2)}) collective-permute-start(bf16[64,1024]{1,0:T(8,128)(2,1)S(1)} %slice.91), channel_id=1, source_target_pairs={{0,2},{2,0},{1,3},{3,1},{4,6},{6,4},{5,7},{7,5},{8,10},{10,8},{9,1... | collective-permute-start | bytes 393224 | tf_op jit(solution)/shard_map/ppermute | solution.py:42
  420.6 21.2 %collective-permute-start.146 = (bf16[64,1024]{1,0:T(8,128)(2,1)S(1)}, bf16[64,1024]{1,0:T(8,128)(2,1)S(1)}, u32[]{:S(2)}, u32[]{:S(2)}) collective-permute-start(bf16[64,1024]{1,0:T(8,128)(2,1)S(1)} %get-tuple-element.378), channel_id=1, source_target_pairs={{8,0},{12,4},{16,8},{20,12},{24,16},{28,20},{0,24},{4,28},{9,1},{1... | collective-permute-start | bytes 393224 | tf_op jit(solution)/shard_map/ppermute | solution.py:55
  422.7 29.7 %collective-permute-start.91 = (bf16[224,1024]{1,0:T(8,128)(2,1)S(1)}, bf16[224,1024]{1,0:T(8,128)(2,1)S(1)}, u32[]{:S(2)}, u32[]{:S(2)}) collective-permute-start(bf16[224,1024]{1,0:T(8,128)(2,1)S(1)} %add_convert_fusion.1), channel_id=1, source_target_pairs={{0,1},{1,0},{2,3},{3,2},{4,5},{5,4},{6,7},{7,6},{8,9},{9,8},{10,11... | collective-permute-start | bytes 1376264 | tf_op jit(solution)/shard_map/ppermute | solution.py:46
  451.1 25.0 %collective-permute-start.127 = (bf16[512,768]{1,0:T(8,128)(2,1)S(1)}, bf16[512,768]{1,0:T(8,128)(2,1)S(1)}, u32[]{:S(2)}, u32[]{:S(2)}) collective-permute-start(bf16[512,768]{1,0:T(8,128)(2,1)S(1)} %bitcast.104), channel_id=1, source_target_pairs={{0,4},{4,0},{8,12},{12,8},{16,20},{20,16},{24,28},{28,24},{1,5},{5... | collective-permute-start | bytes 2359304 | tf_op jit(solution)/shard_map/ppermute | solution.py:50
  455.6 75.7 %collective-permute-start.117 = (bf16[512,1024]{1,0:T(8,128)(2,1)S(1)}, bf16[512,1024]{1,0:T(8,128)(2,1)S(1)}, u32[]{:S(2)}, u32[]{:S(2)}) collective-permute-start(bf16[512,1024]{1,0:T(8,128)(2,1)S(1)} %bitcast.100), channel_id=1, source_target_pairs={{0,4},{4,0},{8,12},{12,8},{16,20},{20,16},{24,28},{28,24},{1,5},{5... | collective-permute-start | bytes 3145736 | tf_op jit(solution)/shard_map/ppermute | solution.py:50
  456.9 63.2 %collective-permute-start.110 = (bf16[512,1024]{1,0:T(8,128)(2,1)S(1)}, bf16[512,1024]{1,0:T(8,128)(2,1)S(1)}, u32[]{:S(2)}, u32[]{:S(2)}) collective-permute-start(bf16[512,1024]{1,0:T(8,128)(2,1)S(1)} %bitcast.101), channel_id=1, source_target_pairs={{0,4},{4,0},{8,12},{12,8},{16,20},{20,16},{24,28},{28,24},{1,5},{5... | collective-permute-start | bytes 3145736 | tf_op jit(solution)/shard_map/ppermute | solution.py:50
  476.1 42.7 %collective-permute-start.77 = (bf16[224,1024]{1,0:T(8,128)(2,1)S(1)}, bf16[224,1024]{1,0:T(8,128)(2,1)S(1)}, u32[]{:S(2)}, u32[]{:S(2)}) collective-permute-start(bf16[224,1024]{1,0:T(8,128)(2,1)S(1)} %get-tuple-element.266.refs_4_), channel_id=1, source_target_pairs={{0,2},{2,0},{1,3},{3,1},{4,6},{6,4},{5,7},{7,5},{8,10},{10,8},{9,1... | collective-permute-start | bytes 1376264 | tf_op jit(solution)/shard_map/ppermute | solution.py:42
  477.3 40.9 %collective-permute-start.149 = (bf16[64,1024]{1,0:T(8,128)(2,1)S(1)}, bf16[64,1024]{1,0:T(8,128)(2,1)S(1)}, u32[]{:S(2)}, u32[]{:S(2)}) collective-permute-start(bf16[64,1024]{1,0:T(8,128)(2,1)S(1)} %get-tuple-element.382), channel_id=1, source_target_pairs={{0,4},{4,0},{8,12},{12,8},{16,20},{20,16},{24,28},{28,24},{1,5},{5... | collective-permute-start | bytes 393224 | tf_op jit(solution)/shard_map/ppermute | solution.py:50
  478.6 39.6 %collective-permute-start.140 = (bf16[64,1024]{1,0:T(8,128)(2,1)S(1)}, bf16[64,1024]{1,0:T(8,128)(2,1)S(1)}, u32[]{:S(2)}, u32[]{:S(2)}) collective-permute-start(bf16[64,1024]{1,0:T(8,128)(2,1)S(1)} %slice.104), channel_id=1, source_target_pairs={{0,2},{2,0},{1,3},{3,1},{4,6},{6,4},{5,7},{7,5},{8,10},{10,8},{9,1... | collective-permute-start | bytes 393224 | tf_op jit(solution)/shard_map/ppermute | solution.py:42
  518.8 30.3 %collective-permute-start.95 = (bf16[224,1024]{1,0:T(8,128)(2,1)S(1)}, bf16[224,1024]{1,0:T(8,128)(2,1)S(1)}, u32[]{:S(2)}, u32[]{:S(2)}) collective-permute-start(bf16[224,1024]{1,0:T(8,128)(2,1)S(1)} %add_convert_fusion), channel_id=1, source_target_pairs={{0,1},{1,0},{2,3},{3,2},{4,5},{5,4},{6,7},{7,6},{8,9},{9,8},{10,11... | collective-permute-start | bytes 1376264 | tf_op jit(solution)/shard_map/ppermute | solution.py:46
  520.2 38.4 %collective-permute-start.79 = (bf16[224,1024]{1,0:T(8,128)(2,1)S(1)}, bf16[224,1024]{1,0:T(8,128)(2,1)S(1)}, u32[]{:S(2)}, u32[]{:S(2)}) collective-permute-start(bf16[224,1024]{1,0:T(8,128)(2,1)S(1)} %add_convert_fusion.4), channel_id=1, source_target_pairs={{0,1},{1,0},{2,3},{3,2},{4,5},{5,4},{6,7},{7,6},{8,9},{9,8},{10,11... | collective-permute-start | bytes 1376264 | tf_op jit(solution)/shard_map/ppermute | solution.py:46
  525.3 23.3 %collective-permute-start.111 = (bf16[128,1024]{1,0:T(8,128)(2,1)S(1)}, bf16[128,1024]{1,0:T(8,128)(2,1)S(1)}, u32[]{:S(2)}, u32[]{:S(2)}) collective-permute-start(bf16[128,1024]{1,0:T(8,128)(2,1)S(1)} %get-tuple-element.322), channel_id=1, source_target_pairs={{8,0},{12,4},{16,8},{20,12},{24,16},{28,20},{0,24},{4,28},{9,1},{1... | collective-permute-start | bytes 786440 | tf_op jit(solution)/shard_map/ppermute | solution.py:55
  531.3 26.5 %collective-permute-start.113 = (bf16[128,1024]{1,0:T(8,128)(2,1)S(1)}, bf16[128,1024]{1,0:T(8,128)(2,1)S(1)}, u32[]{:S(2)}, u32[]{:S(2)}) collective-permute-start(bf16[128,1024]{1,0:T(8,128)(2,1)S(1)} %get-tuple-element.324), channel_id=1, source_target_pairs={{24,0},{28,4},{0,8},{4,12},{8,16},{12,20},{16,24},{20,28},{25,1},{... | collective-permute-start | bytes 786440 | tf_op jit(solution)/shard_map/ppermute | solution.py:55
  557.8 40.4 %collective-permute-start.103 = (bf16[512,768]{1,0:T(8,128)(2,1)S(1)}, bf16[512,768]{1,0:T(8,128)(2,1)S(1)}, u32[]{:S(2)}, u32[]{:S(2)}) collective-permute-start(bf16[512,768]{1,0:T(8,128)(2,1)S(1)} %bitcast.105), channel_id=1, source_target_pairs={{0,4},{4,0},{8,12},{12,8},{16,20},{20,16},{24,28},{28,24},{1,5},{5... | collective-permute-start | bytes 2359304 | tf_op jit(solution)/shard_map/ppermute | solution.py:50
  559.4 26.7 %collective-permute-start.118 = (bf16[128,1024]{1,0:T(8,128)(2,1)S(1)}, bf16[128,1024]{1,0:T(8,128)(2,1)S(1)}, u32[]{:S(2)}, u32[]{:S(2)}) collective-permute-start(bf16[128,1024]{1,0:T(8,128)(2,1)S(1)} %get-tuple-element.330), channel_id=1, source_target_pairs={{8,0},{12,4},{16,8},{20,12},{24,16},{28,20},{0,24},{4,28},{9,1},{1... | collective-permute-start | bytes 786440 | tf_op jit(solution)/shard_map/ppermute | solution.py:55
  561.6 27.7 %collective-permute-start.119 = (bf16[128,1024]{1,0:T(8,128)(2,1)S(1)}, bf16[128,1024]{1,0:T(8,128)(2,1)S(1)}, u32[]{:S(2)}, u32[]{:S(2)}) collective-permute-start(bf16[128,1024]{1,0:T(8,128)(2,1)S(1)} %get-tuple-element.331), channel_id=1, source_target_pairs={{16,0},{20,4},{24,8},{28,12},{0,16},{4,20},{8,24},{12,28},{17,1},{... | collective-permute-start | bytes 786440 | tf_op jit(solution)/shard_map/ppermute | solution.py:55
  561.6 34.7 %collective-permute-start.120 = (bf16[128,1024]{1,0:T(8,128)(2,1)S(1)}, bf16[128,1024]{1,0:T(8,128)(2,1)S(1)}, u32[]{:S(2)}, u32[]{:S(2)}) collective-permute-start(bf16[128,1024]{1,0:T(8,128)(2,1)S(1)} %get-tuple-element.332), channel_id=1, source_target_pairs={{24,0},{28,4},{0,8},{4,12},{8,16},{12,20},{16,24},{20,28},{25,1},{... | collective-permute-start | bytes 786440 | tf_op jit(solution)/shard_map/ppermute | solution.py:55
  563.3 21.7 %collective-permute-start.130 = (bf16[128,768]{1,0:T(8,128)(2,1)S(1)}, bf16[128,768]{1,0:T(8,128)(2,1)S(1)}, u32[]{:S(2)}, u32[]{:S(2)}) collective-permute-start(bf16[128,768]{1,0:T(8,128)(2,1)S(1)} %get-tuple-element.354), channel_id=1, source_target_pairs={{24,0},{28,4},{0,8},{4,12},{8,16},{12,20},{16,24},{20,28},{25,1},{... | collective-permute-start | bytes 589832 | tf_op jit(solution)/shard_map/ppermute | solution.py:55
  584.9 46.5 %collective-permute-start.115 = (bf16[128,1024]{1,0:T(8,128)(2,1)S(1)}, bf16[128,1024]{1,0:T(8,128)(2,1)S(1)}, u32[]{:S(2)}, u32[]{:S(2)}) collective-permute-start(bf16[128,1024]{1,0:T(8,128)(2,1)S(1)} %get-tuple-element.326), channel_id=1, source_target_pairs={{0,1},{1,0},{2,3},{3,2},{4,5},{5,4},{6,7},{7,6},{8,9},{9,8},{10,11... | collective-permute-start | bytes 786440 | tf_op jit(solution)/shard_map/ppermute | solution.py:46
  631.4 20.0 %collective-permute-start.121 = (bf16[128,1024]{1,0:T(8,128)(2,1)}, bf16[128,1024]{1,0:T(8,128)(2,1)}, u32[]{:S(2)}, u32[]{:S(2)}) collective-permute-start(bf16[128,1024]{1,0:T(8,128)(2,1)} %get-tuple-element.334), channel_id=1, source_target_pairs={{0,1},{1,0},{2,3},{3,2},{4,5},{5,4},{6,7},{7,6},{8,9},{9,8},{10,11... | collective-permute-start | bytes 786440 | tf_op jit(solution)/shard_map/ppermute | solution.py:46
  (251 other events, 2632.1 us)
